TPU v7x, 1024 devices: a whole 8x8x8 slice. The times are simulated.
1024 devices in a mesh: dp: 32 (over y, z_lo), expert: 32 (over x, z_hi, core).
Axes of the slice: x: 8, y: 8, z: 8 (z_hi: 2, z_lo: 4; z = z_hi * 4 + z_lo), core: 2. Of those that a mesh axis runs over, the one named last changes fastest.
Arguments:
- tokens: bfloat16 [512, 7168], P('expert', 'dp'), may hold values from -6 to 6
- routes: int32 [512, 8], P('expert'), may hold values from 0 to 31, all different within a row; in each aligned block of 16 rows (0 to 15, 16 to 31, ...) at most 8 rows name the same one
- scores: float32 [512, 8], P('expert'), may hold values from 0.05 to 1
- w_gate: bfloat16 [32, 7168, 1024], P('expert', 'dp'), may hold values from -0.0625 to 0.0625
- w_up: bfloat16 [32, 7168, 1024], P('expert', 'dp'), may hold values from -0.0625 to 0.0625
- w_down: bfloat16 [32, 7168, 1024], P('expert', 'dp'), may hold values from -0.1875 to 0.1875
- cotangent: bfloat16 [512, 7168], P('expert', 'dp'), may hold values from -6 to 6
Outputs:
- layer_out: bfloat16 [512, 7168], P('expert', 'dp')
- grad_tokens: bfloat16 [512, 7168], P('expert', 'dp')
- grad_gate: bfloat16 [32, 7168, 1024], P('expert', 'dp')
- grad_up: bfloat16 [32, 7168, 1024], P('expert', 'dp')
- grad_down: bfloat16 [32, 7168, 1024], P('expert', 'dp')
Inputs may be any that keep to these rules, and one draw needn't show every extreme that they name: `routes`: each row names 8 different experts. In each aligned block of 16 rows (the tokens held by one expert-axis shard) no expert is named by more than 8 rows, a bound that some block reaches.
All inputs are finite; a program needn't handle non-finite values.
Results may differ from a plain program's by a relative error of at most 0.0057.
Values may be sent and summed in bfloat16 or wider, within the bound.
No kernel may reach another device: no remote copies, remote signals or barrier semaphores. Data moves between devices by JAX's collectives and lax.ppermute only.
A program may use at most 32 MiB of HBM per device.

v0:
```python
import jax
import jax.numpy as jnp
from jax import lax
from jax.sharding import PartitionSpec as P

HID = 1024
EXPERTS = 32
CAP = 8


route_scale = 2.5


def slot_table(routes, scores):
    flat_routes = routes.reshape(-1)
    onehot = (flat_routes[:, None] == jnp.arange(EXPERTS, dtype=jnp.int32)[None, :]).astype(
        jnp.int32
    )
    before = jnp.cumsum(onehot, axis=0) - onehot
    slot_rank = jnp.sum(before * onehot, axis=1)
    slot_ids = flat_routes * CAP + slot_rank
    pick_pairs = (jnp.arange(EXPERTS * CAP, dtype=jnp.int32)[:, None] == slot_ids[None, :]).astype(
        jnp.float32
    )
    gate_vals = route_scale * scores / jnp.sum(scores, axis=1, keepdims=True)
    return (pick_pairs, gate_vals)


def local(tokens, routes, scores, w_gate, w_up, w_down, cotangent):
    dp_count = lax.axis_size("dp")
    ex_count = lax.axis_size("expert")
    local_experts = w_gate.shape[0]
    slice_width = tokens.shape[1]
    tok_count = routes.shape[0]
    top_count = routes.shape[1]
    hid_share = HID // dp_count
    slot_count = EXPERTS * CAP
    columns = local_experts * ex_count * CAP
    pick_pairs, gate_vals = slot_table(routes, scores)
    select_tok = pick_pairs.reshape(slot_count, tok_count, top_count).sum(axis=2)
    weighted = (
        (pick_pairs * gate_vals.reshape(1, -1))
        .reshape(slot_count, tok_count, top_count)
        .sum(axis=2)
    )
    x_slots = jnp.dot(
        select_tok.astype(jnp.bfloat16), tokens, preferred_element_type=jnp.float32
    ).astype(jnp.bfloat16)
    do_pairs = gate_vals[:, :, None] * cotangent[:, None, :].astype(jnp.float32)
    do_pairs = do_pairs.reshape(tok_count * top_count, slice_width).astype(jnp.bfloat16)
    do_slots = jnp.dot(
        pick_pairs.astype(jnp.bfloat16), do_pairs, preferred_element_type=jnp.float32
    ).astype(jnp.bfloat16)
    slot_shape = (ex_count, local_experts, CAP, slice_width)
    x_rows, do_rows = (
        lax.all_to_all(
            x_slots.reshape(slot_shape), "expert", split_axis=0, concat_axis=0, tiled=True
        ),
        lax.all_to_all(
            do_slots.reshape(slot_shape), "expert", split_axis=0, concat_axis=0, tiled=True
        ),
    )
    block_count = 2 * hid_share * lax.axis_size("dp") // (2 * hid_share)
    gate_cols = w_gate
    up_cols = w_up
    gate_part = jnp.einsum("sjcd,jdh->hjsc", x_rows, gate_cols, preferred_element_type=jnp.float32)
    up_part = jnp.einsum("sjcd,jdh->hjsc", x_rows, up_cols, preferred_element_type=jnp.float32)
    gate_part = gate_part.reshape(block_count, hid_share, columns)
    up_part = up_part.reshape(block_count, hid_share, columns)
    own_terms = lax.psum_scatter(
        jnp.stack([gate_part, up_part], axis=1).reshape(
            2 * hid_share * lax.axis_size("dp"), columns
        ),
        "dp",
        scatter_dimension=0,
        tiled=True,
    )
    gate_own = own_terms[:hid_share]
    up_own = own_terms[hid_share:]
    hidden_own = (gate_own * jax.nn.sigmoid(gate_own) * up_own).astype(jnp.bfloat16)
    pieces = lax.all_gather(hidden_own, "dp", axis=0, tiled=True)
    width = pieces.shape[0]
    down_cols = w_down
    piece_four = pieces.reshape(width, local_experts, ex_count, CAP)
    out_total = jnp.einsum(
        "jdh,hjsc->dsjc", down_cols, piece_four, preferred_element_type=jnp.float32
    )
    block_grad = jnp.einsum(
        "sjcd,hjsc->jdh", do_rows, piece_four, preferred_element_type=jnp.float32
    )
    out_back = lax.all_to_all(out_total, "expert", split_axis=1, concat_axis=1, tiled=True)
    down_cols = w_down
    term = jnp.einsum("jdh,sjcd->hjsc", down_cols, do_rows, preferred_element_type=jnp.float32)
    grad_hidden = lax.psum_scatter(
        term.reshape(hid_share * lax.axis_size("dp"), columns),
        "dp",
        scatter_dimension=0,
        tiled=True,
    )
    sigma_own = jax.nn.sigmoid(gate_own)
    active_own = gate_own * sigma_own
    grad_pre_gate = (
        grad_hidden * up_own * sigma_own * (1.0 + gate_own * (1.0 - sigma_own))
    ).astype(jnp.bfloat16)
    grad_pre_up = (grad_hidden * active_own).astype(jnp.bfloat16)
    gate_piece = lax.all_gather(grad_pre_gate, "dp", axis=0, tiled=True)
    up_piece = lax.all_gather(grad_pre_up, "dp", axis=0, tiled=True)
    width = gate_piece.shape[0]
    gate_cols = w_gate
    up_cols = w_up
    gate_four = gate_piece.reshape(width, local_experts, ex_count, CAP)
    up_four = up_piece.reshape(width, local_experts, ex_count, CAP)
    input_total = jnp.einsum(
        "jdh,hjsc->dsjc", gate_cols, gate_four, preferred_element_type=jnp.float32
    )
    input_total = input_total + jnp.einsum(
        "jdh,hjsc->dsjc", up_cols, up_four, preferred_element_type=jnp.float32
    )
    gate_block = jnp.einsum("sjcd,hjsc->jdh", x_rows, gate_four, preferred_element_type=jnp.float32)
    up_block = jnp.einsum("sjcd,hjsc->jdh", x_rows, up_four, preferred_element_type=jnp.float32)
    input_back = lax.all_to_all(input_total, "expert", split_axis=1, concat_axis=1, tiled=True)
    layer_out = jnp.dot(
        out_back.reshape(slice_width, slot_count), weighted, precision=lax.Precision.HIGHEST
    )
    grad_tokens = jnp.dot(
        input_back.reshape(slice_width, slot_count), select_tok, precision=lax.Precision.HIGHEST
    )
    return (
        layer_out.T.astype(jnp.bfloat16),
        grad_tokens.T.astype(jnp.bfloat16),
        gate_block.astype(jnp.bfloat16),
        up_block.astype(jnp.bfloat16),
        block_grad.astype(jnp.bfloat16),
    )


def solution(mesh):
    in_specs = (
        P("expert", "dp"),
        P("expert", None),
        P("expert", None),
        P("expert", "dp", None),
        P("expert", "dp", None),
        P("expert", "dp", None),
        P("expert", "dp"),
    )
    out_specs = (
        P("expert", "dp"),
        P("expert", "dp"),
        P("expert", "dp", None),
        P("expert", "dp", None),
        P("expert", "dp", None),
    )
    return jax.shard_map(local, mesh=mesh, in_specs=in_specs, out_specs=out_specs, check_vma=False)
```

profile of v0, /device:TPU:1, one launch (start us, length us, event | category | flops | bytes accessed | tf_op | source)
XLA Modules:
  0.0 660.2 jit_solution(320721209359844192)
XLA Ops:
  7.2 0.0 copy-start
  7.2 0.0 reduce-scatter.5.cloned.1.call-start
  7.2 0.8 copy.72
  8.0 0.1 eq.37
  8.1 0.1 fusion.31
  8.2 0.2 reduce_window_sum.11
  8.4 0.2 select_reduce_fusion.1
  8.6 0.7 reduce_sum.40
  9.3 0.7 multiply_divide_fusion
  10.0 0.1 copy.74
  10.0 0.1 mul.83
  10.1 0.7 convert_element_type.69
  10.8 0.3 convolution_convert_fusion.1
  11.2 0.1 copy.85
  11.3 33.5 %all_to_all.20 = bf16[32,1,8,224]{3,2,1,0:T(8,128)(2,1)S(1)} all-to-all(bf16[32,1,8,224]{3,2,1,0:T(8,128)(2,1)S(1)} %bitcast.133), channel_id=1, replica_groups=mesh['dp'=32,'expert'=32] {'expert'}, dimensions={0} | all-to-all | bytes 229376 | tf_op jit(solution)/shard_map/all_to_all | solution.py:59
  44.7 0.0 copy-done
  44.7 0.0 copy-start.3
  44.7 0.3 convolution_bitcast_fusion
  45.0 0.0 copy-start.2
  45.1 0.0 copy-start.1
  45.1 1.3 copy.87
  46.4 0.0 reduce-scatter.5.cloned.1.call-update
  46.4 0.1 reduce_sum.39
  46.5 0.2 convert_reduce_fusion
  46.7 0.0 copy-done.3
  46.7 0.2 convolution_convert_fusion
  46.9 0.8 copy.75
  47.7 3.8 all-to-all-start
  51.5 0.0 reduce-scatter.3.cloned.1.call-start
  51.5 0.0 copy-done.2
  51.5 0.2 copy.79
  51.7 0.0 copy-done.1
  51.7 0.2 copy.77
  51.9 12.9 %all-to-all-done = bf16[32,1,8,224]{3,2,1,0:T(8,128)(2,1)S(1)} async-done(((bf16[32,1,8,224]{3,2,1,0:T(8,128)(2,1)}), bf16[32,1,8,224]{3,2,1,0:T(8,128)(2,1)S(1)}, u32[]{:S(2)}, u32[]{:S(2)}) %all-to-all-start) | async-done | bytes 114720 | tf_op jit(solution)/shard_map/all_to_all | solution.py:56
  64.8 0.3 convolution_bitcast_fusion.1
  65.2 0.3 convolution_bitcast_fusion.2
  65.5 0.2 pad_maximum_fusion
  65.7 1.5 copy.81
  67.2 0.0 reduce-scatter.3.cloned.1.call-update
  67.3 116.7 %reduce-scatter.5.cloned.1.call-done = f32[32,256]{1,0:T(8,128)} async-done(((f32[1024,256]{1,0:T(8,128)}), f32[32,256]{1,0:T(8,128)}) %reduce-scatter.5.cloned.1.call-update) | async-done | bytes 32784 | tf_op jit(solution)/shard_map/reduce_scatter | solution.py:94
  183.9 170.0 %reduce-scatter.3.cloned.1.call-done = f32[64,256]{1,0:T(8,128)} async-done(((f32[2048,256]{1,0:T(8,128)}), f32[64,256]{1,0:T(8,128)}) %reduce-scatter.3.cloned.1.call-update) | async-done | bytes 65552 | tf_op jit(solution)/shard_map/reduce_scatter | solution.py:70
  353.9 0.8 multiply_convert_fusion
  354.7 63.8 %all_gather.10 = bf16[1024,256]{1,0:T(8,128)(2,1)S(1)} all-gather(bf16[32,256]{1,0:T(8,128)(2,1)S(1)} %get-tuple-element.8), channel_id=1, replica_groups=mesh['dp'=32,'expert'=32] {'dp'}, dimensions={0}, use_global_device_ids=true | all-gather | bytes 540672 | tf_op jit(solution)/shard_map/all_gather | solution.py:106
  418.6 0.2 copy.88
  418.8 0.3 fusion.12
  419.1 62.8 %all_gather.11 = bf16[1024,256]{1,0:T(8,128)(2,1)S(1)} all-gather(bf16[32,256]{1,0:T(8,128)(2,1)S(1)} %get-tuple-element.7), channel_id=1, replica_groups=mesh['dp'=32,'expert'=32] {'dp'}, dimensions={0}, use_global_device_ids=true | all-gather | bytes 540672 | tf_op jit(solution)/shard_map/all_gather | solution.py:107
  481.9 0.2 copy.90
  482.1 1.0 fusion.6
  483.1 62.7 %all-to-all-start.3 = ((f32[224,32,1,8]{0,3,2,1:T(8,128)}), f32[224,32,1,8]{0,3,2,1:T(8,128)S(1)}, u32[]{:S(2)}, u32[]{:S(2)}) async-start(f32[224,32,1,8]{0,3,2,1:T(8,128)} %fusion.6), calls=%async_computation.5 | async-start | bytes 524288 | tf_op jit(solution)/shard_map/all_to_all | solution.py:121
  545.8 64.1 %all_gather.9 = bf16[1024,256]{1,0:T(8,128)(2,1)S(1)} all-gather(bf16[32,256]{1,0:T(8,128)(2,1)S(1)} %get-tuple-element.9), channel_id=1, replica_groups=mesh['dp'=32,'expert'=32] {'dp'}, dimensions={0}, use_global_device_ids=true | all-gather | bytes 540672 | tf_op jit(solution)/shard_map/all_gather | solution.py:81
  609.9 0.2 copy.82
  610.1 1.0 convolution_bitcast_fusion.6
  611.1 1.1 fusion.3
  612.2 0.0 all-to-all-done.3
  612.2 25.0 %all-to-all-start.1 = ((f32[224,32,1,8]{0,3,2,1:T(8,128)}), f32[224,32,1,8]{0,3,2,1:T(8,128)S(1)}, u32[]{:S(2)}, u32[]{:S(2)}) async-start(f32[224,32,1,8]{0,3,2,1:T(8,128)} %convolution_bitcast_fusion.6), calls=%async_computation.2 | async-start | bytes 524288 | tf_op jit(solution)/shard_map/all_to_all | solution.py:91
  637.2 1.3 fusion.4
  638.5 1.3 fusion.5
  639.8 0.8 convolution_convert_fusion.2
  640.6 11.9 %all-to-all-done.1 = f32[224,32,1,8]{0,3,2,1:T(8,128)S(1)} async-done(((f32[224,32,1,8]{0,3,2,1:T(8,128)}), f32[224,32,1,8]{0,3,2,1:T(8,128)S(1)}, u32[]{:S(2)}, u32[]{:S(2)}) %all-to-all-start.1) | async-done | bytes 229408 | tf_op jit(solution)/shard_map/all_to_all | solution.py:91
  652.5 0.8 convolution_convert_fusion.3
  (2 shorter events, 0.0 us)
Async XLA Ops:
  7.2 37.6 %copy-start = (bf16[1,224,1024]{2,1,0:T(8,128)(2,1)S(1)}, bf16[1,224,1024]{2,1,0:T(8,128)(2,1)}, u32[]{:S(2)}) copy-start(bf16[1,224,1024]{2,1,0:T(8,128)(2,1)} %param.12) | copy-start | bytes 1376260
  7.2 176.8 %reduce-scatter.5.cloned.1.call-start = ((), (), s32[]{:S(2)}) async-start(), calls=%async_computation.7 | async-start | bytes 1081344 | tf_op jit(solution)/shard_map/reduce_scatter | solution.py:94
  44.7 1.9 copy-start.3
  45.0 6.5 copy-start.2
  45.1 6.7 %copy-start.1 = (bf16[1,224,1024]{2,1,0:T(8,128)(2,1)S(1)}, bf16[1,224,1024]{2,1,0:T(8,128)(2,1)}, u32[]{:S(2)}) copy-start(bf16[1,224,1024]{2,1,0:T(8,128)(2,1)} %param.10) | copy-start | bytes 1376260
  47.7 17.1 %all-to-all-start = ((bf16[32,1,8,224]{3,2,1,0:T(8,128)(2,1)}), bf16[32,1,8,224]{3,2,1,0:T(8,128)(2,1)S(1)}, u32[]{:S(2)}, u32[]{:S(2)}) async-start(bf16[32,1,8,224]{3,2,1,0:T(8,128)(2,1)} %bitcast.1), calls=%async_computation | async-start | bytes 262144 | tf_op jit(solution)/shard_map/all_to_all | solution.py:56
  51.5 302.5 %reduce-scatter.3.cloned.1.call-start = ((), (), s32[]{:S(2)}) async-start(), calls=%async_computation.6 | async-start | bytes 2162688 | tf_op jit(solution)/shard_map/reduce_scatter | solution.py:70
  483.1 129.1 %all-to-all-start.3 = ((f32[224,32,1,8]{0,3,2,1:T(8,128)}), f32[224,32,1,8]{0,3,2,1:T(8,128)S(1)}, u32[]{:S(2)}, u32[]{:S(2)}) async-start(f32[224,32,1,8]{0,3,2,1:T(8,128)} %fusion.6), calls=%async_computation.5 | async-start | bytes 524288 | tf_op jit(solution)/shard_map/all_to_all | solution.py:121
  612.2 40.3 %all-to-all-start.1 = ((f32[224,32,1,8]{0,3,2,1:T(8,128)}), f32[224,32,1,8]{0,3,2,1:T(8,128)S(1)}, u32[]{:S(2)}, u32[]{:S(2)}) async-start(f32[224,32,1,8]{0,3,2,1:T(8,128)} %convolution_bitcast_fusion.6), calls=%async_computation.2 | async-start | bytes 524288 | tf_op jit(solution)/shard_map/all_to_all | solution.py:91
Sparse Core Ops, SparseCore 0:
  46.5 137.3 reduce-scatter.4
  187.7 166.1 reduce-scatter.2
where the time goes:
time: 661 us; the launch traced here: 660 us
  waiting for transfers between devices  312 us (47%)
  blocking collectives  224 us (34%)
  starting transfers between devices  91.5 us (14%)
  between operations  14.2 us (2%)
  matrix products  9.2 us (1%)
    reduce_scatter x1, waiting for transfers between devices, local(): lax.psum_scatter(jnp.stack([gate_part, up_part], axis=1).reshape(2 * hid_...  170 us
    reduce_scatter x1, waiting for transfers between devices, local(): lax.psum_scatter(term.reshape(hid_share * lax.axis_size('dp'), columns),...  117 us
    all_gather x1, blocking collectives, local(): pieces = lax.all_gather(hidden_own, 'dp', axis=0, tiled=True)  64.1 us
    all_gather x1, blocking collectives, local(): gate_piece = lax.all_gather(grad_pre_gate, 'dp', axis=0, tiled=True)  63.8 us
    all_gather x1, blocking collectives, local(): up_piece = lax.all_gather(grad_pre_up, 'dp', axis=0, tiled=True)  62.8 us
    all_to_all x1, starting transfers between devices, local(): lax.all_to_all(input_total, 'expert', split_axis=1, concat_axis=1, tiled=...  62.7 us
    all_to_all x1, blocking collectives, local(): lax.all_to_all(do_slots.reshape(slot_shape), 'expert', split_axis=0, conc...  33.5 us
    all_to_all x1, starting transfers between devices, local(): lax.all_to_all(out_total, 'expert', split_axis=1, concat_axis=1, tiled=True)  25 us
  transfers between devices with their start and end apart: 5, of which 4 were waited for; matrix products, arithmetic and copies ran while one was open for 1% of the time, Pallas kernels for 0%

commit v1 on v0

v1 whole, which is shorter than its diff:
```python
import jax
import jax.numpy as jnp
from jax import lax
from jax.sharding import PartitionSpec as P

HID = 1024
EXPERTS = 32
CAP = 8
BF16 = jnp.bfloat16
F32 = jnp.float32

route_scale = 2.5


def slot_weights(routes, scores):
    tok_count, top_count = routes.shape
    flat_routes = routes.reshape(-1)
    onehot = (flat_routes[:, None] == jnp.arange(EXPERTS, dtype=jnp.int32)[None, :]).astype(
        jnp.int32
    )
    before = jnp.cumsum(onehot, axis=0) - onehot
    slot_rank = jnp.sum(before * onehot, axis=1)
    slot_ids = flat_routes * CAP + slot_rank
    pick = (
        jnp.arange(EXPERTS * CAP, dtype=jnp.int32)[:, None] == slot_ids[None, :]
    ).reshape(EXPERTS * CAP, tok_count, top_count)
    gate_vals = route_scale * scores / jnp.sum(scores, axis=1, keepdims=True)
    select = jnp.sum(jnp.where(pick, 1.0, 0.0), axis=2)
    weighted = jnp.sum(jnp.where(pick, gate_vals[None], 0.0), axis=2)
    return select, weighted


def dp_groups():
    count = lax.axis_size("dp")
    inner = 4
    outer = count // inner
    inner_groups = [[o * inner + i for i in range(inner)] for o in range(outer)]
    outer_groups = [[o * inner + i for o in range(outer)] for i in range(inner)]
    return inner_groups, outer_groups


def spread(block, groups):
    size = len(groups[0])
    sent = jnp.broadcast_to(block[None], (size,) + block.shape)
    got = lax.all_to_all(
        sent, "dp", split_axis=0, concat_axis=0, axis_index_groups=groups, tiled=True
    )
    return got.reshape((-1,) + block.shape[1:])


def local(tokens, routes, scores, w_gate, w_up, w_down, cotangent):
    dp_count = lax.axis_size("dp")
    ex_count = lax.axis_size("expert")
    width = tokens.shape[1]
    slots = EXPERTS * CAP
    share = HID // dp_count
    cols = ex_count * CAP
    gate_w, up_w, down_w = w_gate[0], w_up[0], w_down[0]

    select, weighted = slot_weights(routes, scores)
    both = jnp.concatenate([tokens, cotangent], axis=1)
    picked = jnp.dot(select.astype(BF16), both, preferred_element_type=F32)
    slot_gate = jnp.sum(weighted, axis=1, keepdims=True)
    lane = lax.broadcasted_iota(jnp.int32, (1, 2 * width), 1)
    sent = (picked * jnp.where(lane < width, 1.0, slot_gate)).astype(BF16)
    rows = lax.all_to_all(
        sent.reshape(ex_count, CAP, 2 * width), "expert", split_axis=0, concat_axis=0, tiled=True
    ).reshape(cols, 2 * width)
    x_rows, do_rows = rows[:, :width], rows[:, width:]

    def part(w, r):
        return lax.dot_general(
            w, r, (((0,), (1,)), ((), ())), preferred_element_type=F32
        ).astype(BF16).reshape(dp_count, share, cols)

    parts = jnp.concatenate(
        [part(gate_w, x_rows), part(up_w, x_rows), part(down_w, do_rows)], axis=1
    )
    parts = lax.all_to_all(parts, "dp", split_axis=0, concat_axis=0, tiled=True)
    own = jnp.sum(parts.astype(F32), axis=0)
    pre_gate, pre_up, grad_hidden = own[:share], own[share : 2 * share], own[2 * share :]
    sigma = jax.nn.sigmoid(pre_gate)
    active = pre_gate * sigma
    block = jnp.concatenate(
        [
            active * pre_up,
            grad_hidden * pre_up * sigma * (1.0 + pre_gate * (1.0 - sigma)),
            grad_hidden * active,
        ],
        axis=0,
    ).astype(BF16)

    inner_groups, outer_groups = dp_groups()
    full = spread(spread(block, inner_groups), outer_groups).reshape(dp_count, 3, share, cols)
    hidden = full[:, 0].reshape(HID, cols)
    grad_gate_pre = full[:, 1].reshape(HID, cols)
    grad_up_pre = full[:, 2].reshape(HID, cols)

    def back(act, w):
        return lax.dot_general(act, w, (((0,), (1,)), ((), ())), preferred_element_type=F32)

    outs = jnp.concatenate(
        [back(hidden, down_w), back(grad_gate_pre, gate_w) + back(grad_up_pre, up_w)], axis=1
    ).astype(BF16)
    home = lax.all_to_all(
        outs.reshape(ex_count, CAP, 2 * width), "expert", split_axis=0, concat_axis=0, tiled=True
    ).reshape(slots, 2 * width).astype(F32)

    def weight_grad(r, act):
        return lax.dot_general(
            r, act, (((0,), (1,)), ((), ())), preferred_element_type=F32
        ).astype(BF16)[None]

    grad_gate = weight_grad(x_rows, grad_gate_pre)
    grad_up = weight_grad(x_rows, grad_up_pre)
    grad_down = weight_grad(do_rows, hidden)

    def combine(mix, vals):
        return lax.dot_general(
            mix, vals, (((0,), (0,)), ((), ())), precision=lax.Precision.HIGHEST
        ).astype(BF16)

    layer_out = combine(weighted, home[:, :width])
    grad_tokens = combine(select, home[:, width:])
    return layer_out, grad_tokens, grad_gate, grad_up, grad_down


def solution(mesh):
    rows = P("expert", "dp")
    table = P("expert", None)
    weight = P("expert", "dp", None)
    return jax.shard_map(
        local,
        mesh=mesh,
        in_specs=(rows, table, table, weight, weight, weight, rows),
        out_specs=(rows, rows, weight, weight, weight),
        check_vma=False,
    )
```

time: 661 us -> 173 us (0.26)
  waiting for transfers between devices: 312 us -> 11.8 us
  blocking collectives: 224 us -> 136 us
  starting transfers between devices: 91.5 us -> 9.27 us
  between operations: 14.2 us -> 0.84 us
    reduce_scatter x2 -> x0, waiting for transfers between devices: 287 us -> none  [the longest x1 170 us: local(): lax.psum_scatter(jnp.stack([gate_part, up_part], axis=1).reshape(2 * hid_...]
    all_gather x3 -> x0, blocking collectives: 191 us -> none  [the longest x1 64.1 us: local(): pieces = lax.all_gather(hidden_own, 'dp', axis=0, tiled=True)]
    all_to_all x1 -> x4, blocking collectives: 33.5 us -> 136 us  [the longest x1 52.3 us: local(): parts = lax.all_to_all(parts, 'dp', split_axis=0, concat_axis=0, tiled=True)]
    all_to_all x3 -> x1, starting transfers between devices: 91.4 us -> 9.27 us  [local(): lax.all_to_all(outs.reshape(ex_count, CAP, 2 * width), 'expert', split_ax...]
    all_to_all x3 -> x1, waiting for transfers between devices: 24.8 us -> 11.8 us  [local(): lax.all_to_all(outs.reshape(ex_count, CAP, 2 * width), 'expert', split_ax...]
  transfers between devices with their start and end apart: 5 -> 1, of which waited for: 4 -> 1; matrix products, arithmetic and copies ran while one was open for 1% -> 2% of each run, Pallas kernels for 0% -> 0%
where the time goes in v1:
time: 173 us; the launch traced here: 172 us
  blocking collectives  136 us (79%)
  waiting for transfers between devices  11.8 us (7%)
  starting transfers between devices  9.27 us (5%)
  matrix products  9.05 us (5%)
  other arithmetic  3.26 us (2%)
  local copies, waits for them, and re-layouts  2.31 us (1%)
    all_to_all x1, blocking collectives, local(): parts = lax.all_to_all(parts, 'dp', split_axis=0, concat_axis=0, tiled=True)  52.3 us
    all_to_all x2, blocking collectives, spread(): lax.all_to_all(sent, 'dp', split_axis=0, concat_axis=0, axis_index_groups...  47.5 us
    all_to_all x1, blocking collectives, local(): lax.all_to_all(sent.reshape(ex_count, CAP, 2 * width), 'expert', split_ax...  35.6 us
    all_to_all x1, waiting for transfers between devices, local(): lax.all_to_all(outs.reshape(ex_count, CAP, 2 * width), 'expert', split_ax...  11.8 us
    all_to_all x1, starting transfers between devices, local(): lax.all_to_all(outs.reshape(ex_count, CAP, 2 * width), 'expert', split_ax...  9.27 us
    dot_general x3, matrix products, weight_grad(): lax.dot_general(r, act, (((0,), (1,)), ((), ())), preferred_element_type=...  3.49 us
  transfers between devices with their start and end apart: 1, of which 1 were waited for; matrix products, arithmetic and copies ran while one was open for 2% of the time, Pallas kernels for 0%

profile of v1, /device:TPU:1, one launch (start us, length us, event | category | flops | bytes accessed | tf_op | source)
XLA Modules:
  0.0 172.1 jit_solution(9345322573910658530)
XLA Ops:
  0.6 0.0 copy-start
  0.6 0.0 copy-start.1
  0.7 0.8 reduce_sum.58
  1.5 0.7 multiply_divide_fusion
  2.1 0.1 copy.27
  2.2 0.8 copy.25
  3.0 0.1 eq.30
  3.1 0.1 fusion.24
  3.2 0.2 reduce_window_sum.11
  3.3 0.2 select_reduce_fusion.3
  3.5 0.1 reduce_sum.57
  3.6 0.2 select_reduce_fusion
  3.8 1.1 fusion.6
  4.8 0.0 copy-start.2
  4.9 0.1 copy.28
  5.0 35.6 %all_to_all.25 = bf16[32,8,448]{2,1,0:T(8,128)(2,1)S(1)} all-to-all(bf16[32,8,448]{2,1,0:T(8,128)(2,1)S(1)} %bitcast.70), channel_id=1, replica_groups=mesh['dp'=32,'expert'=32] {'expert'}, dimensions={0} | all-to-all | bytes 458752 | tf_op jit(solution)/shard_map/all_to_all | solution.py:66
  40.6 0.0 copy-done.1
  40.6 0.3 fusion.1
  40.9 0.2 copy.30
  41.2 0.0 copy-done.2
  41.2 0.3 fusion.2
  41.5 0.2 copy.31
  41.7 0.0 copy-done
  41.7 0.3 fusion
  42.0 0.2 copy.29
  42.2 0.1 pad_maximum_fusion
  42.4 52.3 %all_to_all.26 = bf16[32,96,256]{2,1,0:T(8,128)(2,1)S(1)} all-to-all(bf16[32,96,256]{2,1,0:T(8,128)(2,1)S(1)} %pad_maximum_fusion), channel_id=1, replica_groups=mesh['dp'=32,'expert'=32] {'dp'}, dimensions={0} | all-to-all | bytes 3145728 | tf_op jit(solution)/shard_map/all_to_all | solution.py:79
  94.7 0.2 convert_reduce_fusion
  95.0 9.1 %all_to_all.27 = bf16[4,96,256]{2,1,0:T(8,128)(2,1)S(1)} all-to-all(bf16[4,96,256]{2,1,0:T(8,128)(2,1)S(1)} %broadcast_in_dim.72), channel_id=1, replica_groups={{0,32,64,96},{128,160,192,224},{256,288,320,352},{384,416,448,480},{512..., dimensions={0} | all-to-all | bytes 393216 | tf_op jit(solution)/shard_map/all_to_all | solution.py:45
  104.1 0.1 broadcast_in_dim.74
  104.2 38.4 %all_to_all.28 = bf16[8,384,256]{2,1,0:T(8,128)(2,1)S(1)} all-to-all(bf16[8,384,256]{2,1,0:T(8,128)(2,1)S(1)} %broadcast_in_dim.74), channel_id=1, replica_groups={{0,128,256,384,512,640,768,896},{32,160,288,416,544,672,800,928},{64,19..., dimensions={0} | all-to-all | bytes 3145728 | tf_op jit(solution)/shard_map/all_to_all | solution.py:45
  142.6 0.1 fusion.31
  142.8 0.3 fusion.13
  143.0 0.3 fusion.7
  143.3 0.1 copy.33
  143.5 0.2 copy.32
  143.7 1.4 convolution_convert_fusion.6
  145.0 0.8 pad_maximum_fusion.1
  145.8 9.3 %all-to-all-start.4 = ((bf16[32,8,448]{2,1,0:T(8,128)(2,1)}), bf16[32,8,448]{2,1,0:T(8,128)(2,1)S(1)}, u32[]{:S(2)}, u32[]{:S(2)}) async-start(bf16[32,8,448]{2,1,0:T(8,128)(2,1)} %pad_maximum_fusion.1), calls=%async_computation.4 | async-start | bytes 524288 | tf_op jit(solution)/shard_map/all_to_all | solution.py:105
  155.1 1.1 fusion.4
  156.2 1.1 fusion.3
  157.4 1.2 fusion.5
  158.6 11.8 %all-to-all-done.4 = bf16[32,8,448]{2,1,0:T(8,128)(2,1)S(1)} async-done(((bf16[32,8,448]{2,1,0:T(8,128)(2,1)}), bf16[32,8,448]{2,1,0:T(8,128)(2,1)S(1)}, u32[]{:S(2)}, u32[]{:S(2)}) %all-to-all-start.4) | async-done | bytes 229408 | tf_op jit(solution)/shard_map/all_to_all | solution.py:105
  170.5 0.9 convolution_convert_fusion.7
  171.3 0.8 convolution_convert_fusion.8
  (5 shorter events, 0.1 us)
Async XLA Ops:
  0.6 41.1 %copy-start = (bf16[1,224,1024]{2,1,0:T(8,128)(2,1)S(1)}, bf16[1,224,1024]{2,1,0:T(8,128)(2,1)}, u32[]{:S(2)}) copy-start(bf16[1,224,1024]{2,1,0:T(8,128)(2,1)} %param.10) | copy-start | bytes 1376260
  0.6 40.0 %copy-start.1 = (bf16[1,224,1024]{2,1,0:T(8,128)(2,1)S(1)}, bf16[1,224,1024]{2,1,0:T(8,128)(2,1)}, u32[]{:S(2)}) copy-start(bf16[1,224,1024]{2,1,0:T(8,128)(2,1)} %param.11) | copy-start | bytes 1376260
  4.8 36.3 %copy-start.2 = (bf16[1,224,1024]{2,1,0:T(8,128)(2,1)S(1)}, bf16[1,224,1024]{2,1,0:T(8,128)(2,1)}, u32[]{:S(2)}) copy-start(bf16[1,224,1024]{2,1,0:T(8,128)(2,1)} %param.12) | copy-start | bytes 1376260
  145.8 24.6 %all-to-all-start.4 = ((bf16[32,8,448]{2,1,0:T(8,128)(2,1)}), bf16[32,8,448]{2,1,0:T(8,128)(2,1)S(1)}, u32[]{:S(2)}, u32[]{:S(2)}) async-start(bf16[32,8,448]{2,1,0:T(8,128)(2,1)} %pad_maximum_fusion.1), calls=%async_computation.4 | async-start | bytes 524288 | tf_op jit(solution)/shard_map/all_to_all | solution.py:105

commit v2 on v1

--- a/solution.py
+++ b/solution.py
@@ -30,22 +30,76 @@
     return select, weighted
 
 
-def dp_groups():
-    count = lax.axis_size("dp")
-    inner = 4
-    outer = count // inner
-    inner_groups = [[o * inner + i for i in range(inner)] for o in range(outer)]
-    outer_groups = [[o * inner + i for o in range(outer)] for i in range(inner)]
-    return inner_groups, outer_groups
+INNER = 4
 
 
-def spread(block, groups):
-    size = len(groups[0])
-    sent = jnp.broadcast_to(block[None], (size,) + block.shape)
-    got = lax.all_to_all(
-        sent, "dp", split_axis=0, concat_axis=0, axis_index_groups=groups, tiled=True
+def y_groups():
+    outer = lax.axis_size("dp") // INNER
+    return [[o * INNER + i for o in range(outer)] for i in range(INNER)]
+
+
+def y_swap(blocks):
+    return lax.all_to_all(
+        blocks, "dp", split_axis=0, concat_axis=0, axis_index_groups=y_groups(), tiled=True
     )
-    return got.reshape((-1,) + block.shape[1:])
+
+
+def z_send(block, step):
+    pairs = [
+        (d, d // INNER * INNER + (d + step) % INNER) for d in range(lax.axis_size("dp"))
+    ]
+    return lax.ppermute(block, "dp", pairs)
+
+
+def z_place():
+    return lax.rem(lax.axis_index("dp"), INNER)
+
+
+def z_reduce(blocks):
+    place = z_place()
+    got = [
+        z_send(
+            lax.dynamic_index_in_dim(blocks, lax.rem(place + step, INNER), 0, keepdims=False), step
+        )
+        for step in range(1, INNER)
+    ]
+    total = lax.dynamic_index_in_dim(blocks, place, 0, keepdims=False).astype(F32)
+    for block in got:
+        total = total + block.astype(F32)
+    return total
+
+
+def z_gather(block):
+    place = z_place()
+    full = jnp.zeros((INNER,) + block.shape, block.dtype)
+    full = lax.dynamic_update_index_in_dim(full, block, place, 0)
+    for step in range(1, INNER):
+        full = lax.dynamic_update_index_in_dim(
+            full, z_send(block, step), lax.rem(place + INNER - step, INNER), 0
+        )
+    return full
+
+
+def y_reduce(blocks):
+    return jnp.sum(y_swap(blocks).astype(F32), axis=0)
+
+
+def y_gather(block):
+    outer = lax.axis_size("dp") // INNER
+    return y_swap(jnp.broadcast_to(block[None], (outer,) + block.shape))
+
+
+def pointwise(own):
+    pre_gate, pre_up, grad_hidden = own[0], own[1], own[2]
+    sigma = jax.nn.sigmoid(pre_gate)
+    active = pre_gate * sigma
+    return jnp.stack(
+        [
+            active * pre_up,
+            grad_hidden * pre_up * sigma * (1.0 + pre_gate * (1.0 - sigma)),
+            grad_hidden * active,
+        ]
+    ).astype(BF16)
 
 
 def local(tokens, routes, scores, w_gate, w_up, w_down, cotangent):
@@ -53,7 +107,6 @@
     ex_count = lax.axis_size("expert")
     width = tokens.shape[1]
     slots = EXPERTS * CAP
-    share = HID // dp_count
     cols = ex_count * CAP
     gate_w, up_w, down_w = w_gate[0], w_up[0], w_down[0]
 
@@ -68,33 +121,32 @@
     ).reshape(cols, 2 * width)
     x_rows, do_rows = rows[:, :width], rows[:, width:]
 
+    outer = dp_count // INNER
+    half = HID // 2
+    rows_each = half // dp_count
+
     def part(w, r):
         return lax.dot_general(
             w, r, (((0,), (1,)), ((), ())), preferred_element_type=F32
-        ).astype(BF16).reshape(dp_count, share, cols)
+        ).astype(BF16)
 
-    parts = jnp.concatenate(
-        [part(gate_w, x_rows), part(up_w, x_rows), part(down_w, do_rows)], axis=1
-    )
-    parts = lax.all_to_all(parts, "dp", split_axis=0, concat_axis=0, tiled=True)
-    own = jnp.sum(parts.astype(F32), axis=0)
-    pre_gate, pre_up, grad_hidden = own[:share], own[share : 2 * share], own[2 * share :]
-    sigma = jax.nn.sigmoid(pre_gate)
-    active = pre_gate * sigma
-    block = jnp.concatenate(
-        [
-            active * pre_up,
-            grad_hidden * pre_up * sigma * (1.0 + pre_gate * (1.0 - sigma)),
-            grad_hidden * active,
-        ],
-        axis=0,
-    ).astype(BF16)
+    parts = [part(gate_w, x_rows), part(up_w, x_rows), part(down_w, do_rows)]
+    a = jnp.stack([p[:half].reshape(outer, INNER, rows_each, cols) for p in parts], axis=2)
+    b = jnp.stack([p[half:].reshape(INNER, outer, rows_each, cols) for p in parts], axis=2)
+    a, b = y_reduce(a), z_reduce(b).astype(BF16)
+    a, b = lax.optimization_barrier((a, b))
+    a, b = pointwise(z_reduce(a)), pointwise(y_reduce(b))
+    a, b = lax.optimization_barrier((a, b))
+    a, b = z_gather(a), y_gather(b)
+    a, b = lax.optimization_barrier((a, b))
+    a, b = y_gather(a), z_gather(b)
 
-    inner_groups, outer_groups = dp_groups()
-    full = spread(spread(block, inner_groups), outer_groups).reshape(dp_count, 3, share, cols)
-    hidden = full[:, 0].reshape(HID, cols)
-    grad_gate_pre = full[:, 1].reshape(HID, cols)
-    grad_up_pre = full[:, 2].reshape(HID, cols)
+    def whole(index):
+        return jnp.concatenate(
+            [a[:, :, index].reshape(half, cols), b[:, :, index].reshape(half, cols)], axis=0
+        )
+
+    hidden, grad_gate_pre, grad_up_pre = whole(0), whole(1), whole(2)
 
     def back(act, w):
         return lax.dot_general(act, w, (((0,), (1,)), ((), ())), preferred_element_type=F32)

time: 173 us -> 181 us (1.046)
  blocking collectives: 136 us -> 35.6 us
  starting transfers between devices: 9.27 us -> 68.1 us
  waiting for transfers between devices: 11.8 us -> 53.5 us
  local copies, waits for them, and re-layouts: 2.31 us -> 9.12 us
    all_to_all x3 -> x0, blocking collectives: 99.9 us -> none  [the longest x1 52.3 us: local(): parts = lax.all_to_all(parts, 'dp', split_axis=0, concat_axis=0, tiled=True)]
    ppermute x0 -> x12, starting transfers between devices: none -> 39.5 us  [z_send(): return lax.ppermute(block, 'dp', pairs)]
    all_to_all x0 -> x4, waiting for transfers between devices: none -> 21.8 us  [y_swap(): lax.all_to_all(blocks, 'dp', split_axis=0, concat_axis=0, axis_index_grou...]
    all_to_all x0 -> x4, starting transfers between devices: none -> 20.9 us  [y_swap(): lax.all_to_all(blocks, 'dp', split_axis=0, concat_axis=0, axis_index_grou...]
    ppermute x0 -> x12, waiting for transfers between devices: none -> 19.8 us  [z_send(): return lax.ppermute(block, 'dp', pairs)]
    unnamed x7 -> x21, local copies, waits for them, and re-layouts: 0.78 us -> 3.12 us
  transfers between devices with their start and end apart: 1 -> 17, of which waited for: 1 -> 9; matrix products, arithmetic and copies ran while one was open for 2% -> 4% of each run, Pallas kernels for 0% -> 0%
where the time goes in v2:
time: 181 us; the launch traced here: 180 us
  starting transfers between devices  68.1 us (38%)
  waiting for transfers between devices  53.5 us (30%)
  blocking collectives  35.6 us (20%)
  local copies, waits for them, and re-layouts  9.12 us (5%)
  matrix products  8.03 us (4%)
  other arithmetic  4.32 us (2%)
    ppermute x12, starting transfers between devices, z_send(): return lax.ppermute(block, 'dp', pairs)  39.5 us
    all_to_all x1, blocking collectives, local(): lax.all_to_all(sent.reshape(ex_count, CAP, 2 * width), 'expert', split_ax...  35.6 us
    all_to_all x4, waiting for transfers between devices, y_swap(): lax.all_to_all(blocks, 'dp', split_axis=0, concat_axis=0, axis_index_grou...  21.8 us
    all_to_all x4, starting transfers between devices, y_swap(): lax.all_to_all(blocks, 'dp', split_axis=0, concat_axis=0, axis_index_grou...  20.9 us
    ppermute x12, waiting for transfers between devices, z_send(): return lax.ppermute(block, 'dp', pairs)  19.8 us
    all_to_all x1, waiting for transfers between devices, local(): lax.all_to_all(outs.reshape(ex_count, CAP, 2 * width), 'expert', split_ax...  11.9 us
    all_to_all x1, starting transfers between devices, local(): lax.all_to_all(outs.reshape(ex_count, CAP, 2 * width), 'expert', split_ax...  7.77 us
  transfers between devices with their start and end apart: 17, of which 9 were waited for; matrix products, arithmetic and copies ran while one was open for 4% of the time, Pallas kernels for 0%

profile of v2, /device:TPU:1, one launch (start us, length us, event | category | flops | bytes accessed | tf_op | source)
XLA Modules:
  0.0 179.9 jit_solution(13405842164179329257)
XLA Ops:
  0.7 0.8 reduce_sum.67
  1.4 0.7 multiply_divide_fusion
  2.2 0.8 copy.63
  3.1 0.2 reduce_window_sum.11
  3.3 0.2 select_reduce_fusion.3
  3.6 0.2 select_reduce_fusion
  3.8 0.6 copy-done.8
  4.3 1.1 fusion.6
  5.4 0.1 copy.66
  5.6 35.6 %all_to_all.30 = bf16[32,8,448]{2,1,0:T(8,128)(2,1)S(1)} all-to-all(bf16[32,8,448]{2,1,0:T(8,128)(2,1)S(1)} %bitcast.102), channel_id=1, replica_groups=mesh['dp'=32,'expert'=32] {'expert'}, dimensions={0} | all-to-all | bytes 458752 | tf_op jit(solution)/shard_map/all_to_all | solution.py:119
  41.2 0.3 fusion.1
  41.6 0.1 copy.68
  41.7 0.8 copy-done.1
  42.5 0.3 fusion.2
  42.9 0.1 copy.69
  43.1 0.3 fusion
  43.4 0.1 copy.67
  43.6 1.0 copy.70
  44.6 7.3 %all-to-all-start.1 = ((bf16[8,4,3,16,256]{4,3,1,2,0:T(8,128)(2,1)}), bf16[8,4,3,16,256]{4,3,1,2,0:T(8,128)(2,1)S(1)}, u32[]{:S(2)}, u32[]{:S(2)}) async-start(bf16[8,4,3,16,256]{4,3,1,2,0:T(8,128)(2,1)} %copy.70), calls=%async_computation.1 | async-start | bytes 1572864 | tf_op jit(solution)/shard_map/all_to_all | solution.py:42
  51.9 0.1 copy.73
  52.0 0.1 copy.74
  52.2 0.1 copy.72
  52.4 0.7 dynamic-slice_bitcast_fusion.2
  53.1 4.0 %collective-permute-start = (bf16[8,3,16,256]{3,2,0,1:T(8,128)(2,1)}, bf16[8,3,16,256]{3,2,0,1:T(8,128)(2,1)S(1)}, u32[]{:S(2)}, u32[]{:S(2)}) collective-permute-start(bf16[8,3,16,256]{3,2,0,1:T(8,128)(2,1)} %get-tuple-element.26), channel_id=1, source_target_pairs={{0,32},{32,64},{64,96},{96,0},{128,160},{160,192},{192,224},{224,1... | collective-permute-start | bytes 589832 | tf_op jit(solution)/shard_map/ppermute | solution.py:51
  57.1 5.6 %collective-permute-start.2 = (bf16[8,3,16,256]{3,2,0,1:T(8,128)(2,1)S(1)}, bf16[8,3,16,256]{3,2,0,1:T(8,128)(2,1)S(1)}, u32[]{:S(2)}, u32[]{:S(2)}) collective-permute-start(bf16[8,3,16,256]{3,2,0,1:T(8,128)(2,1)S(1)} %get-tuple-element.27), channel_id=1, source_target_pairs={{0,96},{32,0},{64,32},{96,64},{128,224},{160,128},{192,160},{224,1... | collective-permute-start | bytes 589832 | tf_op jit(solution)/shard_map/ppermute | solution.py:51
  62.7 2.2 %collective-permute-start.1 = (bf16[8,3,16,256]{3,2,0,1:T(8,128)(2,1)S(1)}, bf16[8,3,16,256]{3,2,0,1:T(8,128)(2,1)}, u32[]{:S(2)}, u32[]{:S(2)}) collective-permute-start(bf16[8,3,16,256]{3,2,0,1:T(8,128)(2,1)S(1)} %get-tuple-element.28), channel_id=1, source_target_pairs={{0,64},{32,96},{64,0},{96,32},{128,192},{160,224},{192,128},{224,1... | collective-permute-start | bytes 589832 | tf_op jit(solution)/shard_map/ppermute | solution.py:51
  64.9 0.7 collective-permute-done
  65.6 4.9 %collective-permute-done.2 = bf16[8,3,16,256]{3,2,0,1:T(8,128)(2,1)S(1)} collective-permute-done((bf16[8,3,16,256]{3,2,0,1:T(8,128)(2,1)S(1)}, bf16[8,3,16,256]{3,2,0,1:T(8,128)(2,1)S(1)}, u32[]{:S(2)}, u32[]{:S(2)}) %collective-permute-start.2) | collective-permute-done | bytes 196640 | tf_op jit(solution)/shard_map/ppermute | solution.py:51
  70.6 8.6 %collective-permute-done.1 = bf16[8,3,16,256]{3,2,0,1:T(8,128)(2,1)} collective-permute-done((bf16[8,3,16,256]{3,2,0,1:T(8,128)(2,1)S(1)}, bf16[8,3,16,256]{3,2,0,1:T(8,128)(2,1)}, u32[]{:S(2)}, u32[]{:S(2)}) %collective-permute-start.1) | collective-permute-done | bytes 196640 | tf_op jit(solution)/shard_map/ppermute | solution.py:51
  79.1 1.0 fusion.18
  80.3 1.9 %collective-permute-start.3 = (f32[3,16,256]{2,1,0:T(8,128)S(1)}, f32[3,16,256]{2,1,0:T(8,128)S(1)}, u32[]{:S(2)}, u32[]{:S(2)}) collective-permute-start(f32[3,16,256]{2,1,0:T(8,128)S(1)} %get-tuple-element.35), channel_id=1, source_target_pairs={{0,32},{32,64},{64,96},{96,0},{128,160},{160,192},{192,224},{224,1... | collective-permute-start | bytes 147464 | tf_op jit(solution)/shard_map/ppermute | solution.py:51
  82.2 5.2 %collective-permute-start.5 = (f32[3,16,256]{2,1,0:T(8,128)S(1)}, f32[3,16,256]{2,1,0:T(8,128)S(1)}, u32[]{:S(2)}, u32[]{:S(2)}) collective-permute-start(f32[3,16,256]{2,1,0:T(8,128)S(1)} %get-tuple-element.36), channel_id=1, source_target_pairs={{0,96},{32,0},{64,32},{96,64},{128,224},{160,128},{192,160},{224,1... | collective-permute-start | bytes 147464 | tf_op jit(solution)/shard_map/ppermute | solution.py:51
  87.4 1.9 %collective-permute-start.4 = (f32[3,16,256]{2,1,0:T(8,128)S(1)}, f32[3,16,256]{2,1,0:T(8,128)S(1)}, u32[]{:S(2)}, u32[]{:S(2)}) collective-permute-start(f32[3,16,256]{2,1,0:T(8,128)S(1)} %get-tuple-element.37), channel_id=1, source_target_pairs={{0,64},{32,96},{64,0},{96,32},{128,192},{160,224},{192,128},{224,1... | collective-permute-start | bytes 147464 | tf_op jit(solution)/shard_map/ppermute | solution.py:51
  89.3 0.7 copy.75
  90.0 6.6 %all-to-all-start.2 = ((bf16[8,3,16,256]{3,2,1,0:T(8,128)(2,1)}), bf16[8,3,16,256]{3,2,1,0:T(8,128)(2,1)S(1)}, u32[]{:S(2)}, u32[]{:S(2)}) async-start(bf16[8,3,16,256]{3,2,1,0:T(8,128)(2,1)} %copy.75), calls=%async_computation.2 | async-start | bytes 393216 | tf_op jit(solution)/shard_map/all_to_all | solution.py:42
  96.7 8.3 %all-to-all-done.2 = bf16[8,3,16,256]{3,2,1,0:T(8,128)(2,1)S(1)} async-done(((bf16[8,3,16,256]{3,2,1,0:T(8,128)(2,1)}), bf16[8,3,16,256]{3,2,1,0:T(8,128)(2,1)S(1)}, u32[]{:S(2)}, u32[]{:S(2)}) %all-to-all-start.2) | async-done | bytes 196640 | tf_op jit(solution)/shard_map/all_to_all | solution.py:42
  105.1 2.2 %collective-permute-start.8 = (bf16[3,16,256]{2,1,0:T(8,128)(2,1)S(1)}, bf16[3,16,256]{2,1,0:T(8,128)(2,1)S(1)}, u32[]{:S(2)}, u32[]{:S(2)}) collective-permute-start(bf16[3,16,256]{2,1,0:T(8,128)(2,1)S(1)} %get-tuple-element.13), channel_id=1, source_target_pairs={{0,96},{32,0},{64,32},{96,64},{128,224},{160,128},{192,160},{224,1... | collective-permute-start | bytes 73736 | tf_op jit(solution)/shard_map/ppermute | solution.py:51
  107.3 4.2 %collective-permute-start.7 = (bf16[3,16,256]{2,1,0:T(8,128)(2,1)S(1)}, bf16[3,16,256]{2,1,0:T(8,128)(2,1)S(1)}, u32[]{:S(2)}, u32[]{:S(2)}) collective-permute-start(bf16[3,16,256]{2,1,0:T(8,128)(2,1)S(1)} %get-tuple-element.13), channel_id=1, source_target_pairs={{0,64},{32,96},{64,0},{96,32},{128,192},{160,224},{192,128},{224,1... | collective-permute-start | bytes 73736 | tf_op jit(solution)/shard_map/ppermute | solution.py:51
  111.5 3.4 %collective-permute-start.6 = (bf16[3,16,256]{2,1,0:T(8,128)(2,1)S(1)}, bf16[3,16,256]{2,1,0:T(8,128)(2,1)S(1)}, u32[]{:S(2)}, u32[]{:S(2)}) collective-permute-start(bf16[3,16,256]{2,1,0:T(8,128)(2,1)S(1)} %get-tuple-element.13), channel_id=1, source_target_pairs={{0,32},{32,64},{64,96},{96,0},{128,160},{160,192},{192,224},{224,1... | collective-permute-start | bytes 73736 | tf_op jit(solution)/shard_map/ppermute | solution.py:51
  114.9 0.7 broadcast_in_dim.108
  115.6 3.4 %all-to-all-start.3 = ((bf16[8,3,16,256]{3,2,1,0:T(8,128)(2,1)}), bf16[8,3,16,256]{3,2,1,0:T(8,128)(2,1)S(1)}, u32[]{:S(2)}, u32[]{:S(2)}) async-start(bf16[8,3,16,256]{3,2,1,0:T(8,128)(2,1)} %broadcast_in_dim.108), calls=%async_computation.3 | async-start | bytes 393216 | tf_op jit(solution)/shard_map/all_to_all | solution.py:42
  119.1 8.5 %all-to-all-done.3 = bf16[8,3,16,256]{3,2,1,0:T(8,128)(2,1)S(1)} async-done(((bf16[8,3,16,256]{3,2,1,0:T(8,128)(2,1)}), bf16[8,3,16,256]{3,2,1,0:T(8,128)(2,1)S(1)}, u32[]{:S(2)}, u32[]{:S(2)}) %all-to-all-start.3) | async-done | bytes 196640 | tf_op jit(solution)/shard_map/all_to_all | solution.py:42
  127.6 1.0 broadcast_in_dim.109
  128.5 3.5 %all-to-all-start.4 = ((bf16[8,4,3,16,256]{4,3,1,2,0:T(8,128)(2,1)}), bf16[8,4,3,16,256]{4,3,1,2,0:T(8,128)(2,1)S(1)}, u32[]{:S(2)}, u32[]{:S(2)}) async-start(bf16[8,4,3,16,256]{4,3,1,2,0:T(8,128)(2,1)} %broadcast_in_dim.109), calls=%async_computation.4 | async-start | bytes 1572864 | tf_op jit(solution)/shard_map/all_to_all | solution.py:42
  132.1 1.9 %collective-permute-start.10 = (bf16[8,3,16,256]{3,2,0,1:T(8,128)(2,1)S(1)}, bf16[8,3,16,256]{3,2,0,1:T(8,128)(2,1)S(1)}, u32[]{:S(2)}, u32[]{:S(2)}) collective-permute-start(bf16[8,3,16,256]{3,2,0,1:T(8,128)(2,1)S(1)} %copy.77), channel_id=1, source_target_pairs={{0,64},{32,96},{64,0},{96,32},{128,192},{160,224},{192,128},{224,1... | collective-permute-start | bytes 589832 | tf_op jit(solution)/shard_map/ppermute | solution.py:51
  134.0 4.0 %collective-permute-start.9 = (bf16[8,3,16,256]{3,2,0,1:T(8,128)(2,1)S(1)}, bf16[8,3,16,256]{3,2,0,1:T(8,128)(2,1)S(1)}, u32[]{:S(2)}, u32[]{:S(2)}) collective-permute-start(bf16[8,3,16,256]{3,2,0,1:T(8,128)(2,1)S(1)} %copy.77), channel_id=1, source_target_pairs={{0,32},{32,64},{64,96},{96,0},{128,160},{160,192},{192,224},{224,1... | collective-permute-start | bytes 589832 | tf_op jit(solution)/shard_map/ppermute | solution.py:51
  138.1 3.1 %collective-permute-start.11 = (bf16[8,3,16,256]{3,2,0,1:T(8,128)(2,1)S(1)}, bf16[8,3,16,256]{3,2,0,1:T(8,128)(2,1)S(1)}, u32[]{:S(2)}, u32[]{:S(2)}) collective-permute-start(bf16[8,3,16,256]{3,2,0,1:T(8,128)(2,1)S(1)} %copy.77), channel_id=1, source_target_pairs={{0,96},{32,0},{64,32},{96,64},{128,224},{160,128},{192,160},{224,1... | collective-permute-start | bytes 589832 | tf_op jit(solution)/shard_map/ppermute | solution.py:51
  141.2 1.3 collective-permute-done.9
  142.5 4.3 %collective-permute-done.10 = bf16[8,3,16,256]{3,2,0,1:T(8,128)(2,1)S(1)} collective-permute-done((bf16[8,3,16,256]{3,2,0,1:T(8,128)(2,1)S(1)}, bf16[8,3,16,256]{3,2,0,1:T(8,128)(2,1)S(1)}, u32[]{:S(2)}, u32[]{:S(2)}) %collective-permute-start.10) | collective-permute-done | bytes 196640 | tf_op jit(solution)/shard_map/ppermute | solution.py:51
  147.0 5.0 %all-to-all-done.4 = bf16[8,4,3,16,256]{4,3,1,2,0:T(8,128)(2,1)S(1)} async-done(((bf16[8,4,3,16,256]{4,3,1,2,0:T(8,128)(2,1)}), bf16[8,4,3,16,256]{4,3,1,2,0:T(8,128)(2,1)S(1)}, u32[]{:S(2)}, u32[]{:S(2)}) %all-to-all-start.4) | async-done | bytes 786464 | tf_op jit(solution)/shard_map/all_to_all | solution.py:42
  152.1 0.3 fusion.13
  152.4 0.4 copy-done.6
  152.8 0.5 copy-done.3
  153.3 0.3 fusion.7
  153.8 0.2 copy.81
  154.0 0.3 convolution_convert_fusion.6
  154.3 0.8 pad_maximum_fusion.10
  155.2 7.8 %all-to-all-start.5 = ((bf16[32,8,448]{2,1,0:T(8,128)(2,1)}), bf16[32,8,448]{2,1,0:T(8,128)(2,1)S(1)}, u32[]{:S(2)}, u32[]{:S(2)}) async-start(bf16[32,8,448]{2,1,0:T(8,128)(2,1)} %pad_maximum_fusion.10), calls=%async_computation.5 | async-start | bytes 524288 | tf_op jit(solution)/shard_map/all_to_all | solution.py:157
  162.9 1.1 fusion.4
  164.1 1.1 fusion.3
  165.2 1.2 fusion.5
  166.4 11.9 %all-to-all-done.5 = bf16[32,8,448]{2,1,0:T(8,128)(2,1)S(1)} async-done(((bf16[32,8,448]{2,1,0:T(8,128)(2,1)}), bf16[32,8,448]{2,1,0:T(8,128)(2,1)S(1)}, u32[]{:S(2)}, u32[]{:S(2)}) %all-to-all-start.5) | async-done | bytes 229408 | tf_op jit(solution)/shard_map/all_to_all | solution.py:157
  178.3 0.9 convolution_convert_fusion.7
  179.2 0.8 convolution_convert_fusion.8
  (57 shorter events, 1.4 us)
Async XLA Ops:
  0.6 42.4 %copy-start = (bf16[1,224,1024]{2,1,0:T(8,128)(2,1)S(1)}, bf16[1,224,1024]{2,1,0:T(8,128)(2,1)}, u32[]{:S(2)}) copy-start(bf16[1,224,1024]{2,1,0:T(8,128)(2,1)} %param.10) | copy-start | bytes 1376260
  3.3 37.9 %copy-start.2 = (bf16[1,224,1024]{2,1,0:T(8,128)(2,1)S(1)}, bf16[1,224,1024]{2,1,0:T(8,128)(2,1)}, u32[]{:S(2)}) copy-start(bf16[1,224,1024]{2,1,0:T(8,128)(2,1)} %param.11) | copy-start | bytes 1376260
  3.7 0.6 copy-start.8
  41.5 1.0 copy-start.1
  44.6 35.5 %all-to-all-start.1 = ((bf16[8,4,3,16,256]{4,3,1,2,0:T(8,128)(2,1)}), bf16[8,4,3,16,256]{4,3,1,2,0:T(8,128)(2,1)S(1)}, u32[]{:S(2)}, u32[]{:S(2)}) async-start(bf16[8,4,3,16,256]{4,3,1,2,0:T(8,128)(2,1)} %copy.70), calls=%async_computation.1 | async-start | bytes 1572864 | tf_op jit(solution)/shard_map/all_to_all | solution.py:42
  53.1 12.5 %collective-permute-start = (bf16[8,3,16,256]{3,2,0,1:T(8,128)(2,1)}, bf16[8,3,16,256]{3,2,0,1:T(8,128)(2,1)S(1)}, u32[]{:S(2)}, u32[]{:S(2)}) collective-permute-start(bf16[8,3,16,256]{3,2,0,1:T(8,128)(2,1)} %get-tuple-element.26), channel_id=1, source_target_pairs={{0,32},{32,64},{64,96},{96,0},{128,160},{160,192},{192,224},{224,1... | collective-permute-start | bytes 589832 | tf_op jit(solution)/shard_map/ppermute | solution.py:51
  57.1 13.4 %collective-permute-start.2 = (bf16[8,3,16,256]{3,2,0,1:T(8,128)(2,1)S(1)}, bf16[8,3,16,256]{3,2,0,1:T(8,128)(2,1)S(1)}, u32[]{:S(2)}, u32[]{:S(2)}) collective-permute-start(bf16[8,3,16,256]{3,2,0,1:T(8,128)(2,1)S(1)} %get-tuple-element.27), channel_id=1, source_target_pairs={{0,96},{32,0},{64,32},{96,64},{128,224},{160,128},{192,160},{224,1... | collective-permute-start | bytes 589832 | tf_op jit(solution)/shard_map/ppermute | solution.py:51
  62.7 16.4 %collective-permute-start.1 = (bf16[8,3,16,256]{3,2,0,1:T(8,128)(2,1)S(1)}, bf16[8,3,16,256]{3,2,0,1:T(8,128)(2,1)}, u32[]{:S(2)}, u32[]{:S(2)}) collective-permute-start(bf16[8,3,16,256]{3,2,0,1:T(8,128)(2,1)S(1)} %get-tuple-element.28), channel_id=1, source_target_pairs={{0,64},{32,96},{64,0},{96,32},{128,192},{160,224},{192,128},{224,1... | collective-permute-start | bytes 589832 | tf_op jit(solution)/shard_map/ppermute | solution.py:51
  80.3 16.4 %collective-permute-start.3 = (f32[3,16,256]{2,1,0:T(8,128)S(1)}, f32[3,16,256]{2,1,0:T(8,128)S(1)}, u32[]{:S(2)}, u32[]{:S(2)}) collective-permute-start(f32[3,16,256]{2,1,0:T(8,128)S(1)} %get-tuple-element.35), channel_id=1, source_target_pairs={{0,32},{32,64},{64,96},{96,0},{128,160},{160,192},{192,224},{224,1... | collective-permute-start | bytes 147464 | tf_op jit(solution)/shard_map/ppermute | solution.py:51
  82.2 14.4 %collective-permute-start.5 = (f32[3,16,256]{2,1,0:T(8,128)S(1)}, f32[3,16,256]{2,1,0:T(8,128)S(1)}, u32[]{:S(2)}, u32[]{:S(2)}) collective-permute-start(f32[3,16,256]{2,1,0:T(8,128)S(1)} %get-tuple-element.36), channel_id=1, source_target_pairs={{0,96},{32,0},{64,32},{96,64},{128,224},{160,128},{192,160},{224,1... | collective-permute-start | bytes 147464 | tf_op jit(solution)/shard_map/ppermute | solution.py:51
  87.4 9.3 %collective-permute-start.4 = (f32[3,16,256]{2,1,0:T(8,128)S(1)}, f32[3,16,256]{2,1,0:T(8,128)S(1)}, u32[]{:S(2)}, u32[]{:S(2)}) collective-permute-start(f32[3,16,256]{2,1,0:T(8,128)S(1)} %get-tuple-element.37), channel_id=1, source_target_pairs={{0,64},{32,96},{64,0},{96,32},{128,192},{160,224},{192,128},{224,1... | collective-permute-start | bytes 147464 | tf_op jit(solution)/shard_map/ppermute | solution.py:51
  90.0 15.0 %all-to-all-start.2 = ((bf16[8,3,16,256]{3,2,1,0:T(8,128)(2,1)}), bf16[8,3,16,256]{3,2,1,0:T(8,128)(2,1)S(1)}, u32[]{:S(2)}, u32[]{:S(2)}) async-start(bf16[8,3,16,256]{3,2,1,0:T(8,128)(2,1)} %copy.75), calls=%async_computation.2 | async-start | bytes 393216 | tf_op jit(solution)/shard_map/all_to_all | solution.py:42
  105.1 14.0 %collective-permute-start.8 = (bf16[3,16,256]{2,1,0:T(8,128)(2,1)S(1)}, bf16[3,16,256]{2,1,0:T(8,128)(2,1)S(1)}, u32[]{:S(2)}, u32[]{:S(2)}) collective-permute-start(bf16[3,16,256]{2,1,0:T(8,128)(2,1)S(1)} %get-tuple-element.13), channel_id=1, source_target_pairs={{0,96},{32,0},{64,32},{96,64},{128,224},{160,128},{192,160},{224,1... | collective-permute-start | bytes 73736 | tf_op jit(solution)/shard_map/ppermute | solution.py:51
  107.3 11.7 %collective-permute-start.7 = (bf16[3,16,256]{2,1,0:T(8,128)(2,1)S(1)}, bf16[3,16,256]{2,1,0:T(8,128)(2,1)S(1)}, u32[]{:S(2)}, u32[]{:S(2)}) collective-permute-start(bf16[3,16,256]{2,1,0:T(8,128)(2,1)S(1)} %get-tuple-element.13), channel_id=1, source_target_pairs={{0,64},{32,96},{64,0},{96,32},{128,192},{160,224},{192,128},{224,1... | collective-permute-start | bytes 73736 | tf_op jit(solution)/shard_map/ppermute | solution.py:51
  111.5 7.5 %collective-permute-start.6 = (bf16[3,16,256]{2,1,0:T(8,128)(2,1)S(1)}, bf16[3,16,256]{2,1,0:T(8,128)(2,1)S(1)}, u32[]{:S(2)}, u32[]{:S(2)}) collective-permute-start(bf16[3,16,256]{2,1,0:T(8,128)(2,1)S(1)} %get-tuple-element.13), channel_id=1, source_target_pairs={{0,32},{32,64},{64,96},{96,0},{128,160},{160,192},{192,224},{224,1... | collective-permute-start | bytes 73736 | tf_op jit(solution)/shard_map/ppermute | solution.py:51
  115.6 11.9 %all-to-all-start.3 = ((bf16[8,3,16,256]{3,2,1,0:T(8,128)(2,1)}), bf16[8,3,16,256]{3,2,1,0:T(8,128)(2,1)S(1)}, u32[]{:S(2)}, u32[]{:S(2)}) async-start(bf16[8,3,16,256]{3,2,1,0:T(8,128)(2,1)} %broadcast_in_dim.108), calls=%async_computation.3 | async-start | bytes 393216 | tf_op jit(solution)/shard_map/all_to_all | solution.py:42
  128.5 23.5 %all-to-all-start.4 = ((bf16[8,4,3,16,256]{4,3,1,2,0:T(8,128)(2,1)}), bf16[8,4,3,16,256]{4,3,1,2,0:T(8,128)(2,1)S(1)}, u32[]{:S(2)}, u32[]{:S(2)}) async-start(bf16[8,4,3,16,256]{4,3,1,2,0:T(8,128)(2,1)} %broadcast_in_dim.109), calls=%async_computation.4 | async-start | bytes 1572864 | tf_op jit(solution)/shard_map/all_to_all | solution.py:42
  132.1 14.7 %collective-permute-start.10 = (bf16[8,3,16,256]{3,2,0,1:T(8,128)(2,1)S(1)}, bf16[8,3,16,256]{3,2,0,1:T(8,128)(2,1)S(1)}, u32[]{:S(2)}, u32[]{:S(2)}) collective-permute-start(bf16[8,3,16,256]{3,2,0,1:T(8,128)(2,1)S(1)} %copy.77), channel_id=1, source_target_pairs={{0,64},{32,96},{64,0},{96,32},{128,192},{160,224},{192,128},{224,1... | collective-permute-start | bytes 589832 | tf_op jit(solution)/shard_map/ppermute | solution.py:51
  134.0 8.5 %collective-permute-start.9 = (bf16[8,3,16,256]{3,2,0,1:T(8,128)(2,1)S(1)}, bf16[8,3,16,256]{3,2,0,1:T(8,128)(2,1)S(1)}, u32[]{:S(2)}, u32[]{:S(2)}) collective-permute-start(bf16[8,3,16,256]{3,2,0,1:T(8,128)(2,1)S(1)} %copy.77), channel_id=1, source_target_pairs={{0,32},{32,64},{64,96},{96,0},{128,160},{160,192},{192,224},{224,1... | collective-permute-start | bytes 589832 | tf_op jit(solution)/shard_map/ppermute | solution.py:51
  138.1 8.8 %collective-permute-start.11 = (bf16[8,3,16,256]{3,2,0,1:T(8,128)(2,1)S(1)}, bf16[8,3,16,256]{3,2,0,1:T(8,128)(2,1)S(1)}, u32[]{:S(2)}, u32[]{:S(2)}) collective-permute-start(bf16[8,3,16,256]{3,2,0,1:T(8,128)(2,1)S(1)} %copy.77), channel_id=1, source_target_pairs={{0,96},{32,0},{64,32},{96,64},{128,224},{160,128},{192,160},{224,1... | collective-permute-start | bytes 589832 | tf_op jit(solution)/shard_map/ppermute | solution.py:51
  152.1 0.7 copy-start.6
  152.1 1.5 copy-start.4
  152.1 1.2 copy-start.3
  154.3 8.6 %copy-start.7 = (bf16[8,4,1,16,256]{4,3,1,2,0:T(8,128)(2,1)S(1)}, bf16[8,4,1,16,256]{4,3,1,2,0:T(8,128)(2,1)}, u32[]{:S(2)}) copy-start(bf16[8,4,1,16,256]{4,3,1,2,0:T(8,128)(2,1)} %copy-done.6) | copy-start | bytes 786436
  155.1 8.9 %copy-start.5 = (bf16[8,4,1,16,256]{4,3,1,2,0:T(8,128)(2,1)S(1)}, bf16[8,4,1,16,256]{4,3,1,2,0:T(8,128)(2,1)}, u32[]{:S(2)}) copy-start(bf16[8,4,1,16,256]{4,3,1,2,0:T(8,128)(2,1)} %copy-done.4) | copy-start | bytes 786436
  155.2 23.1 %all-to-all-start.5 = ((bf16[32,8,448]{2,1,0:T(8,128)(2,1)}), bf16[32,8,448]{2,1,0:T(8,128)(2,1)S(1)}, u32[]{:S(2)}, u32[]{:S(2)}) async-start(bf16[32,8,448]{2,1,0:T(8,128)(2,1)} %pad_maximum_fusion.10), calls=%async_computation.5 | async-start | bytes 524288 | tf_op jit(solution)/shard_map/all_to_all | solution.py:157
  165.2 13.1 %copy-start.9 = (f32[256,16]{0,1:T(8,128)S(1)}, f32[256,16]{0,1:T(8,128)}, u32[]{:S(2)}) copy-start(f32[256,16]{0,1:T(8,128)} %copy-done.8) | copy-start | bytes 49156

commit v3 on v1

--- a/solution.py
+++ b/solution.py
@@ -30,22 +30,31 @@
     return select, weighted
 
 
-def dp_groups():
-    count = lax.axis_size("dp")
-    inner = 4
-    outer = count // inner
-    inner_groups = [[o * inner + i for i in range(inner)] for o in range(outer)]
-    outer_groups = [[o * inner + i for o in range(outer)] for i in range(inner)]
-    return inner_groups, outer_groups
+INNER = 4
 
 
-def spread(block, groups):
-    size = len(groups[0])
-    sent = jnp.broadcast_to(block[None], (size,) + block.shape)
-    got = lax.all_to_all(
-        sent, "dp", split_axis=0, concat_axis=0, axis_index_groups=groups, tiled=True
+def parity_groups():
+    pairs = lax.axis_size("dp") // INNER // 2
+    return [
+        [(2 * j + p) * INNER + z for j in range(pairs) for z in range(INNER)] for p in range(2)
+    ]
+
+
+def group_swap(blocks):
+    return lax.all_to_all(
+        blocks, "dp", split_axis=0, concat_axis=0, axis_index_groups=parity_groups(), tiled=True
     )
-    return got.reshape((-1,) + block.shape[1:])
+
+
+def neighbour_swap(block, side):
+    count = lax.axis_size("dp")
+    ring = count // INNER
+
+    def other(y):
+        return y ^ 1 if side == 0 else (y + 1 if y % 2 else y - 1) % ring
+
+    pairs = [(d, other(d // INNER) * INNER + d % INNER) for d in range(count)]
+    return lax.ppermute(block, "dp", pairs)
 
 
 def local(tokens, routes, scores, w_gate, w_up, w_down, cotangent):
@@ -53,7 +62,6 @@
     ex_count = lax.axis_size("expert")
     width = tokens.shape[1]
     slots = EXPERTS * CAP
-    share = HID // dp_count
     cols = ex_count * CAP
     gate_w, up_w, down_w = w_gate[0], w_up[0], w_down[0]
 
@@ -68,33 +76,47 @@
     ).reshape(cols, 2 * width)
     x_rows, do_rows = rows[:, :width], rows[:, width:]
 
+    group = dp_count // 2
+    rows_each = HID // dp_count // 2
+    odd = lax.rem(lax.axis_index("dp") // INNER, 2) == 1
+
     def part(w, r):
         return lax.dot_general(
             w, r, (((0,), (1,)), ((), ())), preferred_element_type=F32
-        ).astype(BF16).reshape(dp_count, share, cols)
+        ).reshape(2, 2, group, rows_each, cols)
 
-    parts = jnp.concatenate(
-        [part(gate_w, x_rows), part(up_w, x_rows), part(down_w, do_rows)], axis=1
-    )
-    parts = lax.all_to_all(parts, "dp", split_axis=0, concat_axis=0, tiled=True)
-    own = jnp.sum(parts.astype(F32), axis=0)
-    pre_gate, pre_up, grad_hidden = own[:share], own[share : 2 * share], own[2 * share :]
+    parts = [part(gate_w, x_rows), part(up_w, x_rows), part(down_w, do_rows)]
+
+    def summed(side):
+        mine = jnp.stack([jnp.where(odd, p[1, side], p[0, side]) for p in parts], axis=1)
+        sent = jnp.stack([jnp.where(odd, p[0, side], p[1, side]) for p in parts], axis=1)
+        return (mine + neighbour_swap(sent.astype(BF16), side).astype(F32)).astype(BF16)
+
+    pair_sums = jnp.stack([summed(0), summed(1)], axis=1)
+    own = jnp.sum(group_swap(pair_sums).astype(F32), axis=0)
+    pre_gate, pre_up, grad_hidden = own[:, 0], own[:, 1], own[:, 2]
     sigma = jax.nn.sigmoid(pre_gate)
     active = pre_gate * sigma
-    block = jnp.concatenate(
+    block = jnp.stack(
         [
             active * pre_up,
             grad_hidden * pre_up * sigma * (1.0 + pre_gate * (1.0 - sigma)),
             grad_hidden * active,
         ],
-        axis=0,
+        axis=1,
     ).astype(BF16)
+    near = group_swap(jnp.broadcast_to(block[None], (group,) + block.shape))
+    near = [near[:, 0], near[:, 1]]
+    far = [neighbour_swap(near[0], 0), neighbour_swap(near[1], 1)]
 
-    inner_groups, outer_groups = dp_groups()
-    full = spread(spread(block, inner_groups), outer_groups).reshape(dp_count, 3, share, cols)
-    hidden = full[:, 0].reshape(HID, cols)
-    grad_gate_pre = full[:, 1].reshape(HID, cols)
-    grad_up_pre = full[:, 2].reshape(HID, cols)
+    def whole(index):
+        own_rows = jnp.stack([near[0][:, index], near[1][:, index]])
+        far_rows = jnp.stack([far[0][:, index], far[1][:, index]])
+        return jnp.stack(
+            [jnp.where(odd, far_rows, own_rows), jnp.where(odd, own_rows, far_rows)]
+        ).reshape(HID, cols)
+
+    hidden, grad_gate_pre, grad_up_pre = whole(0), whole(1), whole(2)
 
     def back(act, w):
         return lax.dot_general(act, w, (((0,), (1,)), ((), ())), preferred_element_type=F32)

time: 173 us -> 170 us (0.983)
  blocking collectives: 136 us -> 59.6 us
  waiting for transfers between devices: 11.8 us -> 44.6 us
  starting transfers between devices: 9.27 us -> 41.6 us
  local copies, waits for them, and re-layouts: 2.31 us -> 6.48 us
  other arithmetic: 3.26 us -> 5.44 us
    all_to_all x4 -> x2, blocking collectives: 136 us -> 59.6 us  [group_swap(): lax.all_to_all(blocks, 'dp', split_axis=0, concat_axis=0, axis_index_grou...]
    all_to_all x0 -> x1, starting transfers between devices: none -> 20.5 us  [local(): lax.all_to_all(sent.reshape(ex_count, CAP, 2 * width), 'expert', split_ax...]
    ppermute x0 -> x4, waiting for transfers between devices: none -> 17.4 us  [neighbour_swap(): return lax.ppermute(block, 'dp', pairs)]
    all_to_all x0 -> x1, waiting for transfers between devices: none -> 15.3 us  [local(): lax.all_to_all(sent.reshape(ex_count, CAP, 2 * width), 'expert', split_ax...]
    ppermute x0 -> x4, starting transfers between devices: none -> 14.6 us  [neighbour_swap(): return lax.ppermute(block, 'dp', pairs)]
    dot_general x0 -> x3, local copies, waits for them, and re-layouts: none -> 3.2 us  [part(): lax.dot_general(w, r, (((0,), (1,)), ((), ())), preferred_element_type=F32)]
    all_to_all x1, starting transfers between devices: 9.27 us -> 6.54 us  [local(): lax.all_to_all(outs.reshape(ex_count, CAP, 2 * width), 'expert', split_ax...]
    dot_general x3, matrix products: 0.93 us -> 2.97 us  [part(): lax.dot_general(w, r, (((0,), (1,)), ((), ())), preferred_element_type=F32)]
  transfers between devices with their start and end apart: 1 -> 6, of which waited for: 1 -> 6; matrix products, arithmetic and copies ran while one was open for 2% -> 2% of each run, Pallas kernels for 0% -> 0%
where the time goes in v3:
time: 170 us; the launch traced here: 169 us
  blocking collectives  59.6 us (35%)
  waiting for transfers between devices  44.6 us (26%)
  starting transfers between devices  41.6 us (24%)
  matrix products  10.1 us (6%)
  local copies, waits for them, and re-layouts  6.48 us (4%)
  other arithmetic  5.44 us (3%)
    all_to_all x2, blocking collectives, group_swap(): lax.all_to_all(blocks, 'dp', split_axis=0, concat_axis=0, axis_index_grou...  59.6 us
    all_to_all x1, starting transfers between devices, local(): lax.all_to_all(sent.reshape(ex_count, CAP, 2 * width), 'expert', split_ax...  20.5 us
    ppermute x4, waiting for transfers between devices, neighbour_swap(): return lax.ppermute(block, 'dp', pairs)  17.4 us
    all_to_all x1, waiting for transfers between devices, local(): lax.all_to_all(sent.reshape(ex_count, CAP, 2 * width), 'expert', split_ax...  15.3 us
    ppermute x4, starting transfers between devices, neighbour_swap(): return lax.ppermute(block, 'dp', pairs)  14.6 us
    all_to_all x1, waiting for transfers between devices, local(): lax.all_to_all(outs.reshape(ex_count, CAP, 2 * width), 'expert', split_ax...  11.9 us
    all_to_all x1, starting transfers between devices, local(): lax.all_to_all(outs.reshape(ex_count, CAP, 2 * width), 'expert', split_ax...  6.54 us
    dot_general x3, matrix products, weight_grad(): lax.dot_general(r, act, (((0,), (1,)), ((), ())), preferred_element_type=...  3.49 us
  transfers between devices with their start and end apart: 6, of which 6 were waited for; matrix products, arithmetic and copies ran while one was open for 2% of the time, Pallas kernels for 0%

profile of v3, /device:TPU:1, one launch (start us, length us, event | category | flops | bytes accessed | tf_op | source)
XLA Modules:
  0.0 168.8 jit_solution(11220960899371196228)
XLA Ops:
  0.6 0.0 copy-start
  0.7 0.8 reduce_sum.58
  1.5 0.7 multiply_divide_fusion
  2.1 0.1 copy.58
  2.2 0.8 copy.56
  3.0 0.1 eq.33
  3.1 0.1 fusion.31
  3.2 0.2 reduce_window_sum.11
  3.3 0.2 select_reduce_fusion.3
  3.5 0.1 reduce_sum.57
  3.6 0.2 select_reduce_fusion
  3.8 1.1 fusion.3
  4.8 0.8 copy.59
  5.7 20.5 %all-to-all-start = ((bf16[32,8,448]{2,1,0:T(8,128)(2,1)}), bf16[32,8,448]{2,1,0:T(8,128)(2,1)S(1)}, u32[]{:S(2)}, u32[]{:S(2)}) async-start(bf16[32,8,448]{2,1,0:T(8,128)(2,1)} %bitcast), calls=%async_computation | async-start | bytes 524288 | tf_op jit(solution)/shard_map/all_to_all | solution.py:74
  26.2 15.3 %all-to-all-done = bf16[32,8,448]{2,1,0:T(8,128)(2,1)S(1)} async-done(((bf16[32,8,448]{2,1,0:T(8,128)(2,1)}), bf16[32,8,448]{2,1,0:T(8,128)(2,1)S(1)}, u32[]{:S(2)}, u32[]{:S(2)}) %all-to-all-start) | async-done | bytes 229408 | tf_op jit(solution)/shard_map/all_to_all | solution.py:74
  41.5 0.3 convolution_bitcast_fusion.1
  41.8 0.3 copy.61
  42.2 1.4 convolution_bitcast_fusion
  43.5 1.3 copy.62
  44.9 0.0 copy-done
  44.9 1.3 convolution_bitcast_fusion.2
  46.2 1.6 copy.60
  47.7 1.2 fusion.19
  49.0 0.1 fusion.17
  49.1 6.0 %collective-permute-start.1 = (bf16[16,3,16,256]{3,2,0,1:T(8,128)(2,1)S(1)}, bf16[16,3,16,256]{3,2,0,1:T(8,128)(2,1)S(1)}, u32[]{:S(2)}, u32[]{:S(2)}) collective-permute-start(bf16[16,3,16,256]{3,2,0,1:T(8,128)(2,1)S(1)} %pad_maximum_fusion.5), channel_id=1, source_target_pairs={{0,896},{32,928},{64,960},{96,992},{128,256},{160,288},{192,320},{... | collective-permute-start | bytes 1179656 | tf_op jit(solution)/shard_map/ppermute | solution.py:57
  55.2 1.9 %collective-permute-start = (bf16[16,3,16,256]{3,2,0,1:T(8,128)(2,1)S(1)}, bf16[16,3,16,256]{3,2,0,1:T(8,128)(2,1)S(1)}, u32[]{:S(2)}, u32[]{:S(2)}) collective-permute-start(bf16[16,3,16,256]{3,2,0,1:T(8,128)(2,1)S(1)} %pad_maximum_fusion.4), channel_id=1, source_target_pairs={{0,128},{32,160},{64,192},{96,224},{128,0},{160,32},{192,64},{224,... | collective-permute-start | bytes 1179656 | tf_op jit(solution)/shard_map/ppermute | solution.py:57
  57.2 0.2 select_bitcast_fusion.3
  57.4 0.1 select_bitcast_fusion.5
  57.5 6.8 %collective-permute-done.1 = bf16[16,3,16,256]{3,2,0,1:T(8,128)(2,1)S(1)} collective-permute-done((bf16[16,3,16,256]{3,2,0,1:T(8,128)(2,1)S(1)}, bf16[16,3,16,256]{3,2,0,1:T(8,128)(2,1)S(1)}, u32[]{:S(2)}, u32[]{:S(2)}) %collective-permute-start.1) | collective-permute-done | bytes 393248 | tf_op jit(solution)/shard_map/ppermute | solution.py:57
  64.3 0.1 fusion.15
  64.5 2.7 %collective-permute-done = bf16[16,3,16,256]{3,2,0,1:T(8,128)(2,1)S(1)} collective-permute-done((bf16[16,3,16,256]{3,2,0,1:T(8,128)(2,1)S(1)}, bf16[16,3,16,256]{3,2,0,1:T(8,128)(2,1)S(1)}, u32[]{:S(2)}, u32[]{:S(2)}) %collective-permute-start) | collective-permute-done | bytes 393248 | tf_op jit(solution)/shard_map/ppermute | solution.py:57
  67.1 0.1 fusion.16
  67.3 0.1 pad_maximum_fusion
  67.3 0.1 copy.63
  67.4 28.1 %all_to_all.20 = bf16[16,2,3,16,256]{4,3,2,1,0:T(8,128)(2,1)S(1)} all-to-all(bf16[16,2,3,16,256]{4,3,2,1,0:T(8,128)(2,1)S(1)} %copy.63), channel_id=1, replica_groups={{0,32,64,96,256,288,320,352,512,544,576,608,768,800,832,864},{128,160,1..., dimensions={0} | all-to-all | bytes 1572864 | tf_op jit(solution)/shard_map/all_to_all | solution.py:44
  95.5 0.1 convert_reduce_fusion
  95.7 0.1 broadcast_in_dim.65
  95.7 31.5 %all_to_all.21 = bf16[16,2,3,16,256]{4,3,2,1,0:T(8,128)(2,1)S(1)} all-to-all(bf16[16,2,3,16,256]{4,3,2,1,0:T(8,128)(2,1)S(1)} %broadcast_in_dim.65), channel_id=1, replica_groups={{0,32,64,96,256,288,320,352,512,544,576,608,768,800,832,864},{128,160,1..., dimensions={0} | all-to-all | bytes 1572864 | tf_op jit(solution)/shard_map/all_to_all | solution.py:44
  127.2 0.1 fusion.38
  127.4 4.3 %collective-permute-start.3 = (bf16[16,3,16,256]{3,2,0,1:T(8,128)(2,1)S(1)}, bf16[16,3,16,256]{3,2,0,1:T(8,128)(2,1)S(1)}, u32[]{:S(2)}, u32[]{:S(2)}) collective-permute-start(bf16[16,3,16,256]{3,2,0,1:T(8,128)(2,1)S(1)} %bitcast.128), channel_id=1, source_target_pairs={{0,896},{32,928},{64,960},{96,992},{128,256},{160,288},{192,320},{... | collective-permute-start | bytes 1179656 | tf_op jit(solution)/shard_map/ppermute | solution.py:57
  131.7 2.3 %collective-permute-start.2 = (bf16[16,3,16,256]{3,2,0,1:T(8,128)(2,1)S(1)}, bf16[16,3,16,256]{3,2,0,1:T(8,128)(2,1)S(1)}, u32[]{:S(2)}, u32[]{:S(2)}) collective-permute-start(bf16[16,3,16,256]{3,2,0,1:T(8,128)(2,1)S(1)} %bitcast.126), channel_id=1, source_target_pairs={{0,128},{32,160},{64,192},{96,224},{128,0},{160,32},{192,64},{224,... | collective-permute-start | bytes 1179656 | tf_op jit(solution)/shard_map/ppermute | solution.py:57
  134.1 4.4 %collective-permute-done.3 = bf16[16,3,16,256]{3,2,0,1:T(8,128)(2,1)S(1)} collective-permute-done((bf16[16,3,16,256]{3,2,0,1:T(8,128)(2,1)S(1)}, bf16[16,3,16,256]{3,2,0,1:T(8,128)(2,1)S(1)}, u32[]{:S(2)}, u32[]{:S(2)}) %collective-permute-start.3) | collective-permute-done | bytes 393248 | tf_op jit(solution)/shard_map/ppermute | solution.py:57
  138.5 3.6 %collective-permute-done.2 = bf16[16,3,16,256]{3,2,0,1:T(8,128)(2,1)S(1)} collective-permute-done((bf16[16,3,16,256]{3,2,0,1:T(8,128)(2,1)S(1)}, bf16[16,3,16,256]{3,2,0,1:T(8,128)(2,1)S(1)}, u32[]{:S(2)}, u32[]{:S(2)}) %collective-permute-start.2) | collective-permute-done | bytes 393248 | tf_op jit(solution)/shard_map/ppermute | solution.py:57
  142.1 0.1 broadcast_select_fusion.3
  142.2 0.1 pad_maximum_fusion.2
  142.2 0.3 fusion.12
  142.5 0.1 broadcast_select_fusion.1
  142.6 0.1 pad_maximum_fusion.3
  142.6 0.3 fusion.4
  142.9 0.1 copy.67
  143.0 0.1 broadcast_select_fusion.5
  143.1 0.0 copy-start.3
  143.1 0.1 pad_maximum_fusion.1
  143.2 0.2 copy.66
  143.4 0.7 copy-done.3
  144.1 0.3 convolution_convert_fusion.3
  144.5 0.8 pad_maximum_fusion.12
  145.3 6.5 %all-to-all-start.3 = ((bf16[32,8,448]{2,1,0:T(8,128)(2,1)}), bf16[32,8,448]{2,1,0:T(8,128)(2,1)S(1)}, u32[]{:S(2)}, u32[]{:S(2)}) async-start(bf16[32,8,448]{2,1,0:T(8,128)(2,1)} %pad_maximum_fusion.12), calls=%async_computation.3 | async-start | bytes 524288 | tf_op jit(solution)/shard_map/all_to_all | solution.py:127
  151.8 1.1 fusion.1
  152.9 1.1 fusion
  154.1 1.2 fusion.2
  155.3 11.9 %all-to-all-done.3 = bf16[32,8,448]{2,1,0:T(8,128)(2,1)S(1)} async-done(((bf16[32,8,448]{2,1,0:T(8,128)(2,1)}), bf16[32,8,448]{2,1,0:T(8,128)(2,1)S(1)}, u32[]{:S(2)}, u32[]{:S(2)}) %all-to-all-start.3) | async-done | bytes 229408 | tf_op jit(solution)/shard_map/all_to_all | solution.py:127
  167.2 0.9 convolution_convert_fusion.4
  168.1 0.8 convolution_convert_fusion.5
  (16 shorter events, 0.3 us)
Async XLA Ops:
  0.6 44.2 %copy-start = (bf16[1,224,1024]{2,1,0:T(8,128)(2,1)S(1)}, bf16[1,224,1024]{2,1,0:T(8,128)(2,1)}, u32[]{:S(2)}) copy-start(bf16[1,224,1024]{2,1,0:T(8,128)(2,1)} %param.10) | copy-start | bytes 1376260
  0.6 40.9 %copy-start.2 = (bf16[1,224,1024]{2,1,0:T(8,128)(2,1)S(1)}, bf16[1,224,1024]{2,1,0:T(8,128)(2,1)}, u32[]{:S(2)}) copy-start(bf16[1,224,1024]{2,1,0:T(8,128)(2,1)} %param.11) | copy-start | bytes 1376260
  5.7 35.8 %all-to-all-start = ((bf16[32,8,448]{2,1,0:T(8,128)(2,1)}), bf16[32,8,448]{2,1,0:T(8,128)(2,1)S(1)}, u32[]{:S(2)}, u32[]{:S(2)}) async-start(bf16[32,8,448]{2,1,0:T(8,128)(2,1)} %bitcast), calls=%async_computation | async-start | bytes 524288 | tf_op jit(solution)/shard_map/all_to_all | solution.py:74
  49.1 8.1 %copy-start.1 = (f32[1024,256]{1,0:T(8,128)S(1)}, f32[1024,256]{1,0:T(8,128)}, u32[]{:S(2)}) copy-start(f32[1024,256]{1,0:T(8,128)} %copy.62) | copy-start | bytes 3145732
  49.1 15.2 %collective-permute-start.1 = (bf16[16,3,16,256]{3,2,0,1:T(8,128)(2,1)S(1)}, bf16[16,3,16,256]{3,2,0,1:T(8,128)(2,1)S(1)}, u32[]{:S(2)}, u32[]{:S(2)}) collective-permute-start(bf16[16,3,16,256]{3,2,0,1:T(8,128)(2,1)S(1)} %pad_maximum_fusion.5), channel_id=1, source_target_pairs={{0,896},{32,928},{64,960},{96,992},{128,256},{160,288},{192,320},{... | collective-permute-start | bytes 1179656 | tf_op jit(solution)/shard_map/ppermute | solution.py:57
  55.2 11.9 %collective-permute-start = (bf16[16,3,16,256]{3,2,0,1:T(8,128)(2,1)S(1)}, bf16[16,3,16,256]{3,2,0,1:T(8,128)(2,1)S(1)}, u32[]{:S(2)}, u32[]{:S(2)}) collective-permute-start(bf16[16,3,16,256]{3,2,0,1:T(8,128)(2,1)S(1)} %pad_maximum_fusion.4), channel_id=1, source_target_pairs={{0,128},{32,160},{64,192},{96,224},{128,0},{160,32},{192,64},{224,... | collective-permute-start | bytes 1179656 | tf_op jit(solution)/shard_map/ppermute | solution.py:57
  127.4 11.1 %collective-permute-start.3 = (bf16[16,3,16,256]{3,2,0,1:T(8,128)(2,1)S(1)}, bf16[16,3,16,256]{3,2,0,1:T(8,128)(2,1)S(1)}, u32[]{:S(2)}, u32[]{:S(2)}) collective-permute-start(bf16[16,3,16,256]{3,2,0,1:T(8,128)(2,1)S(1)} %bitcast.128), channel_id=1, source_target_pairs={{0,896},{32,928},{64,960},{96,992},{128,256},{160,288},{192,320},{... | collective-permute-start | bytes 1179656 | tf_op jit(solution)/shard_map/ppermute | solution.py:57
  131.7 10.4 %collective-permute-start.2 = (bf16[16,3,16,256]{3,2,0,1:T(8,128)(2,1)S(1)}, bf16[16,3,16,256]{3,2,0,1:T(8,128)(2,1)S(1)}, u32[]{:S(2)}, u32[]{:S(2)}) collective-permute-start(bf16[16,3,16,256]{3,2,0,1:T(8,128)(2,1)S(1)} %bitcast.126), channel_id=1, source_target_pairs={{0,128},{32,160},{64,192},{96,224},{128,0},{160,32},{192,64},{224,... | collective-permute-start | bytes 1179656 | tf_op jit(solution)/shard_map/ppermute | solution.py:57
  143.1 1.0 copy-start.3
  145.3 21.9 %all-to-all-start.3 = ((bf16[32,8,448]{2,1,0:T(8,128)(2,1)}), bf16[32,8,448]{2,1,0:T(8,128)(2,1)S(1)}, u32[]{:S(2)}, u32[]{:S(2)}) async-start(bf16[32,8,448]{2,1,0:T(8,128)(2,1)} %pad_maximum_fusion.12), calls=%async_computation.3 | async-start | bytes 524288 | tf_op jit(solution)/shard_map/all_to_all | solution.py:127

commit v4 on v3

v4 whole, which is shorter than its diff:
```python
import jax
import jax.numpy as jnp
from jax import lax
from jax.experimental import pallas as pl
from jax.experimental.pallas import tpu as pltpu
from jax.sharding import PartitionSpec as P

HID = 1024
EXPERTS = 32
CAP = 8
BF16 = jnp.bfloat16
F32 = jnp.float32
INNER = 4
LANES = 128

route_scale = 2.5


def pitch_of(width):
    return -(-width // LANES) * LANES


def flip(block):
    return block.astype(F32).T.astype(BF16)


def pick_kernel(routes_ref, scores_ref, tokens_ref, cotangent_ref, sent_ref, mix_ref, pick_ref):
    tok_count, top_count = routes_ref.shape
    slots = sent_ref.shape[0]
    width = tokens_ref.shape[1]
    pitch = sent_ref.shape[1] // 2
    scores = scores_ref[...]
    gates = route_scale * scores / jnp.sum(scores, axis=1, keepdims=True)
    routes = routes_ref[...]
    slot = lax.broadcasted_iota(jnp.int32, (tok_count, slots), 1)
    shift = CAP.bit_length() - 1
    expert, rank = slot >> shift, slot & (CAP - 1)
    hit = jnp.zeros((tok_count, slots), F32)
    gate = jnp.zeros((tok_count, slots), F32)
    for k in range(top_count):
        same = routes[:, k : k + 1] == expert
        hit = hit + jnp.where(same, 1.0, 0.0)
        gate = gate + jnp.where(same, gates[:, k : k + 1], 0.0)
    row = lax.broadcasted_iota(jnp.int32, (tok_count, tok_count), 0)
    col = lax.broadcasted_iota(jnp.int32, (tok_count, tok_count), 1)
    earlier = jnp.where(col < row, 1.0, 0.0).astype(BF16)
    before = jnp.dot(earlier, hit.astype(BF16), preferred_element_type=F32)
    pick = jnp.where(before == rank.astype(F32), hit, 0.0)
    mix = pick * gate
    mix_ref[...] = mix
    pick_ref[...] = pick.astype(BF16)
    picker = pick.T.astype(BF16)
    slot_gate = jnp.sum(mix.T, axis=1, keepdims=True)
    sent_ref[...] = jnp.zeros(sent_ref.shape, BF16)
    rows = jnp.dot(picker, tokens_ref[...], preferred_element_type=F32)
    sent_ref[:, :width] = rows.astype(BF16)
    rows = jnp.dot(picker, cotangent_ref[...], preferred_element_type=F32)
    sent_ref[:, pitch : pitch + width] = (rows * slot_gate).astype(BF16)


def start_of(odd, other, side, span):
    parity = 1 - odd if other else odd
    return pl.multiple_of((parity * 2 + side) * span, span)


def part_kernel(odd_ref, rows_ref, gate_ref, up_ref, down_ref, own_ref, sent_ref):
    odd = odd_ref[0]
    width = gate_ref.shape[0]
    pitch = rows_ref.shape[1] // 2
    _, group, depth, cols = own_ref.shape
    each = depth // 3
    span = group * each
    x = flip(rows_ref[:, :width])
    do = flip(rows_ref[:, pitch : pitch + width])
    for side in range(2):
        for other, to_ref in ((True, sent_ref), (False, own_ref)):
            start = start_of(odd, other, side, span)
            for index, (w_ref, r) in enumerate(((gate_ref, x), (up_ref, x), (down_ref, do))):
                part = lax.dot_general(
                    w_ref[:, pl.ds(start, span)],
                    r,
                    (((0,), (0,)), ((), ())),
                    preferred_element_type=F32,
                )
                to_ref[side, :, index * each : (index + 1) * each, :] = part.reshape(
                    group, each, cols
                ).astype(to_ref.dtype)


def pieces(odd, near_ref, far_refs):
    group, _, depth, cols = near_ref.shape
    each = depth // 3
    span = group * each
    for side in range(2):
        for other in (False, True):
            source = far_refs[side] if other else near_ref.at[:, side]
            blocks = [
                source[:, index * each : (index + 1) * each, :].reshape(span, cols)
                for index in range(3)
            ]
            yield start_of(odd, other, side, span), span, blocks


def out_kernel(odd_ref, near_ref, far0_ref, far1_ref, gate_ref, up_ref, down_ref, outs_ref):
    width = gate_ref.shape[0]
    pitch = outs_ref.shape[1] // 2
    cols = outs_ref.shape[0]
    out = jnp.zeros((width, cols), F32)
    grad = jnp.zeros((width, cols), F32)
    for start, span, blocks in pieces(odd_ref[0], near_ref, (far0_ref, far1_ref)):
        hidden, grad_gate, grad_up = blocks

        def times(w_ref, block):
            return jnp.dot(w_ref[:, pl.ds(start, span)], block, preferred_element_type=F32)

        out = out + times(down_ref, hidden)
        grad = grad + times(gate_ref, grad_gate) + times(up_ref, grad_up)
    outs_ref[...] = jnp.zeros(outs_ref.shape, BF16)
    outs_ref[:, :width] = out.T.astype(BF16)
    outs_ref[:, pitch : pitch + width] = grad.T.astype(BF16)


def grad_kernel(odd_ref, near_ref, far0_ref, far1_ref, rows_ref, gate_ref, up_ref, down_ref):
    width = gate_ref.shape[0]
    pitch = rows_ref.shape[1] // 2
    x = flip(rows_ref[:, :width])
    do = flip(rows_ref[:, pitch : pitch + width])
    for start, span, blocks in pieces(odd_ref[0], near_ref, (far0_ref, far1_ref)):
        hidden, grad_gate, grad_up = blocks
        for to_ref, r, block in ((gate_ref, x, grad_gate), (up_ref, x, grad_up), (down_ref, do, hidden)):
            to_ref[:, pl.ds(start, span)] = lax.dot_general(
                r, block, (((1,), (1,)), ((), ())), preferred_element_type=F32
            ).astype(BF16)


def combine_kernel(home_ref, mix_ref, pick_ref, out_ref, grad_ref):
    width = out_ref.shape[1]
    pitch = home_ref.shape[1] // 2
    out_ref[...] = jnp.dot(
        mix_ref[...],
        home_ref[:, :width].astype(F32),
        precision=lax.Precision.HIGHEST,
        preferred_element_type=F32,
    ).astype(BF16)
    grad_ref[...] = jnp.dot(
        pick_ref[...], home_ref[:, pitch : pitch + width], preferred_element_type=F32
    ).astype(BF16)


VMEM = pl.BlockSpec(memory_space=pltpu.VMEM)
SMEM = pl.BlockSpec(memory_space=pltpu.SMEM)


def run(kernel, outs, args, flops):
    outs = [jax.ShapeDtypeStruct(shape, dtype) for shape, dtype in outs]
    moved = sum(a.size * a.dtype.itemsize for a in list(args) + outs)
    return pl.pallas_call(
        kernel,
        out_shape=outs,
        in_specs=[SMEM if a.shape == (1,) else VMEM for a in args],
        out_specs=[VMEM] * len(outs),
        cost_estimate=pl.CostEstimate(flops=flops, bytes_accessed=moved, transcendentals=0),
    )(*args)


def parity_groups():
    pairs = lax.axis_size("dp") // INNER // 2
    return [
        [(2 * j + p) * INNER + z for j in range(pairs) for z in range(INNER)] for p in range(2)
    ]


def group_swap(blocks):
    return lax.all_to_all(
        blocks, "dp", split_axis=0, concat_axis=0, axis_index_groups=parity_groups(), tiled=True
    )


def neighbour_swap(block, side):
    count = lax.axis_size("dp")
    ring = count // INNER

    def other(y):
        return y ^ 1 if side == 0 else (y + 1 if y % 2 else y - 1) % ring

    pairs = [(d, other(d // INNER) * INNER + d % INNER) for d in range(count)]
    return lax.ppermute(block, "dp", pairs)


def expert_swap(rows):
    count = lax.axis_size("expert")
    got = lax.all_to_all(
        rows.reshape(count, CAP, rows.shape[1]),
        "expert",
        split_axis=0,
        concat_axis=0,
        tiled=True,
    )
    return got.reshape(rows.shape)


def local(tokens, routes, scores, w_gate, w_up, w_down, cotangent):
    tok_count, width = tokens.shape
    slots = EXPERTS * CAP
    pitch = pitch_of(width)
    group = lax.axis_size("dp") // 2
    each = HID // lax.axis_size("dp") // 2
    depth = 3 * each
    weights = (w_gate[0], w_up[0], w_down[0])
    odd = lax.rem(lax.axis_index("dp") // INNER, 2).astype(jnp.int32).reshape(1)
    work = 6 * slots * HID * width

    sent, mix, pick = run(
        pick_kernel,
        [((slots, 2 * pitch), BF16), ((tok_count, slots), F32), ((tok_count, slots), BF16)],
        (routes, scores, tokens, cotangent),
        4 * slots * tok_count * width,
    )
    rows = expert_swap(sent)
    cols = rows.shape[0]
    shape = (2, group, depth, cols)
    own, sent = run(part_kernel, [(shape, F32), (shape, BF16)], (odd, rows) + weights, work)
    pair_sums = jnp.stack(
        [(own[s] + neighbour_swap(sent[s], s).astype(F32)).astype(BF16) for s in range(2)], axis=1
    )
    own = jnp.sum(group_swap(pair_sums).astype(F32), axis=0)
    pre_gate, pre_up, grad_hidden = own[:, :each], own[:, each : 2 * each], own[:, 2 * each :]
    sigma = jax.nn.sigmoid(pre_gate)
    active = pre_gate * sigma
    block = jnp.concatenate(
        [
            active * pre_up,
            grad_hidden * pre_up * sigma * (1.0 + pre_gate * (1.0 - sigma)),
            grad_hidden * active,
        ],
        axis=1,
    ).astype(BF16)
    near = group_swap(jnp.broadcast_to(block[None], (group,) + block.shape))
    full = (odd, near, neighbour_swap(near[:, 0], 0), neighbour_swap(near[:, 1], 1))
    (outs,) = run(out_kernel, [((cols, 2 * pitch), BF16)], full + weights, work)
    home = expert_swap(outs)
    grads = run(grad_kernel, [((width, HID), BF16)] * 3, full + (rows,), work)
    layer_out, grad_tokens = run(
        combine_kernel,
        [((tok_count, width), BF16)] * 2,
        (home, mix, pick),
        4 * slots * tok_count * width,
    )
    return (layer_out, grad_tokens) + tuple(g[None] for g in grads)


def solution(mesh):
    rows = P("expert", "dp")
    table = P("expert", None)
    weight = P("expert", "dp", None)
    return jax.shard_map(
        local,
        mesh=mesh,
        in_specs=(rows, table, table, weight, weight, weight, rows),
        out_specs=(rows, rows, weight, weight, weight),
        check_vma=False,
    )
```

time: 170 us -> 171 us (level)
  Pallas kernels: 0 us -> 13.7 us
  matrix products: 10.1 us -> 0 us
  other arithmetic: 5.44 us -> 0.48 us
  blocking collectives: 59.6 us -> 62.9 us
  starting transfers between devices: 41.6 us -> 39.3 us
  waiting for transfers between devices: 44.6 us -> 46.5 us
    pallas_call x0 -> x5, Pallas kernels: none -> 13.7 us  [run(): pl.pallas_call(kernel, out_shape=outs, in_specs=[SMEM if a.shape == (1,)...]
    dot_general x12 -> x0, matrix products: 10.1 us -> none  [the longest x3 3.49 us: weight_grad(): lax.dot_general(r, act, (((0,), (1,)), ((), ())), preferred_element_type=...]
    dot_general x4 -> x0, local copies, waits for them, and re-layouts: 3.4 us -> none  [the longest x3 3.2 us: part(): lax.dot_general(w, r, (((0,), (1,)), ((), ())), preferred_element_type=F32)]
    all_to_all x2, blocking collectives: 59.6 us -> 62.9 us  [group_swap(): lax.all_to_all(blocks, 'dp', split_axis=0, concat_axis=0, axis_index_grou...]
    unnamed x11 -> x14, local copies, waits for them, and re-layouts: 1.58 us -> 4.85 us
    select_n x7 -> x0, other arithmetic: 1.8 us -> none  [the longest x2 1.34 us: summed(): jnp.where(odd, p[0, side], p[1, side])]
  transfers between devices with their start and end apart: 6 -> 6, of which waited for: 6 -> 6; matrix products, arithmetic and copies ran while one was open for 2% -> 0% of each run, Pallas kernels for 0% -> 2%
where the time goes in v4:
time: 171 us; the launch traced here: 170 us
  blocking collectives  62.9 us (37%)
  waiting for transfers between devices  46.5 us (27%)
  starting transfers between devices  39.3 us (23%)
  Pallas kernels  13.7 us (8%)
  local copies, waits for them, and re-layouts  6.33 us (4%)
    all_to_all x2, blocking collectives, group_swap(): lax.all_to_all(blocks, 'dp', split_axis=0, concat_axis=0, axis_index_grou...  62.9 us
    all_to_all x2, waiting for transfers between devices, expert_swap(): lax.all_to_all(rows.reshape(count, CAP, rows.shape[1]), 'expert', split_a...  27.6 us
    all_to_all x2, starting transfers between devices, expert_swap(): lax.all_to_all(rows.reshape(count, CAP, rows.shape[1]), 'expert', split_a...  26.1 us
    ppermute x4, waiting for transfers between devices, neighbour_swap(): return lax.ppermute(block, 'dp', pairs)  18.9 us
    pallas_call x5, Pallas kernels, run(): pl.pallas_call(kernel, out_shape=outs, in_specs=[SMEM if a.shape == (1,)...  13.7 us
    ppermute x4, starting transfers between devices, neighbour_swap(): return lax.ppermute(block, 'dp', pairs)  13.2 us
    unnamed x14, local copies, waits for them, and re-layouts  4.85 us
  transfers between devices with their start and end apart: 6, of which 6 were waited for; matrix products, arithmetic and copies ran while one was open for 0% of the time, Pallas kernels for 2%

profile of v4, /device:TPU:1, one launch (start us, length us, event | category | flops | bytes accessed | tf_op | source)
XLA Modules:
  0.0 169.9 jit_solution(10573515295141334790)
XLA Ops:
  0.6 1.4 copy.16.routes_ref
  2.0 1.4 copy.17.scores_ref
  3.3 2.1 %shard_map.110 = (bf16[256,512]{1,0:T(8,128)(2,1)}, f32[16,256]{1,0:T(8,128)}, bf16[16,256]{1,0:T(8,128)(2,1)}) custom-call(s32[16,8]{1,0:T(8,128)} %copy.16.routes_ref, f32[16,8]{1,0:T(8,128)} %copy.17.scores_ref, bf16[16,224]{1,0:T(8,128)(2,1)} %tokens_ref.1, bf16[16,224]{1,0:T(8,128)(2,1)} %cotangent_ref.1), custom_call_target="tpu_custom_call" | custom-call | flops 3670016 | bytes 302080 | tf_op jit(solution)/shard_map/pallas_call | solution.py:157
  5.4 20.5 %all-to-all-start = ((bf16[32,8,512]{2,1,0:T(8,128)(2,1)}), bf16[32,8,512]{2,1,0:T(8,128)(2,1)S(1)}, u32[]{:S(2)}, u32[]{:S(2)}) async-start(bf16[32,8,512]{2,1,0:T(8,128)(2,1)} %bitcast.49), calls=%async_computation | async-start | bytes 524288 | tf_op jit(solution)/shard_map/all_to_all | solution.py:192
  26.0 15.3 %all-to-all-done = bf16[32,8,512]{2,1,0:T(8,128)(2,1)S(1)} async-done(((bf16[32,8,512]{2,1,0:T(8,128)(2,1)}), bf16[32,8,512]{2,1,0:T(8,128)(2,1)S(1)}, u32[]{:S(2)}, u32[]{:S(2)}) %all-to-all-start) | async-done | bytes 262176 | tf_op jit(solution)/shard_map/all_to_all | solution.py:192
  41.3 0.0 copy-start.1
  41.3 0.7 copy-done.1
  42.0 3.5 %shard_map.111 = (f32[2,16,48,256]{3,2,1,0:T(8,128)}, bf16[2,16,48,256]{3,2,1,0:T(8,128)(2,1)}) custom-call(s32[1]{0:T(128)} %bitcast.odd_ref, bf16[256,512]{1,0:T(8,128)(2,1)} %bitcast.39, bf16[224,1024]{1,0:T(8,128)(2,1)} %bitcast.41, bf16[224,1024]{1,0:T(8,128)(2,1)} %bitcast.43, bf16[224,1024]{1,0:T(8,128)(2,1)} %bitcast.45), custom_call_target="tpu_custom_call" | custom-call | flops 352321536 | bytes 3997700 | tf_op jit(solution)/shard_map/pallas_call | solution.py:157
  45.5 0.0 copy-start.2
  45.5 1.3 slice_bitcast_fusion.3
  46.8 3.3 %collective-permute-start = (bf16[16,48,256]{2,1,0:T(8,128)(2,1)S(1)}, bf16[16,48,256]{2,1,0:T(8,128)(2,1)S(1)}, u32[]{:S(2)}, u32[]{:S(2)}) collective-permute-start(bf16[16,48,256]{2,1,0:T(8,128)(2,1)S(1)} %get-tuple-element.29), channel_id=1, source_target_pairs={{0,128},{32,160},{64,192},{96,224},{128,0},{160,32},{192,64},{224,... | collective-permute-start | bytes 1179656 | tf_op jit(solution)/shard_map/ppermute | solution.py:187
  50.1 5.4 %collective-permute-start.1 = (bf16[16,48,256]{2,1,0:T(8,128)(2,1)S(1)}, bf16[16,48,256]{2,1,0:T(8,128)(2,1)S(1)}, u32[]{:S(2)}, u32[]{:S(2)}) collective-permute-start(bf16[16,48,256]{2,1,0:T(8,128)(2,1)S(1)} %get-tuple-element.30), channel_id=1, source_target_pairs={{0,896},{32,928},{64,960},{96,992},{128,256},{160,288},{192,320},{... | collective-permute-start | bytes 1179656 | tf_op jit(solution)/shard_map/ppermute | solution.py:187
  55.5 3.4 %collective-permute-done = bf16[16,48,256]{2,1,0:T(8,128)(2,1)S(1)} collective-permute-done((bf16[16,48,256]{2,1,0:T(8,128)(2,1)S(1)}, bf16[16,48,256]{2,1,0:T(8,128)(2,1)S(1)}, u32[]{:S(2)}, u32[]{:S(2)}) %collective-permute-start) | collective-permute-done | bytes 393248 | tf_op jit(solution)/shard_map/ppermute | solution.py:187
  59.0 5.4 %collective-permute-done.1 = bf16[16,48,256]{2,1,0:T(8,128)(2,1)S(1)} collective-permute-done((bf16[16,48,256]{2,1,0:T(8,128)(2,1)S(1)}, bf16[16,48,256]{2,1,0:T(8,128)(2,1)S(1)}, u32[]{:S(2)}, u32[]{:S(2)}) %collective-permute-start.1) | collective-permute-done | bytes 393248 | tf_op jit(solution)/shard_map/ppermute | solution.py:187
  64.4 0.0 copy-done.2
  64.4 0.3 fusion.2
  64.6 0.1 pad_maximum_fusion
  64.7 0.1 copy.18
  64.8 34.4 %all_to_all.20 = bf16[16,2,48,256]{3,2,1,0:T(8,128)(2,1)S(1)} all-to-all(bf16[16,2,48,256]{3,2,1,0:T(8,128)(2,1)S(1)} %copy.18), channel_id=1, replica_groups={{0,32,64,96,256,288,320,352,512,544,576,608,768,800,832,864},{128,160,1..., dimensions={0} | all-to-all | bytes 1572864 | tf_op jit(solution)/shard_map/all_to_all | solution.py:174
  99.2 0.1 convert_reduce_fusion
  99.3 0.1 broadcast_in_dim.15
  99.4 28.5 %all_to_all.21.near_ref = bf16[16,2,48,256]{3,2,1,0:T(8,128)(2,1)S(1)} all-to-all(bf16[16,2,48,256]{3,2,1,0:T(8,128)(2,1)S(1)} %broadcast_in_dim.15), channel_id=1, replica_groups={{0,32,64,96,256,288,320,352,512,544,576,608,768,800,832,864},{128,160,1..., dimensions={0} | all-to-all | bytes 1572864 | tf_op jit(solution)/shard_map/all_to_all | solution.py:174
  127.9 0.0 copy-start
  127.9 0.1 slice_bitcast_fusion
  128.0 1.9 %collective-permute-start.2 = (bf16[16,48,256]{2,1,0:T(8,128)(2,1)S(1)}, bf16[16,48,256]{2,1,0:T(8,128)(2,1)S(1)}, u32[]{:S(2)}, u32[]{:S(2)}) collective-permute-start(bf16[16,48,256]{2,1,0:T(8,128)(2,1)S(1)} %get-tuple-element.28), channel_id=1, source_target_pairs={{0,128},{32,160},{64,192},{96,224},{128,0},{160,32},{192,64},{224,... | collective-permute-start | bytes 1179656 | tf_op jit(solution)/shard_map/ppermute | solution.py:187
  129.9 2.5 %collective-permute-start.3 = (bf16[16,48,256]{2,1,0:T(8,128)(2,1)S(1)}, bf16[16,48,256]{2,1,0:T(8,128)(2,1)S(1)}, u32[]{:S(2)}, u32[]{:S(2)}) collective-permute-start(bf16[16,48,256]{2,1,0:T(8,128)(2,1)S(1)} %get-tuple-element.27), channel_id=1, source_target_pairs={{0,896},{32,928},{64,960},{96,992},{128,256},{160,288},{192,320},{... | collective-permute-start | bytes 1179656 | tf_op jit(solution)/shard_map/ppermute | solution.py:187
  132.5 6.9 %collective-permute-done.2.far0_ref = bf16[16,48,256]{2,1,0:T(8,128)(2,1)S(1)} collective-permute-done((bf16[16,48,256]{2,1,0:T(8,128)(2,1)S(1)}, bf16[16,48,256]{2,1,0:T(8,128)(2,1)S(1)}, u32[]{:S(2)}, u32[]{:S(2)}) %collective-permute-start.2) | collective-permute-done | bytes 393248 | tf_op jit(solution)/shard_map/ppermute | solution.py:187
  139.4 0.0 copy-start.3
  139.4 3.1 %collective-permute-done.3.far1_ref = bf16[16,48,256]{2,1,0:T(8,128)(2,1)S(1)} collective-permute-done((bf16[16,48,256]{2,1,0:T(8,128)(2,1)S(1)}, bf16[16,48,256]{2,1,0:T(8,128)(2,1)S(1)}, u32[]{:S(2)}, u32[]{:S(2)}) %collective-permute-start.3) | collective-permute-done | bytes 393248 | tf_op jit(solution)/shard_map/ppermute | solution.py:187
  142.5 0.0 copy-done
  142.5 0.0 copy-done.3
  142.5 0.0 copy-start.4
  142.5 0.7 copy-done.4
  143.3 3.1 %shard_map.112 = bf16[256,512]{1,0:T(8,128)(2,1)} custom-call(s32[1]{0:T(128)} %bitcast.odd_ref, bf16[16,2,48,256]{3,2,1,0:T(8,128)(2,1)} %copy-done, bf16[16,48,256]{2,1,0:T(8,128)(2,1)} %copy-done.3, bf16[16,48,256]{2,1,0:T(8,128)(2,1)} %copy-done.4, bf16[224,1024]{1,0:T(8,128)(2,1)} %bitcast.42, bf16[224,1024]{1,0:T(8,128)(2,1)} %bitcast.44, ...), custom_call_target="tpu_custom_call" | custom-call | flops 352321536 | bytes 3211268 | tf_op jit(solution)/shard_map/pallas_call | solution.py:157
  146.4 5.6 %all-to-all-start.3 = ((bf16[32,8,512]{2,1,0:T(8,128)(2,1)}), bf16[32,8,512]{2,1,0:T(8,128)(2,1)S(1)}, u32[]{:S(2)}, u32[]{:S(2)}) async-start(bf16[32,8,512]{2,1,0:T(8,128)(2,1)} %bitcast.48), calls=%async_computation.3 | async-start | bytes 524288 | tf_op jit(solution)/shard_map/all_to_all | solution.py:192
  152.0 3.1 %shard_map.114 = (bf16[224,1024]{1,0:T(8,128)(2,1)}, bf16[224,1024]{1,0:T(8,128)(2,1)}, bf16[224,1024]{1,0:T(8,128)(2,1)}) custom-call(s32[1]{0:T(128)} %bitcast.odd_ref, bf16[16,2,48,256]{3,2,1,0:T(8,128)(2,1)} %copy-done, bf16[16,48,256]{2,1,0:T(8,128)(2,1)} %copy-done.3, bf16[16,48,256]{2,1,0:T(8,128)(2,1)} %copy-done.4, bf16[256,512]{1,0:T(8,128)(2,1)} %bitcast.40), custom_call_target="tpu_custom_call" | custom-call | flops 352321536 | bytes 3211268 | tf_op jit(solution)/shard_map/pallas_call | solution.py:157
  155.1 12.3 %all-to-all-done.3 = bf16[32,8,512]{2,1,0:T(8,128)(2,1)S(1)} async-done(((bf16[32,8,512]{2,1,0:T(8,128)(2,1)}), bf16[32,8,512]{2,1,0:T(8,128)(2,1)S(1)}, u32[]{:S(2)}, u32[]{:S(2)}) %all-to-all-start.3) | async-done | bytes 262176 | tf_op jit(solution)/shard_map/all_to_all | solution.py:192
  167.4 0.0 copy-start.5
  167.4 0.7 copy-done.5
  168.1 1.8 %shard_map.113 = (bf16[16,224]{1,0:T(8,128)(2,1)}, bf16[16,224]{1,0:T(8,128)(2,1)}) custom-call(bf16[256,512]{1,0:T(8,128)(2,1)} %bitcast.47, f32[16,256]{1,0:T(8,128)} %get-tuple-element.18.mix_ref, bf16[16,256]{1,0:T(8,128)(2,1)} %get-tuple-element.19.pick_ref), custom_call_target="tpu_custom_call" | custom-call | flops 3670016 | bytes 301056 | tf_op jit(solution)/shard_map/pallas_call | solution.py:157
  (2 shorter events, 0.0 us)
Async XLA Ops:
  5.4 35.9 %all-to-all-start = ((bf16[32,8,512]{2,1,0:T(8,128)(2,1)}), bf16[32,8,512]{2,1,0:T(8,128)(2,1)S(1)}, u32[]{:S(2)}, u32[]{:S(2)}) async-start(bf16[32,8,512]{2,1,0:T(8,128)(2,1)} %bitcast.49), calls=%async_computation | async-start | bytes 524288 | tf_op jit(solution)/shard_map/all_to_all | solution.py:192
  41.3 0.7 copy-start.1
  45.5 18.9 %copy-start.2 = (f32[2,16,48,256]{3,2,1,0:T(8,128)S(1)}, f32[2,16,48,256]{3,2,1,0:T(8,128)}, u32[]{:S(2)}) copy-start(f32[2,16,48,256]{3,2,1,0:T(8,128)} %get-tuple-element.16) | copy-start | bytes 4718596
  46.8 12.2 %collective-permute-start = (bf16[16,48,256]{2,1,0:T(8,128)(2,1)S(1)}, bf16[16,48,256]{2,1,0:T(8,128)(2,1)S(1)}, u32[]{:S(2)}, u32[]{:S(2)}) collective-permute-start(bf16[16,48,256]{2,1,0:T(8,128)(2,1)S(1)} %get-tuple-element.29), channel_id=1, source_target_pairs={{0,128},{32,160},{64,192},{96,224},{128,0},{160,32},{192,64},{224,... | collective-permute-start | bytes 1179656 | tf_op jit(solution)/shard_map/ppermute | solution.py:187
  50.1 14.3 %collective-permute-start.1 = (bf16[16,48,256]{2,1,0:T(8,128)(2,1)S(1)}, bf16[16,48,256]{2,1,0:T(8,128)(2,1)S(1)}, u32[]{:S(2)}, u32[]{:S(2)}) collective-permute-start(bf16[16,48,256]{2,1,0:T(8,128)(2,1)S(1)} %get-tuple-element.30), channel_id=1, source_target_pairs={{0,896},{32,928},{64,960},{96,992},{128,256},{160,288},{192,320},{... | collective-permute-start | bytes 1179656 | tf_op jit(solution)/shard_map/ppermute | solution.py:187
  127.9 14.6 %copy-start = (bf16[16,2,48,256]{3,2,1,0:T(8,128)(2,1)}, bf16[16,2,48,256]{3,2,1,0:T(8,128)(2,1)S(1)}, u32[]{:S(2)}) copy-start(bf16[16,2,48,256]{3,2,1,0:T(8,128)(2,1)S(1)} %all_to_all.21.near_ref) | copy-start | bytes 2359300
  128.0 11.4 %collective-permute-start.2 = (bf16[16,48,256]{2,1,0:T(8,128)(2,1)S(1)}, bf16[16,48,256]{2,1,0:T(8,128)(2,1)S(1)}, u32[]{:S(2)}, u32[]{:S(2)}) collective-permute-start(bf16[16,48,256]{2,1,0:T(8,128)(2,1)S(1)} %get-tuple-element.28), channel_id=1, source_target_pairs={{0,128},{32,160},{64,192},{96,224},{128,0},{160,32},{192,64},{224,... | collective-permute-start | bytes 1179656 | tf_op jit(solution)/shard_map/ppermute | solution.py:187
  129.9 12.6 %collective-permute-start.3 = (bf16[16,48,256]{2,1,0:T(8,128)(2,1)S(1)}, bf16[16,48,256]{2,1,0:T(8,128)(2,1)S(1)}, u32[]{:S(2)}, u32[]{:S(2)}) collective-permute-start(bf16[16,48,256]{2,1,0:T(8,128)(2,1)S(1)} %get-tuple-element.27), channel_id=1, source_target_pairs={{0,896},{32,928},{64,960},{96,992},{128,256},{160,288},{192,320},{... | collective-permute-start | bytes 1179656 | tf_op jit(solution)/shard_map/ppermute | solution.py:187
  139.4 3.1 %copy-start.3 = (bf16[16,48,256]{2,1,0:T(8,128)(2,1)}, bf16[16,48,256]{2,1,0:T(8,128)(2,1)S(1)}, u32[]{:S(2)}) copy-start(bf16[16,48,256]{2,1,0:T(8,128)(2,1)S(1)} %collective-permute-done.2.far0_ref) | copy-start | bytes 1179652
  142.5 0.7 copy-start.4
  146.4 20.9 %all-to-all-start.3 = ((bf16[32,8,512]{2,1,0:T(8,128)(2,1)}), bf16[32,8,512]{2,1,0:T(8,128)(2,1)S(1)}, u32[]{:S(2)}, u32[]{:S(2)}) async-start(bf16[32,8,512]{2,1,0:T(8,128)(2,1)} %bitcast.48), calls=%async_computation.3 | async-start | bytes 524288 | tf_op jit(solution)/shard_map/all_to_all | solution.py:192
  167.4 0.7 copy-start.5

commit v5 on v4

v5 whole, which is shorter than its diff:
```python
import jax
import jax.numpy as jnp
from jax import lax
from jax.experimental import pallas as pl
from jax.experimental.pallas import tpu as pltpu
from jax.sharding import PartitionSpec as P

HID = 1024
EXPERTS = 32
CAP = 8
BF16 = jnp.bfloat16
F32 = jnp.float32
INNER = 4
LANES = 128

route_scale = 2.5


def pitch_of(width):
    return -(-width // LANES) * LANES


def flip(block):
    return block.astype(F32).T.astype(BF16)


def pick_kernel(routes_ref, scores_ref, tokens_ref, cotangent_ref, sent_ref, mix_ref):
    top_count, tok_count = routes_ref.shape
    slots = sent_ref.shape[0]
    width = tokens_ref.shape[1]
    pitch = sent_ref.shape[1] // 2
    scores = scores_ref[...].T
    gates = route_scale * scores / jnp.sum(scores, axis=1, keepdims=True)
    routes = routes_ref[...].astype(F32).T.astype(jnp.int32)
    slot = lax.broadcasted_iota(jnp.int32, (tok_count, slots), 1)
    shift = CAP.bit_length() - 1
    expert, rank = slot >> shift, slot & (CAP - 1)
    hit = jnp.zeros((tok_count, slots), F32)
    gate = jnp.zeros((tok_count, slots), F32)
    for k in range(top_count):
        same = routes[:, k : k + 1] == expert
        hit = hit + jnp.where(same, 1.0, 0.0)
        gate = gate + jnp.where(same, gates[:, k : k + 1], 0.0)
    row = lax.broadcasted_iota(jnp.int32, (tok_count, tok_count), 0)
    col = lax.broadcasted_iota(jnp.int32, (tok_count, tok_count), 1)
    earlier = jnp.where(col < row, 1.0, 0.0).astype(BF16)
    before = jnp.dot(earlier, hit.astype(BF16), preferred_element_type=F32)
    pick = jnp.where(before == rank.astype(F32), hit, 0.0)
    mix = pick * gate
    high = mix.astype(BF16)
    rest = mix - high.astype(F32)
    middle = rest.astype(BF16)
    low = (rest - middle.astype(F32)).astype(BF16)
    for index, term in enumerate((pick.astype(BF16), high, middle, low)):
        mix_ref[index * tok_count : (index + 1) * tok_count, :] = term
    picker = pick.T.astype(BF16)
    slot_gate = jnp.sum(mix.T, axis=1, keepdims=True)
    sent_ref[...] = jnp.zeros(sent_ref.shape, BF16)
    rows = jnp.dot(picker, tokens_ref[...], preferred_element_type=F32)
    sent_ref[:, :width] = rows.astype(BF16)
    rows = jnp.dot(picker, cotangent_ref[...], preferred_element_type=F32)
    sent_ref[:, pitch : pitch + width] = (rows * slot_gate).astype(BF16)


def start_of(odd, other, side, span):
    parity = 1 - odd if other else odd
    return pl.multiple_of((parity * 2 + side) * span, span)


def part_kernel(other, sides):
    def kernel(odd_ref, rows_ref, gate_ref, up_ref, down_ref, *to_refs):
        width = gate_ref.shape[0]
        pitch = rows_ref.shape[1] // 2
        group, depth, cols = to_refs[0].shape
        each = depth // 3
        span = group * each
        x = flip(rows_ref[:, :width])
        do = flip(rows_ref[:, pitch : pitch + width])
        for side, to_ref in zip(sides, to_refs):
            start = start_of(odd_ref[0], other, side, span)
            for index, (w_ref, r) in enumerate(((gate_ref, x), (up_ref, x), (down_ref, do))):
                part = lax.dot_general(
                    w_ref[:, pl.ds(start, span)],
                    r,
                    (((0,), (0,)), ((), ())),
                    preferred_element_type=F32,
                )
                to_ref[:, index * each : (index + 1) * each, :] = part.reshape(
                    group, each, cols
                ).astype(to_ref.dtype)

    return kernel


def pieces(odd, near_ref, far_refs, others):
    sample = far_refs[0] if near_ref is None else near_ref
    group, depth, cols = sample.shape[0], sample.shape[-2], sample.shape[-1]
    each = depth // 3
    span = group * each
    for side in range(2):
        for other in others:
            source = far_refs[side] if other else near_ref.at[:, side]
            blocks = [
                source[:, index * each : (index + 1) * each, :].reshape(span, cols)
                for index in range(3)
            ]
            yield start_of(odd, other, side, span), span, blocks


def out_terms(parts, gate_ref, up_ref, down_ref, out, grad):
    for start, span, blocks in parts:
        hidden, grad_gate, grad_up = blocks

        def times(w_ref, block):
            return jnp.dot(w_ref[:, pl.ds(start, span)], block, preferred_element_type=F32)

        out = out + times(down_ref, hidden)
        grad = grad + times(gate_ref, grad_gate) + times(up_ref, grad_up)
    return out, grad


def near_kernel(odd_ref, near_ref, gate_ref, up_ref, down_ref, out_ref, grad_ref):
    zero = jnp.zeros(out_ref.shape, F32)
    parts = pieces(odd_ref[0], near_ref, None, (False,))
    out_ref[...], grad_ref[...] = out_terms(parts, gate_ref, up_ref, down_ref, zero, zero)


def far_kernel(
    odd_ref, far0_ref, far1_ref, gate_ref, up_ref, down_ref, out_ref, grad_ref, outs_ref
):
    width = gate_ref.shape[0]
    pitch = outs_ref.shape[1] // 2
    parts = pieces(odd_ref[0], None, (far0_ref, far1_ref), (True,))
    out, grad = out_terms(parts, gate_ref, up_ref, down_ref, out_ref[...], grad_ref[...])
    outs_ref[...] = jnp.zeros(outs_ref.shape, BF16)
    outs_ref[:, :width] = out.T.astype(BF16)
    outs_ref[:, pitch : pitch + width] = grad.T.astype(BF16)


def grad_kernel(odd_ref, near_ref, far0_ref, far1_ref, rows_ref, gate_ref, up_ref, down_ref):
    width = gate_ref.shape[0]
    pitch = rows_ref.shape[1] // 2
    x = flip(rows_ref[:, :width])
    do = flip(rows_ref[:, pitch : pitch + width])
    for start, span, blocks in pieces(
        odd_ref[0], near_ref, (far0_ref, far1_ref), (False, True)
    ):
        hidden, grad_gate, grad_up = blocks
        for to_ref, r, block in ((gate_ref, x, grad_gate), (up_ref, x, grad_up), (down_ref, do, hidden)):
            to_ref[:, pl.ds(start, span)] = lax.dot_general(
                r, block, (((1,), (1,)), ((), ())), preferred_element_type=F32
            ).astype(BF16)


def combine_kernel(home_ref, mix_ref, out_ref, grad_ref):
    rows, width = out_ref.shape
    pitch = home_ref.shape[1] // 2
    sums = jnp.dot(mix_ref[...], home_ref[...], preferred_element_type=F32)
    gated = sums[rows : 2 * rows] + sums[2 * rows : 3 * rows] + sums[3 * rows :]
    out_ref[...] = gated[:, :width].astype(BF16)
    grad_ref[...] = sums[:rows, pitch : pitch + width].astype(BF16)


VMEM = pl.BlockSpec(memory_space=pltpu.VMEM)
SMEM = pl.BlockSpec(memory_space=pltpu.SMEM)


def run(kernel, outs, args, flops, grant=16):
    outs = [jax.ShapeDtypeStruct(shape, dtype) for shape, dtype in outs]
    moved = sum(a.size * a.dtype.itemsize for a in list(args) + outs)
    return pl.pallas_call(
        kernel,
        out_shape=outs,
        in_specs=[SMEM if a.shape == (1,) else VMEM for a in args],
        out_specs=[VMEM] * len(outs),
        compiler_params=pltpu.CompilerParams(vmem_limit_bytes=grant * 2**20),
        cost_estimate=pl.CostEstimate(flops=flops, bytes_accessed=moved, transcendentals=0),
    )(*args)


def parity_groups():
    pairs = lax.axis_size("dp") // INNER // 2
    return [
        [(2 * j + p) * INNER + z for j in range(pairs) for z in range(INNER)] for p in range(2)
    ]


def group_swap(blocks):
    return lax.all_to_all(
        blocks, "dp", split_axis=0, concat_axis=0, axis_index_groups=parity_groups(), tiled=True
    )


def neighbour_swap(block, side):
    count = lax.axis_size("dp")
    ring = count // INNER

    def other(y):
        return y ^ 1 if side == 0 else (y + 1 if y % 2 else y - 1) % ring

    pairs = [(d, other(d // INNER) * INNER + d % INNER) for d in range(count)]
    return lax.ppermute(block, "dp", pairs)


def expert_swap(rows):
    count = lax.axis_size("expert")
    got = lax.all_to_all(
        rows.reshape(count, CAP, rows.shape[1]),
        "expert",
        split_axis=0,
        concat_axis=0,
        tiled=True,
    )
    return got.reshape(rows.shape)


def local(tokens, routes, scores, w_gate, w_up, w_down, cotangent):
    tok_count, width = tokens.shape
    slots = EXPERTS * CAP
    pitch = pitch_of(width)
    group = lax.axis_size("dp") // 2
    each = HID // lax.axis_size("dp") // 2
    depth = 3 * each
    weights = (w_gate[0], w_up[0], w_down[0])
    odd = lax.rem(lax.axis_index("dp") // INNER, 2).astype(jnp.int32).reshape(1)
    work = 6 * slots * HID * width

    sent, mix = run(
        pick_kernel,
        [((slots, 2 * pitch), BF16), ((4 * tok_count, slots), BF16)],
        (routes.T, scores.T, tokens, cotangent),
        4 * slots * tok_count * width,
    )
    rows = expert_swap(sent)
    cols = rows.shape[0]
    shape = (group, depth, cols)
    inputs = (odd, rows) + weights
    got = []
    for side in range(2):
        (sent,) = run(part_kernel(True, (side,)), [(shape, BF16)], inputs, work // 4)
        got.append(neighbour_swap(sent, side))
    own = run(part_kernel(False, (0, 1)), [(shape, F32)] * 2, inputs, work // 2)
    pair_sums = jnp.stack([(o + g.astype(F32)).astype(BF16) for o, g in zip(own, got)], axis=1)
    own = jnp.sum(group_swap(pair_sums).astype(F32), axis=0)
    pre_gate, pre_up, grad_hidden = own[:, :each], own[:, each : 2 * each], own[:, 2 * each :]
    sigma = jax.nn.sigmoid(pre_gate)
    active = pre_gate * sigma
    block = jnp.concatenate(
        [
            active * pre_up,
            grad_hidden * pre_up * sigma * (1.0 + pre_gate * (1.0 - sigma)),
            grad_hidden * active,
        ],
        axis=1,
    ).astype(BF16)
    near = group_swap(jnp.broadcast_to(block[None], (group,) + block.shape))
    far = tuple(neighbour_swap(near[:, side], side) for side in range(2))
    halves = run(near_kernel, [((width, cols), F32)] * 2, (odd, near) + weights, work // 2)
    (outs,) = run(
        far_kernel, [((cols, 2 * pitch), BF16)], (odd,) + far + weights + tuple(halves), work // 2
    )
    home = expert_swap(outs)
    grads = run(grad_kernel, [((width, HID), BF16)] * 3, (odd, near) + far + (rows,), work)
    layer_out, grad_tokens = run(
        combine_kernel,
        [((tok_count, width), BF16)] * 2,
        (home, mix),
        16 * slots * tok_count * width,
    )
    return (layer_out, grad_tokens) + tuple(g[None] for g in grads)


def solution(mesh):
    rows = P("expert", "dp")
    table = P("expert", None)
    weight = P("expert", "dp", None)
    return jax.shard_map(
        local,
        mesh=mesh,
        in_specs=(rows, table, table, weight, weight, weight, rows),
        out_specs=(rows, rows, weight, weight, weight),
        check_vma=False,
    )
```

time: 171 us -> 162 us (0.947)
  Pallas kernels: 13.7 us -> 6.71 us
  blocking collectives: 62.9 us -> 59.6 us
    pallas_call x5 -> x8, Pallas kernels: 13.7 us -> 6.71 us  [run(): pl.pallas_call(kernel, out_shape=outs, in_specs=[SMEM if a.shape == (1,)...]
    all_to_all x2, blocking collectives: 62.9 us -> 59.6 us  [group_swap(): lax.all_to_all(blocks, 'dp', split_axis=0, concat_axis=0, axis_index_grou...]
where the time goes in v5:
time: 162 us
  blocking collectives  59.6 us (37%)
  waiting for transfers between devices  48.1 us (30%)
  starting transfers between devices  41 us (25%)
  Pallas kernels  6.71 us (4%)
  local copies, waits for them, and re-layouts  5.05 us (3%)
    all_to_all x2, blocking collectives, group_swap(): lax.all_to_all(blocks, 'dp', split_axis=0, concat_axis=0, axis_index_grou...  59.6 us
    all_to_all x2, waiting for transfers between devices, expert_swap(): lax.all_to_all(rows.reshape(count, CAP, rows.shape[1]), 'expert', split_a...  29 us
    all_to_all x2, starting transfers between devices, expert_swap(): lax.all_to_all(rows.reshape(count, CAP, rows.shape[1]), 'expert', split_a...  26.7 us
    ppermute x4, waiting for transfers between devices, neighbour_swap(): return lax.ppermute(block, 'dp', pairs)  19.1 us
    ppermute x4, starting transfers between devices, neighbour_swap(): return lax.ppermute(block, 'dp', pairs)  14.3 us
    pallas_call x8, Pallas kernels, run(): pl.pallas_call(kernel, out_shape=outs, in_specs=[SMEM if a.shape == (1,)...  6.71 us
    unnamed x14, local copies, waits for them, and re-layouts  4.85 us
  transfers between devices with their start and end apart: 6, of which 6 were waited for; matrix products, arithmetic and copies ran while one was open for 0% of the time, Pallas kernels for 2%

profile of v5, /device:TPU:1, one launch (start us, length us, event | category | flops | bytes accessed | tf_op | source)
XLA Modules:
  0.0 161.7 jit_solution(9826355631427770387)
XLA Ops:
  0.6 0.0 copy-start
  0.6 0.0 copy-start.3
  0.7 0.7 copy-done.3
  1.4 0.0 copy-start.4
  1.4 0.7 copy-done.4
  2.1 0.0 copy-start.5
  2.1 0.7 copy-done.5
  2.8 0.0 copy-start.6
  2.8 0.7 copy-done.6
  3.5 1.3 shard_map.110
  4.8 20.5 %all-to-all-start = ((bf16[32,8,512]{2,1,0:T(8,128)(2,1)}), bf16[32,8,512]{2,1,0:T(8,128)(2,1)S(1)}, u32[]{:S(2)}, u32[]{:S(2)}) async-start(bf16[32,8,512]{2,1,0:T(8,128)(2,1)} %bitcast.3), calls=%async_computation | async-start | bytes 524288 | tf_op jit(solution)/shard_map/all_to_all | solution.py:207
  25.3 15.3 %all-to-all-done = bf16[32,8,512]{2,1,0:T(8,128)(2,1)S(1)} async-done(((bf16[32,8,512]{2,1,0:T(8,128)(2,1)}), bf16[32,8,512]{2,1,0:T(8,128)(2,1)S(1)}, u32[]{:S(2)}, u32[]{:S(2)}) %all-to-all-start) | async-done | bytes 262176 | tf_op jit(solution)/shard_map/all_to_all | solution.py:207
  40.6 0.0 copy-done
  40.6 0.0 copy-start.1
  40.6 1.0 copy-done.1
  41.7 0.0 copy-start.2
  41.7 1.0 copy-done.2
  42.7 0.4 shard_map.113
  43.1 5.9 %collective-permute-start.1 = (bf16[16,48,256]{2,1,0:T(8,128)(2,1)S(1)}, bf16[16,48,256]{2,1,0:T(8,128)(2,1)S(1)}, u32[]{:S(2)}, u32[]{:S(2)}) collective-permute-start(bf16[16,48,256]{2,1,0:T(8,128)(2,1)S(1)} %shard_map.113), channel_id=1, source_target_pairs={{0,896},{32,928},{64,960},{96,992},{128,256},{160,288},{192,320},{... | collective-permute-start | bytes 1179656 | tf_op jit(solution)/shard_map/ppermute | solution.py:202
  49.0 0.4 shard_map.112
  49.5 1.9 %collective-permute-start = (bf16[16,48,256]{2,1,0:T(8,128)(2,1)S(1)}, bf16[16,48,256]{2,1,0:T(8,128)(2,1)S(1)}, u32[]{:S(2)}, u32[]{:S(2)}) collective-permute-start(bf16[16,48,256]{2,1,0:T(8,128)(2,1)S(1)} %shard_map.112), channel_id=1, source_target_pairs={{0,128},{32,160},{64,192},{96,224},{128,0},{160,32},{192,64},{224,... | collective-permute-start | bytes 1179656 | tf_op jit(solution)/shard_map/ppermute | solution.py:202
  51.4 0.5 shard_map.111
  51.9 6.2 %collective-permute-done.1 = bf16[16,48,256]{2,1,0:T(8,128)(2,1)S(1)} collective-permute-done((bf16[16,48,256]{2,1,0:T(8,128)(2,1)S(1)}, bf16[16,48,256]{2,1,0:T(8,128)(2,1)S(1)}, u32[]{:S(2)}, u32[]{:S(2)}) %collective-permute-start.1) | collective-permute-done | bytes 393248 | tf_op jit(solution)/shard_map/ppermute | solution.py:202
  58.2 0.1 fusion.1
  58.3 3.0 %collective-permute-done = bf16[16,48,256]{2,1,0:T(8,128)(2,1)S(1)} collective-permute-done((bf16[16,48,256]{2,1,0:T(8,128)(2,1)S(1)}, bf16[16,48,256]{2,1,0:T(8,128)(2,1)S(1)}, u32[]{:S(2)}, u32[]{:S(2)}) %collective-permute-start) | collective-permute-done | bytes 393248 | tf_op jit(solution)/shard_map/ppermute | solution.py:202
  61.3 0.1 fusion
  61.5 0.1 pad_maximum_fusion
  61.5 0.1 copy.14
  61.6 28.4 %all_to_all.20 = bf16[16,2,48,256]{3,2,1,0:T(8,128)(2,1)S(1)} all-to-all(bf16[16,2,48,256]{3,2,1,0:T(8,128)(2,1)S(1)} %copy.14), channel_id=1, replica_groups={{0,32,64,96,256,288,320,352,512,544,576,608,768,800,832,864},{128,160,1..., dimensions={0} | all-to-all | bytes 1572864 | tf_op jit(solution)/shard_map/all_to_all | solution.py:189
  90.0 0.1 convert_reduce_fusion
  90.1 0.1 broadcast_in_dim.15
  90.2 31.2 %all_to_all.21.near_ref = bf16[16,2,48,256]{3,2,1,0:T(8,128)(2,1)S(1)} all-to-all(bf16[16,2,48,256]{3,2,1,0:T(8,128)(2,1)S(1)} %broadcast_in_dim.15), channel_id=1, replica_groups={{0,32,64,96,256,288,320,352,512,544,576,608,768,800,832,864},{128,160,1..., dimensions={0} | all-to-all | bytes 1572864 | tf_op jit(solution)/shard_map/all_to_all | solution.py:189
  121.4 0.1 slice_bitcast_fusion
  121.5 4.5 %collective-permute-start.2 = (bf16[16,48,256]{2,1,0:T(8,128)(2,1)S(1)}, bf16[16,48,256]{2,1,0:T(8,128)(2,1)S(1)}, u32[]{:S(2)}, u32[]{:S(2)}) collective-permute-start(bf16[16,48,256]{2,1,0:T(8,128)(2,1)S(1)} %get-tuple-element.28), channel_id=1, source_target_pairs={{0,128},{32,160},{64,192},{96,224},{128,0},{160,32},{192,64},{224,... | collective-permute-start | bytes 1179656 | tf_op jit(solution)/shard_map/ppermute | solution.py:202
  126.0 1.9 %collective-permute-start.3 = (bf16[16,48,256]{2,1,0:T(8,128)(2,1)S(1)}, bf16[16,48,256]{2,1,0:T(8,128)(2,1)S(1)}, u32[]{:S(2)}, u32[]{:S(2)}) collective-permute-start(bf16[16,48,256]{2,1,0:T(8,128)(2,1)S(1)} %get-tuple-element.27), channel_id=1, source_target_pairs={{0,896},{32,928},{64,960},{96,992},{128,256},{160,288},{192,320},{... | collective-permute-start | bytes 1179656 | tf_op jit(solution)/shard_map/ppermute | solution.py:202
  128.0 0.3 shard_map.114
  128.3 5.4 %collective-permute-done.2.far0_ref = bf16[16,48,256]{2,1,0:T(8,128)(2,1)S(1)} collective-permute-done((bf16[16,48,256]{2,1,0:T(8,128)(2,1)S(1)}, bf16[16,48,256]{2,1,0:T(8,128)(2,1)S(1)}, u32[]{:S(2)}, u32[]{:S(2)}) %collective-permute-start.2) | collective-permute-done | bytes 393248 | tf_op jit(solution)/shard_map/ppermute | solution.py:202
  133.7 4.5 %collective-permute-done.3.far1_ref = bf16[16,48,256]{2,1,0:T(8,128)(2,1)S(1)} collective-permute-done((bf16[16,48,256]{2,1,0:T(8,128)(2,1)S(1)}, bf16[16,48,256]{2,1,0:T(8,128)(2,1)S(1)}, u32[]{:S(2)}, u32[]{:S(2)}) %collective-permute-start.3) | collective-permute-done | bytes 393248 | tf_op jit(solution)/shard_map/ppermute | solution.py:202
  138.2 1.2 shard_map.115
  139.3 6.2 %all-to-all-start.3 = ((bf16[32,8,512]{2,1,0:T(8,128)(2,1)}), bf16[32,8,512]{2,1,0:T(8,128)(2,1)S(1)}, u32[]{:S(2)}, u32[]{:S(2)}) async-start(bf16[32,8,512]{2,1,0:T(8,128)(2,1)} %bitcast.12), calls=%async_computation.3 | async-start | bytes 524288 | tf_op jit(solution)/shard_map/all_to_all | solution.py:207
  145.5 1.7 %shard_map.117 = (bf16[224,1024]{1,0:T(8,128)(2,1)}, bf16[224,1024]{1,0:T(8,128)(2,1)}, bf16[224,1024]{1,0:T(8,128)(2,1)}) custom-call(s32[1]{0:T(128)} %bitcast.odd_ref, bf16[16,2,48,256]{3,2,1,0:T(8,128)(2,1)S(1)} %all_to_all.21.near_ref, bf16[16,48,256]{2,1,0:T(8,128)(2,1)S(1)} %collective-permute-done.2.far0_ref, ...), custom_call_target="tpu_custom_call" | custom-call | flops 352321536 | bytes 3211268 | tf_op jit(solution)/shard_map/pallas_call | solution.py:171
  147.2 13.7 %all-to-all-done.3 = bf16[32,8,512]{2,1,0:T(8,128)(2,1)S(1)} async-done(((bf16[32,8,512]{2,1,0:T(8,128)(2,1)}), bf16[32,8,512]{2,1,0:T(8,128)(2,1)S(1)}, u32[]{:S(2)}, u32[]{:S(2)}) %all-to-all-start.3) | async-done | bytes 262176 | tf_op jit(solution)/shard_map/all_to_all | solution.py:207
  160.9 0.8 shard_map.116
  (2 shorter events, 0.0 us)
Async XLA Ops:
  0.6 40.0 %copy-start = (bf16[1,224,1024]{2,1,0:T(8,128)(2,1)S(1)}, bf16[1,224,1024]{2,1,0:T(8,128)(2,1)}, u32[]{:S(2)}) copy-start(bf16[1,224,1024]{2,1,0:T(8,128)(2,1)} %param.10) | copy-start | bytes 1376260
  0.6 0.8 copy-start.3
  1.4 0.7 copy-start.4
  2.1 0.7 copy-start.5
  2.8 0.7 copy-start.6
  4.8 35.9 %all-to-all-start = ((bf16[32,8,512]{2,1,0:T(8,128)(2,1)}), bf16[32,8,512]{2,1,0:T(8,128)(2,1)S(1)}, u32[]{:S(2)}, u32[]{:S(2)}) async-start(bf16[32,8,512]{2,1,0:T(8,128)(2,1)} %bitcast.3), calls=%async_computation | async-start | bytes 524288 | tf_op jit(solution)/shard_map/all_to_all | solution.py:207
  40.6 1.0 copy-start.1
  41.7 1.0 copy-start.2
  43.1 15.0 %collective-permute-start.1 = (bf16[16,48,256]{2,1,0:T(8,128)(2,1)S(1)}, bf16[16,48,256]{2,1,0:T(8,128)(2,1)S(1)}, u32[]{:S(2)}, u32[]{:S(2)}) collective-permute-start(bf16[16,48,256]{2,1,0:T(8,128)(2,1)S(1)} %shard_map.113), channel_id=1, source_target_pairs={{0,896},{32,928},{64,960},{96,992},{128,256},{160,288},{192,320},{... | collective-permute-start | bytes 1179656 | tf_op jit(solution)/shard_map/ppermute | solution.py:202
  49.5 11.9 %collective-permute-start = (bf16[16,48,256]{2,1,0:T(8,128)(2,1)S(1)}, bf16[16,48,256]{2,1,0:T(8,128)(2,1)S(1)}, u32[]{:S(2)}, u32[]{:S(2)}) collective-permute-start(bf16[16,48,256]{2,1,0:T(8,128)(2,1)S(1)} %shard_map.112), channel_id=1, source_target_pairs={{0,128},{32,160},{64,192},{96,224},{128,0},{160,32},{192,64},{224,... | collective-permute-start | bytes 1179656 | tf_op jit(solution)/shard_map/ppermute | solution.py:202
  121.5 12.2 %collective-permute-start.2 = (bf16[16,48,256]{2,1,0:T(8,128)(2,1)S(1)}, bf16[16,48,256]{2,1,0:T(8,128)(2,1)S(1)}, u32[]{:S(2)}, u32[]{:S(2)}) collective-permute-start(bf16[16,48,256]{2,1,0:T(8,128)(2,1)S(1)} %get-tuple-element.28), channel_id=1, source_target_pairs={{0,128},{32,160},{64,192},{96,224},{128,0},{160,32},{192,64},{224,... | collective-permute-start | bytes 1179656 | tf_op jit(solution)/shard_map/ppermute | solution.py:202
  126.0 12.1 %collective-permute-start.3 = (bf16[16,48,256]{2,1,0:T(8,128)(2,1)S(1)}, bf16[16,48,256]{2,1,0:T(8,128)(2,1)S(1)}, u32[]{:S(2)}, u32[]{:S(2)}) collective-permute-start(bf16[16,48,256]{2,1,0:T(8,128)(2,1)S(1)} %get-tuple-element.27), channel_id=1, source_target_pairs={{0,896},{32,928},{64,960},{96,992},{128,256},{160,288},{192,320},{... | collective-permute-start | bytes 1179656 | tf_op jit(solution)/shard_map/ppermute | solution.py:202
  139.3 21.5 %all-to-all-start.3 = ((bf16[32,8,512]{2,1,0:T(8,128)(2,1)}), bf16[32,8,512]{2,1,0:T(8,128)(2,1)S(1)}, u32[]{:S(2)}, u32[]{:S(2)}) async-start(bf16[32,8,512]{2,1,0:T(8,128)(2,1)} %bitcast.12), calls=%async_computation.3 | async-start | bytes 524288 | tf_op jit(solution)/shard_map/all_to_all | solution.py:207

commit v6 on v5

--- a/solution.py
+++ b/solution.py
@@ -62,92 +62,61 @@
     sent_ref[:, pitch : pitch + width] = (rows * slot_gate).astype(BF16)
 
 
-def start_of(odd, other, side, span):
-    parity = 1 - odd if other else odd
-    return pl.multiple_of((parity * 2 + side) * span, span)
-
-
-def part_kernel(other, sides):
-    def kernel(odd_ref, rows_ref, gate_ref, up_ref, down_ref, *to_refs):
-        width = gate_ref.shape[0]
+def row_kernel(base):
+    def kernel(rows_ref, gate_ref, up_ref, down_ref, *refs):
+        to_ref = refs[-1]
+        width, span = gate_ref.shape
         pitch = rows_ref.shape[1] // 2
-        group, depth, cols = to_refs[0].shape
+        group, depth, cols = to_ref.shape
         each = depth // 3
-        span = group * each
         x = flip(rows_ref[:, :width])
         do = flip(rows_ref[:, pitch : pitch + width])
-        for side, to_ref in zip(sides, to_refs):
-            start = start_of(odd_ref[0], other, side, span)
-            for index, (w_ref, r) in enumerate(((gate_ref, x), (up_ref, x), (down_ref, do))):
-                part = lax.dot_general(
-                    w_ref[:, pl.ds(start, span)],
-                    r,
-                    (((0,), (0,)), ((), ())),
-                    preferred_element_type=F32,
-                )
-                to_ref[:, index * each : (index + 1) * each, :] = part.reshape(
-                    group, each, cols
-                ).astype(to_ref.dtype)
+        for index, (w_ref, r) in enumerate(((gate_ref, x), (up_ref, x), (down_ref, do))):
+            part = lax.dot_general(
+                w_ref[...], r, (((0,), (0,)), ((), ())), preferred_element_type=F32
+            ).reshape(group, each, cols)
+            at = pl.ds(index * each, each)
+            if base:
+                part = part + refs[0][:, at, :]
+            to_ref[:, at, :] = part.astype(to_ref.dtype)
 
     return kernel
 
 
-def pieces(odd, near_ref, far_refs, others):
-    sample = far_refs[0] if near_ref is None else near_ref
-    group, depth, cols = sample.shape[0], sample.shape[-2], sample.shape[-1]
+def array_rows(ref, index):
+    group, depth, cols = ref.shape
     each = depth // 3
-    span = group * each
-    for side in range(2):
-        for other in others:
-            source = far_refs[side] if other else near_ref.at[:, side]
-            blocks = [
-                source[:, index * each : (index + 1) * each, :].reshape(span, cols)
-                for index in range(3)
-            ]
-            yield start_of(odd, other, side, span), span, blocks
-
-
-def out_terms(parts, gate_ref, up_ref, down_ref, out, grad):
-    for start, span, blocks in parts:
-        hidden, grad_gate, grad_up = blocks
-
-        def times(w_ref, block):
-            return jnp.dot(w_ref[:, pl.ds(start, span)], block, preferred_element_type=F32)
-
-        out = out + times(down_ref, hidden)
-        grad = grad + times(gate_ref, grad_gate) + times(up_ref, grad_up)
-    return out, grad
-
-
-def near_kernel(odd_ref, near_ref, gate_ref, up_ref, down_ref, out_ref, grad_ref):
-    zero = jnp.zeros(out_ref.shape, F32)
-    parts = pieces(odd_ref[0], near_ref, None, (False,))
-    out_ref[...], grad_ref[...] = out_terms(parts, gate_ref, up_ref, down_ref, zero, zero)
-
-
-def far_kernel(
-    odd_ref, far0_ref, far1_ref, gate_ref, up_ref, down_ref, out_ref, grad_ref, outs_ref
-):
+    return ref[:, index * each : (index + 1) * each, :].reshape(group * each, cols)
+
+
+def out_kernel(near_ref, gate_ref, up_ref, down_ref, outs_ref):
     width = gate_ref.shape[0]
     pitch = outs_ref.shape[1] // 2
-    parts = pieces(odd_ref[0], None, (far0_ref, far1_ref), (True,))
-    out, grad = out_terms(parts, gate_ref, up_ref, down_ref, out_ref[...], grad_ref[...])
-    outs_ref[...] = jnp.zeros(outs_ref.shape, BF16)
-    outs_ref[:, :width] = out.T.astype(BF16)
-    outs_ref[:, pitch : pitch + width] = grad.T.astype(BF16)
+
+    def times(w_ref, index):
+        return jnp.dot(w_ref[...], array_rows(near_ref, index), preferred_element_type=F32)
+
+    out = times(down_ref, 0)
+    grad = times(gate_ref, 1) + times(up_ref, 2)
+    outs_ref[...] = jnp.zeros(outs_ref.shape, outs_ref.dtype)
+    outs_ref[:, :width] = out.T.astype(outs_ref.dtype)
+    outs_ref[:, pitch : pitch + width] = grad.T.astype(outs_ref.dtype)
 
 
 def grad_kernel(odd_ref, near_ref, far0_ref, far1_ref, rows_ref, gate_ref, up_ref, down_ref):
+    odd = odd_ref[0]
     width = gate_ref.shape[0]
     pitch = rows_ref.shape[1] // 2
+    half = gate_ref.shape[1] // 2
     x = flip(rows_ref[:, :width])
     do = flip(rows_ref[:, pitch : pitch + width])
-    for start, span, blocks in pieces(
-        odd_ref[0], near_ref, (far0_ref, far1_ref), (False, True)
-    ):
-        hidden, grad_gate, grad_up = blocks
-        for to_ref, r, block in ((gate_ref, x, grad_gate), (up_ref, x, grad_up), (down_ref, do, hidden)):
-            to_ref[:, pl.ds(start, span)] = lax.dot_general(
+    places = ((near_ref, odd * half), (far0_ref, (1 - odd) * half))
+    places += ((far1_ref, (1 - odd) * half + half // 2),)
+    for ref, start in places:
+        for to_ref, r, index in ((gate_ref, x, 1), (up_ref, x, 2), (down_ref, do, 0)):
+            block = array_rows(ref, index)
+            span = block.shape[0]
+            to_ref[:, pl.ds(pl.multiple_of(start, half // 2), span)] = lax.dot_general(
                 r, block, (((1,), (1,)), ((), ())), preferred_element_type=F32
             ).astype(BF16)
 
@@ -173,7 +142,7 @@
         out_shape=outs,
         in_specs=[SMEM if a.shape == (1,) else VMEM for a in args],
         out_specs=[VMEM] * len(outs),
-        compiler_params=pltpu.CompilerParams(vmem_limit_bytes=grant * 2**20),
+        compiler_params=pltpu.CompilerParams(vmem_limit_bytes=grant and grant * 2**20),
         cost_estimate=pl.CostEstimate(flops=flops, bytes_accessed=moved, transcendentals=0),
     )(*args)
 
@@ -219,9 +188,8 @@
     slots = EXPERTS * CAP
     pitch = pitch_of(width)
     group = lax.axis_size("dp") // 2
-    each = HID // lax.axis_size("dp") // 2
-    depth = 3 * each
-    weights = (w_gate[0], w_up[0], w_down[0])
+    each = HID // lax.axis_size("dp")
+    half = HID // 2
     odd = lax.rem(lax.axis_index("dp") // INNER, 2).astype(jnp.int32).reshape(1)
     work = 6 * slots * HID * width
 
@@ -230,19 +198,25 @@
         [((slots, 2 * pitch), BF16), ((4 * tok_count, slots), BF16)],
         (routes.T, scores.T, tokens, cotangent),
         4 * slots * tok_count * width,
-    )
+        grant=None,
+    )
+    sent, odd = lax.optimization_barrier((sent, odd))
     rows = expert_swap(sent)
     cols = rows.shape[0]
-    shape = (group, depth, cols)
-    inputs = (odd, rows) + weights
-    got = []
-    for side in range(2):
-        (sent,) = run(part_kernel(True, (side,)), [(shape, BF16)], inputs, work // 4)
-        got.append(neighbour_swap(sent, side))
-    own = run(part_kernel(False, (0, 1)), [(shape, F32)] * 2, inputs, work // 2)
-    pair_sums = jnp.stack([(o + g.astype(F32)).astype(BF16) for o, g in zip(own, got)], axis=1)
+    def columns(start):
+        return tuple(
+            lax.dynamic_slice_in_dim(w[0], start, half, axis=1) for w in (w_gate, w_up, w_down)
+        )
+
+    mine = columns(odd[0] * half)
+    theirs = neighbour_swap(jnp.stack(columns((1 - odd[0]) * half)), 0)
+    theirs = (theirs[0], theirs[1], theirs[2])
+    pair_rows = neighbour_swap(rows, 0)
+    shape = (group, 3 * each, cols)
+    (share,) = run(row_kernel(False), [(shape, F32)], (rows,) + mine, work // 2)
+    (pair_sums,) = run(row_kernel(True), [(shape, BF16)], (pair_rows,) + theirs + (share,), work // 2)
     own = jnp.sum(group_swap(pair_sums).astype(F32), axis=0)
-    pre_gate, pre_up, grad_hidden = own[:, :each], own[:, each : 2 * each], own[:, 2 * each :]
+    pre_gate, pre_up, grad_hidden = own[:each], own[each : 2 * each], own[2 * each :]
     sigma = jax.nn.sigmoid(pre_gate)
     active = pre_gate * sigma
     block = jnp.concatenate(
@@ -251,13 +225,17 @@
             grad_hidden * pre_up * sigma * (1.0 + pre_gate * (1.0 - sigma)),
             grad_hidden * active,
         ],
-        axis=1,
+        axis=0,
     ).astype(BF16)
     near = group_swap(jnp.broadcast_to(block[None], (group,) + block.shape))
-    far = tuple(neighbour_swap(near[:, side], side) for side in range(2))
-    halves = run(near_kernel, [((width, cols), F32)] * 2, (odd, near) + weights, work // 2)
-    (outs,) = run(
-        far_kernel, [((cols, 2 * pitch), BF16)], (odd,) + far + weights + tuple(halves), work // 2
+    outs_shape = (cols, 2 * pitch)
+    (sent,) = run(out_kernel, [(outs_shape, BF16)], (near,) + theirs, work // 2)
+    got = neighbour_swap(sent, 0)
+    (outs,) = run(out_kernel, [(outs_shape, F32)], (near,) + mine, work // 2)
+    outs = (outs + got.astype(F32)).astype(BF16)
+    outs, late = lax.optimization_barrier((outs, near))
+    far = tuple(
+        neighbour_swap(late[side * group // 2 : (side + 1) * group // 2], side) for side in range(2)
     )
     home = expert_swap(outs)
     grads = run(grad_kernel, [((width, HID), BF16)] * 3, (odd, near) + far + (rows,), work)

time: 162 us -> 152 us (0.938)
  blocking collectives: 59.6 us -> 97.7 us
  waiting for transfers between devices: 48.1 us -> 20.6 us
  starting transfers between devices: 41 us -> 22.3 us
  local copies, waits for them, and re-layouts: 5.05 us -> 2.64 us
    all_to_all x0 -> x1, blocking collectives: none -> 35.1 us  [expert_swap(): lax.all_to_all(rows.reshape(count, CAP, rows.shape[1]), 'expert', split_a...]
    all_to_all x2 -> x1, waiting for transfers between devices: 29 us -> 0.01 us  [expert_swap(): lax.all_to_all(rows.reshape(count, CAP, rows.shape[1]), 'expert', split_a...]
    all_to_all x2 -> x1, starting transfers between devices: 26.7 us -> 6.19 us  [expert_swap(): lax.all_to_all(rows.reshape(count, CAP, rows.shape[1]), 'expert', split_a...]
    unnamed x14 -> x4, local copies, waits for them, and re-layouts: 4.85 us -> 0.01 us
    all_to_all x2, blocking collectives: 59.6 us -> 62.6 us  [group_swap(): lax.all_to_all(blocks, 'dp', split_axis=0, concat_axis=0, axis_index_grou...]
    dynamic_slice x0 -> x2, local copies, waits for them, and re-layouts: none -> 2.46 us  [columns(): lax.dynamic_slice_in_dim(w[0], start, half, axis=1)]
    ppermute x4 -> x5, starting transfers between devices: 14.3 us -> 16.1 us  [neighbour_swap(): return lax.ppermute(block, 'dp', pairs)]
    ppermute x4 -> x5, waiting for transfers between devices: 19.1 us -> 20.6 us  [neighbour_swap(): return lax.ppermute(block, 'dp', pairs)]
  transfers between devices with their start and end apart: 6 -> 6, of which waited for: 6 -> 4; matrix products, arithmetic and copies ran while one was open for 0% -> 0% of each run, Pallas kernels for 2% -> 2%
where the time goes in v6:
time: 152 us; the launch traced here: 151 us
  blocking collectives  97.7 us (64%)
  starting transfers between devices  22.3 us (15%)
  waiting for transfers between devices  20.6 us (14%)
  Pallas kernels  6.49 us (4%)
  local copies, waits for them, and re-layouts  2.64 us (2%)
    all_to_all x2, blocking collectives, group_swap(): lax.all_to_all(blocks, 'dp', split_axis=0, concat_axis=0, axis_index_grou...  62.6 us
    all_to_all x1, blocking collectives, expert_swap(): lax.all_to_all(rows.reshape(count, CAP, rows.shape[1]), 'expert', split_a...  35.1 us
    ppermute x5, waiting for transfers between devices, neighbour_swap(): return lax.ppermute(block, 'dp', pairs)  20.6 us
    ppermute x5, starting transfers between devices, neighbour_swap(): return lax.ppermute(block, 'dp', pairs)  16.1 us
    pallas_call x7, Pallas kernels, run(): pl.pallas_call(kernel, out_shape=outs, in_specs=[SMEM if a.shape == (1,)...  6.49 us
    all_to_all x1, starting transfers between devices, expert_swap(): lax.all_to_all(rows.reshape(count, CAP, rows.shape[1]), 'expert', split_a...  6.19 us
  transfers between devices with their start and end apart: 6, of which 4 were waited for; matrix products, arithmetic and copies ran while one was open for 0% of the time, Pallas kernels for 2%

profile of v6, /device:TPU:1, one launch (start us, length us, event | category | flops | bytes accessed | tf_op | source)
XLA Modules:
  0.0 151.5 jit_solution(11501057568672678116)
XLA Ops:
  0.7 2.1 %shard_map.110 = (bf16[256,512]{1,0:T(8,128)(2,1)}, bf16[64,256]{1,0:T(8,128)(2,1)}) custom-call(s32[8,16]{1,0:T(8,128)} %bitcast.29, f32[8,16]{1,0:T(8,128)} %bitcast.30, bf16[16,224]{1,0:T(8,128)(2,1)} %tokens_ref.1, bf16[16,224]{1,0:T(8,128)(2,1)} %cotangent_ref.1), custom_call_target="tpu_custom_call" | custom-call | flops 3670016 | bytes 310272 | tf_op jit(solution)/shard_map/pallas_call | solution.py:140
  2.7 1.1 dynamic-slice_bitcast_fusion.2
  3.8 0.0 copy-start.1
  3.8 1.4 dynamic-slice_bitcast_fusion
  5.2 0.1 pad_maximum_fusion
  5.3 4.1 %collective-permute-start.1 = (bf16[3,224,512]{2,1,0:T(8,128)(2,1)S(1)}, bf16[3,224,512]{2,1,0:T(8,128)(2,1)S(1)}, u32[]{:S(2)}, u32[]{:S(2)}) collective-permute-start(bf16[3,224,512]{2,1,0:T(8,128)(2,1)S(1)} %pad_maximum_fusion), channel_id=1, source_target_pairs={{0,128},{32,160},{64,192},{96,224},{128,0},{160,32},{192,64},{224,... | collective-permute-start | bytes 2064392 | tf_op jit(solution)/shard_map/ppermute | solution.py:171
  9.5 0.0 copy-done.1
  9.5 35.1 %all_to_all.20 = bf16[32,8,512]{2,1,0:T(8,128)(2,1)S(1)} all-to-all(bf16[32,8,512]{2,1,0:T(8,128)(2,1)S(1)} %bitcast.28), channel_id=1, replica_groups=mesh['dp'=32,'expert'=32] {'expert'}, dimensions={0} | all-to-all | bytes 524288 | tf_op jit(solution)/shard_map/all_to_all | solution.py:176
  44.5 2.0 %collective-permute-start = (bf16[256,512]{1,0:T(8,128)(2,1)S(1)}, bf16[256,512]{1,0:T(8,128)(2,1)S(1)}, u32[]{:S(2)}, u32[]{:S(2)}) collective-permute-start(bf16[256,512]{1,0:T(8,128)(2,1)S(1)} %bitcast.24), channel_id=1, source_target_pairs={{0,128},{32,160},{64,192},{96,224},{128,0},{160,32},{192,64},{224,... | collective-permute-start | bytes 786440 | tf_op jit(solution)/shard_map/ppermute | solution.py:171
  46.5 0.5 shard_map.111.refs_0_
  47.1 0.0 collective-permute-done.1
  47.1 6.8 %collective-permute-done.rows_ref = bf16[256,512]{1,0:T(8,128)(2,1)S(1)} collective-permute-done((bf16[256,512]{1,0:T(8,128)(2,1)S(1)}, bf16[256,512]{1,0:T(8,128)(2,1)S(1)}, u32[]{:S(2)}, u32[]{:S(2)}) %collective-permute-start) | collective-permute-done | bytes 262176 | tf_op jit(solution)/shard_map/ppermute | solution.py:171
  53.9 0.5 shard_map.112
  54.5 32.4 %all_to_all.21 = bf16[16,96,256]{2,1,0:T(8,128)(2,1)S(1)} all-to-all(bf16[16,96,256]{2,1,0:T(8,128)(2,1)S(1)} %shard_map.112), channel_id=1, replica_groups={{0,32,64,96,256,288,320,352,512,544,576,608,768,800,832,864},{128,160,1..., dimensions={0} | all-to-all | bytes 1572864 | tf_op jit(solution)/shard_map/all_to_all | solution.py:158
  86.9 0.1 convert_reduce_fusion
  87.1 0.1 broadcast_in_dim.15
  87.2 30.1 %all_to_all.22.near_ref = bf16[16,96,256]{2,1,0:T(8,128)(2,1)S(1)} all-to-all(bf16[16,96,256]{2,1,0:T(8,128)(2,1)S(1)} %broadcast_in_dim.15), channel_id=1, replica_groups={{0,32,64,96,256,288,320,352,512,544,576,608,768,800,832,864},{128,160,1..., dimensions={0} | all-to-all | bytes 1572864 | tf_op jit(solution)/shard_map/all_to_all | solution.py:158
  117.3 0.4 shard_map.114
  117.7 4.5 %collective-permute-start.2 = (bf16[256,512]{1,0:T(8,128)(2,1)S(1)}, bf16[256,512]{1,0:T(8,128)(2,1)S(1)}, u32[]{:S(2)}, u32[]{:S(2)}) collective-permute-start(bf16[256,512]{1,0:T(8,128)(2,1)S(1)} %shard_map.114), channel_id=1, source_target_pairs={{0,128},{32,160},{64,192},{96,224},{128,0},{160,32},{192,64},{224,... | collective-permute-start | bytes 786440 | tf_op jit(solution)/shard_map/ppermute | solution.py:171
  122.3 0.4 shard_map.113
  122.7 4.5 %collective-permute-done.2 = bf16[256,512]{1,0:T(8,128)(2,1)S(1)} collective-permute-done((bf16[256,512]{1,0:T(8,128)(2,1)S(1)}, bf16[256,512]{1,0:T(8,128)(2,1)S(1)}, u32[]{:S(2)}, u32[]{:S(2)}) %collective-permute-start.2) | collective-permute-done | bytes 262176 | tf_op jit(solution)/shard_map/ppermute | solution.py:171
  127.2 0.8 add_convert_fusion
  127.9 6.2 %all-to-all-start.3 = ((bf16[32,8,512]{2,1,0:T(8,128)(2,1)}), bf16[32,8,512]{2,1,0:T(8,128)(2,1)S(1)}, u32[]{:S(2)}, u32[]{:S(2)}) async-start(bf16[32,8,512]{2,1,0:T(8,128)(2,1)} %bitcast.13), calls=%async_computation.3 | async-start | bytes 524288 | tf_op jit(solution)/shard_map/all_to_all | solution.py:176
  134.1 0.0 copy-start
  134.2 0.1 fusion.1
  134.2 2.8 %collective-permute-start.4 = (bf16[8,96,256]{2,1,0:T(8,128)(2,1)S(1)}, bf16[8,96,256]{2,1,0:T(8,128)(2,1)S(1)}, u32[]{:S(2)}, u32[]{:S(2)}) collective-permute-start(bf16[8,96,256]{2,1,0:T(8,128)(2,1)S(1)} %get-tuple-element.27), channel_id=1, source_target_pairs={{0,896},{32,928},{64,960},{96,992},{128,256},{160,288},{192,320},{... | collective-permute-start | bytes 1179656 | tf_op jit(solution)/shard_map/ppermute | solution.py:171
  137.0 2.6 %collective-permute-start.3 = (bf16[8,96,256]{2,1,0:T(8,128)(2,1)S(1)}, bf16[8,96,256]{2,1,0:T(8,128)(2,1)S(1)}, u32[]{:S(2)}, u32[]{:S(2)}) collective-permute-start(bf16[8,96,256]{2,1,0:T(8,128)(2,1)S(1)} %get-tuple-element.28), channel_id=1, source_target_pairs={{0,128},{32,160},{64,192},{96,224},{128,0},{160,32},{192,64},{224,... | collective-permute-start | bytes 1179656 | tf_op jit(solution)/shard_map/ppermute | solution.py:171
  139.6 8.2 %collective-permute-done.4.far1_ref = bf16[8,96,256]{2,1,0:T(8,128)(2,1)S(1)} collective-permute-done((bf16[8,96,256]{2,1,0:T(8,128)(2,1)S(1)}, bf16[8,96,256]{2,1,0:T(8,128)(2,1)S(1)}, u32[]{:S(2)}, u32[]{:S(2)}) %collective-permute-start.4) | collective-permute-done | bytes 393248 | tf_op jit(solution)/shard_map/ppermute | solution.py:171
  147.8 1.2 collective-permute-done.3.far0_ref
  149.0 1.7 %shard_map.116 = (bf16[224,1024]{1,0:T(8,128)(2,1)}, bf16[224,1024]{1,0:T(8,128)(2,1)}, bf16[224,1024]{1,0:T(8,128)(2,1)}) custom-call(s32[1]{0:T(128)} %bitcast.2.odd_ref, bf16[16,96,256]{2,1,0:T(8,128)(2,1)S(1)} %all_to_all.22.near_ref, bf16[8,96,256]{2,1,0:T(8,128)(2,1)S(1)} %collective-permute-done.3.far0_ref, ...), custom_call_target="tpu_custom_call" | custom-call | flops 352321536 | bytes 3211268 | tf_op jit(solution)/shard_map/pallas_call | solution.py:140
  150.7 0.0 all-to-all-done.3
  150.7 0.0 copy-done
  150.7 0.8 shard_map.115
  (3 shorter events, 0.1 us)
Async XLA Ops:
  3.8 5.6 %copy-start.1 = (bf16[256,512]{1,0:T(8,128)(2,1)S(1)}, bf16[256,512]{1,0:T(8,128)(2,1)}, u32[]{:S(2)}) copy-start(bf16[256,512]{1,0:T(8,128)(2,1)} %get-tuple-element.17) | copy-start | bytes 786436
  5.3 41.8 %collective-permute-start.1 = (bf16[3,224,512]{2,1,0:T(8,128)(2,1)S(1)}, bf16[3,224,512]{2,1,0:T(8,128)(2,1)S(1)}, u32[]{:S(2)}, u32[]{:S(2)}) collective-permute-start(bf16[3,224,512]{2,1,0:T(8,128)(2,1)S(1)} %pad_maximum_fusion), channel_id=1, source_target_pairs={{0,128},{32,160},{64,192},{96,224},{128,0},{160,32},{192,64},{224,... | collective-permute-start | bytes 2064392 | tf_op jit(solution)/shard_map/ppermute | solution.py:171
  44.5 9.4 %collective-permute-start = (bf16[256,512]{1,0:T(8,128)(2,1)S(1)}, bf16[256,512]{1,0:T(8,128)(2,1)S(1)}, u32[]{:S(2)}, u32[]{:S(2)}) collective-permute-start(bf16[256,512]{1,0:T(8,128)(2,1)S(1)} %bitcast.24), channel_id=1, source_target_pairs={{0,128},{32,160},{64,192},{96,224},{128,0},{160,32},{192,64},{224,... | collective-permute-start | bytes 786440 | tf_op jit(solution)/shard_map/ppermute | solution.py:171
  117.7 9.4 %collective-permute-start.2 = (bf16[256,512]{1,0:T(8,128)(2,1)S(1)}, bf16[256,512]{1,0:T(8,128)(2,1)S(1)}, u32[]{:S(2)}, u32[]{:S(2)}) collective-permute-start(bf16[256,512]{1,0:T(8,128)(2,1)S(1)} %shard_map.114), channel_id=1, source_target_pairs={{0,128},{32,160},{64,192},{96,224},{128,0},{160,32},{192,64},{224,... | collective-permute-start | bytes 786440 | tf_op jit(solution)/shard_map/ppermute | solution.py:171
  127.9 22.7 %all-to-all-start.3 = ((bf16[32,8,512]{2,1,0:T(8,128)(2,1)}), bf16[32,8,512]{2,1,0:T(8,128)(2,1)S(1)}, u32[]{:S(2)}, u32[]{:S(2)}) async-start(bf16[32,8,512]{2,1,0:T(8,128)(2,1)} %bitcast.13), calls=%async_computation.3 | async-start | bytes 524288 | tf_op jit(solution)/shard_map/all_to_all | solution.py:176
  134.1 16.5 %copy-start = (bf16[64,256]{1,0:T(8,128)(2,1)S(1)}, bf16[64,256]{1,0:T(8,128)(2,1)}, u32[]{:S(2)}) copy-start(bf16[64,256]{1,0:T(8,128)(2,1)} %get-tuple-element.20.mix_ref) | copy-start | bytes 98308
  134.2 13.6 %collective-permute-start.4 = (bf16[8,96,256]{2,1,0:T(8,128)(2,1)S(1)}, bf16[8,96,256]{2,1,0:T(8,128)(2,1)S(1)}, u32[]{:S(2)}, u32[]{:S(2)}) collective-permute-start(bf16[8,96,256]{2,1,0:T(8,128)(2,1)S(1)} %get-tuple-element.27), channel_id=1, source_target_pairs={{0,896},{32,928},{64,960},{96,992},{128,256},{160,288},{192,320},{... | collective-permute-start | bytes 1179656 | tf_op jit(solution)/shard_map/ppermute | solution.py:171
  137.0 12.0 %collective-permute-start.3 = (bf16[8,96,256]{2,1,0:T(8,128)(2,1)S(1)}, bf16[8,96,256]{2,1,0:T(8,128)(2,1)S(1)}, u32[]{:S(2)}, u32[]{:S(2)}) collective-permute-start(bf16[8,96,256]{2,1,0:T(8,128)(2,1)S(1)} %get-tuple-element.28), channel_id=1, source_target_pairs={{0,128},{32,160},{64,192},{96,224},{128,0},{160,32},{192,64},{224,... | collective-permute-start | bytes 1179656 | tf_op jit(solution)/shard_map/ppermute | solution.py:171

commit v7 on v6

--- a/solution.py
+++ b/solution.py
@@ -209,8 +209,8 @@
         )
 
     mine = columns(odd[0] * half)
-    theirs = neighbour_swap(jnp.stack(columns((1 - odd[0]) * half)), 0)
-    theirs = (theirs[0], theirs[1], theirs[2])
+    theirs = tuple(neighbour_swap(w, 0) for w in columns((1 - odd[0]) * half))
+    rows, theirs = lax.optimization_barrier((rows, theirs))
     pair_rows = neighbour_swap(rows, 0)
     shape = (group, 3 * each, cols)
     (share,) = run(row_kernel(False), [(shape, F32)], (rows,) + mine, work // 2)

time: 152 us -> 159 us (1.046)
  blocking collectives: 97.7 us -> 65.4 us
  starting transfers between devices: 22.3 us -> 53.4 us
  waiting for transfers between devices: 20.6 us -> 29.7 us
    all_to_all x1 -> x0, blocking collectives: 35.1 us -> none  [expert_swap(): lax.all_to_all(rows.reshape(count, CAP, rows.shape[1]), 'expert', split_a...]
    all_to_all x1 -> x2, starting transfers between devices: 6.19 us -> 34.3 us  [expert_swap(): lax.all_to_all(rows.reshape(count, CAP, rows.shape[1]), 'expert', split_a...]
    ppermute x5 -> x7, waiting for transfers between devices: 20.6 us -> 29.7 us  [neighbour_swap(): return lax.ppermute(block, 'dp', pairs)]
    ppermute x5 -> x7, starting transfers between devices: 16.1 us -> 19.2 us  [neighbour_swap(): return lax.ppermute(block, 'dp', pairs)]
    all_to_all x2, blocking collectives: 62.6 us -> 65.4 us  [group_swap(): lax.all_to_all(blocks, 'dp', split_axis=0, concat_axis=0, axis_index_grou...]
  transfers between devices with their start and end apart: 6 -> 9, of which waited for: 4 -> 7; matrix products, arithmetic and copies ran while one was open for 0% -> 1% of each run, Pallas kernels for 2% -> 2%
where the time goes in v7:
time: 159 us; the launch traced here: 158 us
  blocking collectives  65.4 us (41%)
  starting transfers between devices  53.4 us (34%)
  waiting for transfers between devices  29.7 us (19%)
  Pallas kernels  6.56 us (4%)
    all_to_all x2, blocking collectives, group_swap(): lax.all_to_all(blocks, 'dp', split_axis=0, concat_axis=0, axis_index_grou...  65.4 us
    all_to_all x2, starting transfers between devices, expert_swap(): lax.all_to_all(rows.reshape(count, CAP, rows.shape[1]), 'expert', split_a...  34.3 us
    ppermute x7, waiting for transfers between devices, neighbour_swap(): return lax.ppermute(block, 'dp', pairs)  29.7 us
    ppermute x7, starting transfers between devices, neighbour_swap(): return lax.ppermute(block, 'dp', pairs)  19.2 us
    pallas_call x7, Pallas kernels, run(): pl.pallas_call(kernel, out_shape=outs, in_specs=[SMEM if a.shape == (1,)...  6.56 us
  transfers between devices with their start and end apart: 9, of which 7 were waited for; matrix products, arithmetic and copies ran while one was open for 1% of the time, Pallas kernels for 2%

profile of v7, /device:TPU:1, one launch (start us, length us, event | category | flops | bytes accessed | tf_op | source)
XLA Modules:
  0.0 158.1 jit_solution(10713699626612567203)
XLA Ops:
  0.6 0.0 copy-start.1
  0.6 0.0 copy-start.2
  0.7 2.1 %shard_map.110 = (bf16[256,512]{1,0:T(8,128)(2,1)}, bf16[64,256]{1,0:T(8,128)(2,1)}) custom-call(s32[8,16]{1,0:T(8,128)} %bitcast.29, f32[8,16]{1,0:T(8,128)} %bitcast.30, bf16[16,224]{1,0:T(8,128)(2,1)} %tokens_ref.1, bf16[16,224]{1,0:T(8,128)(2,1)} %cotangent_ref.1), custom_call_target="tpu_custom_call" | custom-call | flops 3670016 | bytes 310272 | tf_op jit(solution)/shard_map/pallas_call | solution.py:140
  2.8 20.5 %all-to-all-start = ((bf16[32,8,512]{2,1,0:T(8,128)(2,1)}), bf16[32,8,512]{2,1,0:T(8,128)(2,1)S(1)}, u32[]{:S(2)}, u32[]{:S(2)}) async-start(bf16[32,8,512]{2,1,0:T(8,128)(2,1)} %bitcast.28), calls=%async_computation | async-start | bytes 524288 | tf_op jit(solution)/shard_map/all_to_all | solution.py:176
  23.3 1.1 dynamic-slice_bitcast_fusion
  24.4 3.3 %collective-permute-start.2 = (bf16[224,512]{1,0:T(8,128)(2,1)S(1)}, bf16[224,512]{1,0:T(8,128)(2,1)S(1)}, u32[]{:S(2)}, u32[]{:S(2)}) collective-permute-start(bf16[224,512]{1,0:T(8,128)(2,1)S(1)} %get-tuple-element.38), channel_id=1, source_target_pairs={{0,128},{32,160},{64,192},{96,224},{128,0},{160,32},{192,64},{224,... | collective-permute-start | bytes 688136 | tf_op jit(solution)/shard_map/ppermute | solution.py:171
  27.8 0.0 copy-done.1
  27.8 2.0 %collective-permute-start.1 = (bf16[224,512]{1,0:T(8,128)(2,1)S(1)}, bf16[224,512]{1,0:T(8,128)(2,1)S(1)}, u32[]{:S(2)}, u32[]{:S(2)}) collective-permute-start(bf16[224,512]{1,0:T(8,128)(2,1)S(1)} %get-tuple-element.40), channel_id=1, source_target_pairs={{0,128},{32,160},{64,192},{96,224},{128,0},{160,32},{192,64},{224,... | collective-permute-start | bytes 688136 | tf_op jit(solution)/shard_map/ppermute | solution.py:171
  29.8 0.0 copy-done.2
  29.8 3.3 %collective-permute-start = (bf16[224,512]{1,0:T(8,128)(2,1)S(1)}, bf16[224,512]{1,0:T(8,128)(2,1)S(1)}, u32[]{:S(2)}, u32[]{:S(2)}) collective-permute-start(bf16[224,512]{1,0:T(8,128)(2,1)S(1)} %get-tuple-element.42), channel_id=1, source_target_pairs={{0,128},{32,160},{64,192},{96,224},{128,0},{160,32},{192,64},{224,... | collective-permute-start | bytes 688136 | tf_op jit(solution)/shard_map/ppermute | solution.py:171
  33.2 0.1 collective-permute-done.2.down_ref
  33.3 4.9 %collective-permute-done.1.up_ref = bf16[224,512]{1,0:T(8,128)(2,1)S(1)} collective-permute-done((bf16[224,512]{1,0:T(8,128)(2,1)S(1)}, bf16[224,512]{1,0:T(8,128)(2,1)S(1)}, u32[]{:S(2)}, u32[]{:S(2)}) %collective-permute-start.1) | collective-permute-done | bytes 229408 | tf_op jit(solution)/shard_map/ppermute | solution.py:171
  38.2 4.9 %collective-permute-done.gate_ref = bf16[224,512]{1,0:T(8,128)(2,1)S(1)} collective-permute-done((bf16[224,512]{1,0:T(8,128)(2,1)S(1)}, bf16[224,512]{1,0:T(8,128)(2,1)S(1)}, u32[]{:S(2)}, u32[]{:S(2)}) %collective-permute-start) | collective-permute-done | bytes 229408 | tf_op jit(solution)/shard_map/ppermute | solution.py:171
  43.1 0.0 all-to-all-done
  43.1 3.3 %collective-permute-start.3 = (bf16[256,512]{1,0:T(8,128)(2,1)S(1)}, bf16[256,512]{1,0:T(8,128)(2,1)S(1)}, u32[]{:S(2)}, u32[]{:S(2)}) collective-permute-start(bf16[256,512]{1,0:T(8,128)(2,1)S(1)} %bitcast.24), channel_id=1, source_target_pairs={{0,128},{32,160},{64,192},{96,224},{128,0},{160,32},{192,64},{224,... | collective-permute-start | bytes 786440 | tf_op jit(solution)/shard_map/ppermute | solution.py:171
  46.4 0.5 shard_map.111.refs_0_
  47.0 4.8 %collective-permute-done.3.rows_ref = bf16[256,512]{1,0:T(8,128)(2,1)S(1)} collective-permute-done((bf16[256,512]{1,0:T(8,128)(2,1)S(1)}, bf16[256,512]{1,0:T(8,128)(2,1)S(1)}, u32[]{:S(2)}, u32[]{:S(2)}) %collective-permute-start.3) | collective-permute-done | bytes 262176 | tf_op jit(solution)/shard_map/ppermute | solution.py:171
  51.8 0.5 shard_map.112
  52.3 36.1 %all_to_all.20 = bf16[16,96,256]{2,1,0:T(8,128)(2,1)S(1)} all-to-all(bf16[16,96,256]{2,1,0:T(8,128)(2,1)S(1)} %shard_map.112), channel_id=1, replica_groups={{0,32,64,96,256,288,320,352,512,544,576,608,768,800,832,864},{128,160,1..., dimensions={0} | all-to-all | bytes 1572864 | tf_op jit(solution)/shard_map/all_to_all | solution.py:158
  88.4 0.1 convert_reduce_fusion
  88.6 0.1 broadcast_in_dim.15
  88.7 29.3 %all_to_all.21.near_ref = bf16[16,96,256]{2,1,0:T(8,128)(2,1)S(1)} all-to-all(bf16[16,96,256]{2,1,0:T(8,128)(2,1)S(1)} %broadcast_in_dim.15), channel_id=1, replica_groups={{0,32,64,96,256,288,320,352,512,544,576,608,768,800,832,864},{128,160,1..., dimensions={0} | all-to-all | bytes 1572864 | tf_op jit(solution)/shard_map/all_to_all | solution.py:158
  118.0 0.4 shard_map.114
  118.4 1.9 %collective-permute-start.4 = (bf16[256,512]{1,0:T(8,128)(2,1)S(1)}, bf16[256,512]{1,0:T(8,128)(2,1)S(1)}, u32[]{:S(2)}, u32[]{:S(2)}) collective-permute-start(bf16[256,512]{1,0:T(8,128)(2,1)S(1)} %shard_map.114), channel_id=1, source_target_pairs={{0,128},{32,160},{64,192},{96,224},{128,0},{160,32},{192,64},{224,... | collective-permute-start | bytes 786440 | tf_op jit(solution)/shard_map/ppermute | solution.py:171
  120.3 0.4 shard_map.113
  120.8 5.9 %collective-permute-done.4 = bf16[256,512]{1,0:T(8,128)(2,1)S(1)} collective-permute-done((bf16[256,512]{1,0:T(8,128)(2,1)S(1)}, bf16[256,512]{1,0:T(8,128)(2,1)S(1)}, u32[]{:S(2)}, u32[]{:S(2)}) %collective-permute-start.4) | collective-permute-done | bytes 262176 | tf_op jit(solution)/shard_map/ppermute | solution.py:171
  126.7 0.8 add_convert_fusion
  127.5 13.8 %all-to-all-start.3 = ((bf16[32,8,512]{2,1,0:T(8,128)(2,1)}), bf16[32,8,512]{2,1,0:T(8,128)(2,1)S(1)}, u32[]{:S(2)}, u32[]{:S(2)}) async-start(bf16[32,8,512]{2,1,0:T(8,128)(2,1)} %bitcast.13), calls=%async_computation.3 | async-start | bytes 524288 | tf_op jit(solution)/shard_map/all_to_all | solution.py:176
  141.2 0.0 copy-start
  141.2 0.1 fusion.1
  141.3 1.9 %collective-permute-start.6 = (bf16[8,96,256]{2,1,0:T(8,128)(2,1)S(1)}, bf16[8,96,256]{2,1,0:T(8,128)(2,1)S(1)}, u32[]{:S(2)}, u32[]{:S(2)}) collective-permute-start(bf16[8,96,256]{2,1,0:T(8,128)(2,1)S(1)} %get-tuple-element.35), channel_id=1, source_target_pairs={{0,896},{32,928},{64,960},{96,992},{128,256},{160,288},{192,320},{... | collective-permute-start | bytes 1179656 | tf_op jit(solution)/shard_map/ppermute | solution.py:171
  143.2 3.4 %collective-permute-start.5 = (bf16[8,96,256]{2,1,0:T(8,128)(2,1)S(1)}, bf16[8,96,256]{2,1,0:T(8,128)(2,1)S(1)}, u32[]{:S(2)}, u32[]{:S(2)}) collective-permute-start(bf16[8,96,256]{2,1,0:T(8,128)(2,1)S(1)} %get-tuple-element.36), channel_id=1, source_target_pairs={{0,128},{32,160},{64,192},{96,224},{128,0},{160,32},{192,64},{224,... | collective-permute-start | bytes 1179656 | tf_op jit(solution)/shard_map/ppermute | solution.py:171
  146.7 8.2 %collective-permute-done.6.far1_ref = bf16[8,96,256]{2,1,0:T(8,128)(2,1)S(1)} collective-permute-done((bf16[8,96,256]{2,1,0:T(8,128)(2,1)S(1)}, bf16[8,96,256]{2,1,0:T(8,128)(2,1)S(1)}, u32[]{:S(2)}, u32[]{:S(2)}) %collective-permute-start.6) | collective-permute-done | bytes 393248 | tf_op jit(solution)/shard_map/ppermute | solution.py:171
  154.9 0.8 collective-permute-done.5.far0_ref
  155.7 1.7 %shard_map.116 = (bf16[224,1024]{1,0:T(8,128)(2,1)}, bf16[224,1024]{1,0:T(8,128)(2,1)}, bf16[224,1024]{1,0:T(8,128)(2,1)}) custom-call(s32[1]{0:T(128)} %bitcast.2.odd_ref, bf16[16,96,256]{2,1,0:T(8,128)(2,1)S(1)} %all_to_all.21.near_ref, bf16[8,96,256]{2,1,0:T(8,128)(2,1)S(1)} %collective-permute-done.5.far0_ref, ...), custom_call_target="tpu_custom_call" | custom-call | flops 352321536 | bytes 3211268 | tf_op jit(solution)/shard_map/pallas_call | solution.py:140
  157.4 0.0 all-to-all-done.3
  157.4 0.0 copy-done
  157.4 0.8 shard_map.115
  (4 shorter events, 0.1 us)
Async XLA Ops:
  0.6 27.1 %copy-start.1 = (bf16[1,224,1024]{2,1,0:T(8,128)(2,1)S(1)}, bf16[1,224,1024]{2,1,0:T(8,128)(2,1)}, u32[]{:S(2)}) copy-start(bf16[1,224,1024]{2,1,0:T(8,128)(2,1)} %param.11) | copy-start | bytes 1376260
  0.6 29.1 %copy-start.2 = (bf16[1,224,1024]{2,1,0:T(8,128)(2,1)S(1)}, bf16[1,224,1024]{2,1,0:T(8,128)(2,1)}, u32[]{:S(2)}) copy-start(bf16[1,224,1024]{2,1,0:T(8,128)(2,1)} %param.10) | copy-start | bytes 1376260
  2.8 40.3 %all-to-all-start = ((bf16[32,8,512]{2,1,0:T(8,128)(2,1)}), bf16[32,8,512]{2,1,0:T(8,128)(2,1)S(1)}, u32[]{:S(2)}, u32[]{:S(2)}) async-start(bf16[32,8,512]{2,1,0:T(8,128)(2,1)} %bitcast.28), calls=%async_computation | async-start | bytes 524288 | tf_op jit(solution)/shard_map/all_to_all | solution.py:176
  24.4 8.9 %collective-permute-start.2 = (bf16[224,512]{1,0:T(8,128)(2,1)S(1)}, bf16[224,512]{1,0:T(8,128)(2,1)S(1)}, u32[]{:S(2)}, u32[]{:S(2)}) collective-permute-start(bf16[224,512]{1,0:T(8,128)(2,1)S(1)} %get-tuple-element.38), channel_id=1, source_target_pairs={{0,128},{32,160},{64,192},{96,224},{128,0},{160,32},{192,64},{224,... | collective-permute-start | bytes 688136 | tf_op jit(solution)/shard_map/ppermute | solution.py:171
  27.8 10.4 %collective-permute-start.1 = (bf16[224,512]{1,0:T(8,128)(2,1)S(1)}, bf16[224,512]{1,0:T(8,128)(2,1)S(1)}, u32[]{:S(2)}, u32[]{:S(2)}) collective-permute-start(bf16[224,512]{1,0:T(8,128)(2,1)S(1)} %get-tuple-element.40), channel_id=1, source_target_pairs={{0,128},{32,160},{64,192},{96,224},{128,0},{160,32},{192,64},{224,... | collective-permute-start | bytes 688136 | tf_op jit(solution)/shard_map/ppermute | solution.py:171
  29.8 13.3 %collective-permute-start = (bf16[224,512]{1,0:T(8,128)(2,1)S(1)}, bf16[224,512]{1,0:T(8,128)(2,1)S(1)}, u32[]{:S(2)}, u32[]{:S(2)}) collective-permute-start(bf16[224,512]{1,0:T(8,128)(2,1)S(1)} %get-tuple-element.42), channel_id=1, source_target_pairs={{0,128},{32,160},{64,192},{96,224},{128,0},{160,32},{192,64},{224,... | collective-permute-start | bytes 688136 | tf_op jit(solution)/shard_map/ppermute | solution.py:171
  43.1 8.6 %collective-permute-start.3 = (bf16[256,512]{1,0:T(8,128)(2,1)S(1)}, bf16[256,512]{1,0:T(8,128)(2,1)S(1)}, u32[]{:S(2)}, u32[]{:S(2)}) collective-permute-start(bf16[256,512]{1,0:T(8,128)(2,1)S(1)} %bitcast.24), channel_id=1, source_target_pairs={{0,128},{32,160},{64,192},{96,224},{128,0},{160,32},{192,64},{224,... | collective-permute-start | bytes 786440 | tf_op jit(solution)/shard_map/ppermute | solution.py:171
  118.4 8.3 %collective-permute-start.4 = (bf16[256,512]{1,0:T(8,128)(2,1)S(1)}, bf16[256,512]{1,0:T(8,128)(2,1)S(1)}, u32[]{:S(2)}, u32[]{:S(2)}) collective-permute-start(bf16[256,512]{1,0:T(8,128)(2,1)S(1)} %shard_map.114), channel_id=1, source_target_pairs={{0,128},{32,160},{64,192},{96,224},{128,0},{160,32},{192,64},{224,... | collective-permute-start | bytes 786440 | tf_op jit(solution)/shard_map/ppermute | solution.py:171
  127.5 29.9 %all-to-all-start.3 = ((bf16[32,8,512]{2,1,0:T(8,128)(2,1)}), bf16[32,8,512]{2,1,0:T(8,128)(2,1)S(1)}, u32[]{:S(2)}, u32[]{:S(2)}) async-start(bf16[32,8,512]{2,1,0:T(8,128)(2,1)} %bitcast.13), calls=%async_computation.3 | async-start | bytes 524288 | tf_op jit(solution)/shard_map/all_to_all | solution.py:176
  141.2 16.1 %copy-start = (bf16[64,256]{1,0:T(8,128)(2,1)S(1)}, bf16[64,256]{1,0:T(8,128)(2,1)}, u32[]{:S(2)}) copy-start(bf16[64,256]{1,0:T(8,128)(2,1)} %get-tuple-element.28.mix_ref) | copy-start | bytes 98308
  141.3 13.6 %collective-permute-start.6 = (bf16[8,96,256]{2,1,0:T(8,128)(2,1)S(1)}, bf16[8,96,256]{2,1,0:T(8,128)(2,1)S(1)}, u32[]{:S(2)}, u32[]{:S(2)}) collective-permute-start(bf16[8,96,256]{2,1,0:T(8,128)(2,1)S(1)} %get-tuple-element.35), channel_id=1, source_target_pairs={{0,896},{32,928},{64,960},{96,992},{128,256},{160,288},{192,320},{... | collective-permute-start | bytes 1179656 | tf_op jit(solution)/shard_map/ppermute | solution.py:171
  143.2 12.4 %collective-permute-start.5 = (bf16[8,96,256]{2,1,0:T(8,128)(2,1)S(1)}, bf16[8,96,256]{2,1,0:T(8,128)(2,1)S(1)}, u32[]{:S(2)}, u32[]{:S(2)}) collective-permute-start(bf16[8,96,256]{2,1,0:T(8,128)(2,1)S(1)} %get-tuple-element.36), channel_id=1, source_target_pairs={{0,128},{32,160},{64,192},{96,224},{128,0},{160,32},{192,64},{224,... | collective-permute-start | bytes 1179656 | tf_op jit(solution)/shard_map/ppermute | solution.py:171

commit v8 on v7

--- a/solution.py
+++ b/solution.py
@@ -24,7 +24,11 @@
     return block.astype(F32).T.astype(BF16)
 
 
-def pick_kernel(routes_ref, scores_ref, tokens_ref, cotangent_ref, sent_ref, mix_ref):
+def pick_kernel(odd_ref, routes_ref, scores_ref, tokens_ref, cotangent_ref, *refs):
+    weights, (sent_ref, mix_ref), mine, theirs = refs[:3], refs[3:5], refs[5:8], refs[8:11]
+    copies = list(column_copies(odd_ref[0], weights, mine, theirs, refs[11]))
+    for copy in copies:
+        copy.start()
     top_count, tok_count = routes_ref.shape
     slots = sent_ref.shape[0]
     width = tokens_ref.shape[1]
@@ -60,20 +64,33 @@
     sent_ref[:, :width] = rows.astype(BF16)
     rows = jnp.dot(picker, cotangent_ref[...], preferred_element_type=F32)
     sent_ref[:, pitch : pitch + width] = (rows * slot_gate).astype(BF16)
+    for copy in copies:
+        copy.wait()
+
+
+def column_copies(odd, weights, mine, theirs, sems):
+    half = mine[0].shape[1]
+    for index, w_ref in enumerate(weights):
+        for side, to_refs in enumerate((theirs, mine)):
+            parity = odd if side else 1 - odd
+            at = pl.ds(pl.multiple_of(parity * half, half), half)
+            yield pltpu.make_async_copy(
+                w_ref.at[:, at], to_refs[index], sems.at[2 * index + side]
+            )
 
 
 def row_kernel(base):
-    def kernel(rows_ref, gate_ref, up_ref, down_ref, *refs):
+    def kernel(rows_ref, weights_ref, *refs):
         to_ref = refs[-1]
-        width, span = gate_ref.shape
+        width = weights_ref.shape[1]
         pitch = rows_ref.shape[1] // 2
         group, depth, cols = to_ref.shape
         each = depth // 3
         x = flip(rows_ref[:, :width])
         do = flip(rows_ref[:, pitch : pitch + width])
-        for index, (w_ref, r) in enumerate(((gate_ref, x), (up_ref, x), (down_ref, do))):
+        for index, r in enumerate((x, x, do)):
             part = lax.dot_general(
-                w_ref[...], r, (((0,), (0,)), ((), ())), preferred_element_type=F32
+                weights_ref[index], r, (((0,), (0,)), ((), ())), preferred_element_type=F32
             ).reshape(group, each, cols)
             at = pl.ds(index * each, each)
             if base:
@@ -89,15 +106,16 @@
     return ref[:, index * each : (index + 1) * each, :].reshape(group * each, cols)
 
 
-def out_kernel(near_ref, gate_ref, up_ref, down_ref, outs_ref):
-    width = gate_ref.shape[0]
+def out_kernel(near_ref, weights_ref, outs_ref):
+    width = weights_ref.shape[1]
     pitch = outs_ref.shape[1] // 2
 
-    def times(w_ref, index):
-        return jnp.dot(w_ref[...], array_rows(near_ref, index), preferred_element_type=F32)
-
-    out = times(down_ref, 0)
-    grad = times(gate_ref, 1) + times(up_ref, 2)
+    def times(weight, index):
+        rows = array_rows(near_ref, index)
+        return jnp.dot(weights_ref[weight], rows, preferred_element_type=F32)
+
+    out = times(2, 0)
+    grad = times(0, 1) + times(1, 2)
     outs_ref[...] = jnp.zeros(outs_ref.shape, outs_ref.dtype)
     outs_ref[:, :width] = out.T.astype(outs_ref.dtype)
     outs_ref[:, pitch : pitch + width] = grad.T.astype(outs_ref.dtype)
@@ -134,7 +152,7 @@
 SMEM = pl.BlockSpec(memory_space=pltpu.SMEM)
 
 
-def run(kernel, outs, args, flops, grant=16):
+def run(kernel, outs, args, flops):
     outs = [jax.ShapeDtypeStruct(shape, dtype) for shape, dtype in outs]
     moved = sum(a.size * a.dtype.itemsize for a in list(args) + outs)
     return pl.pallas_call(
@@ -142,7 +160,7 @@
         out_shape=outs,
         in_specs=[SMEM if a.shape == (1,) else VMEM for a in args],
         out_specs=[VMEM] * len(outs),
-        compiler_params=pltpu.CompilerParams(vmem_limit_bytes=grant and grant * 2**20),
+        compiler_params=pltpu.CompilerParams(vmem_limit_bytes=16 * 2**20),
         cost_estimate=pl.CostEstimate(flops=flops, bytes_accessed=moved, transcendentals=0),
     )(*args)
 
@@ -193,28 +211,23 @@
     odd = lax.rem(lax.axis_index("dp") // INNER, 2).astype(jnp.int32).reshape(1)
     work = 6 * slots * HID * width
 
-    sent, mix = run(
+    place = pl.BlockSpec(memory_space=pl.ANY)
+    shapes = ((slots, 2 * pitch), (4 * tok_count, slots)) + ((width, half),) * 6
+    sent, mix, *split = pl.pallas_call(
         pick_kernel,
-        [((slots, 2 * pitch), BF16), ((4 * tok_count, slots), BF16)],
-        (routes.T, scores.T, tokens, cotangent),
-        4 * slots * tok_count * width,
-        grant=None,
-    )
-    sent, odd = lax.optimization_barrier((sent, odd))
+        out_shape=[jax.ShapeDtypeStruct(dims, BF16) for dims in shapes],
+        in_specs=[SMEM] + [VMEM] * 4 + [place] * 3,
+        out_specs=[VMEM] * 2 + [place] * 6,
+        scratch_shapes=[pltpu.SemaphoreType.DMA((6,))],
+    )(odd, routes.T, scores.T, tokens, cotangent, w_gate[0], w_up[0], w_down[0])
+    mine = jnp.stack(split[:3])
+    theirs = neighbour_swap(jnp.stack(split[3:]), 0)
     rows = expert_swap(sent)
     cols = rows.shape[0]
-    def columns(start):
-        return tuple(
-            lax.dynamic_slice_in_dim(w[0], start, half, axis=1) for w in (w_gate, w_up, w_down)
-        )
-
-    mine = columns(odd[0] * half)
-    theirs = tuple(neighbour_swap(w, 0) for w in columns((1 - odd[0]) * half))
-    rows, theirs = lax.optimization_barrier((rows, theirs))
     pair_rows = neighbour_swap(rows, 0)
     shape = (group, 3 * each, cols)
-    (share,) = run(row_kernel(False), [(shape, F32)], (rows,) + mine, work // 2)
-    (pair_sums,) = run(row_kernel(True), [(shape, BF16)], (pair_rows,) + theirs + (share,), work // 2)
+    (share,) = run(row_kernel(False), [(shape, F32)], (rows, mine), work // 2)
+    (pair_sums,) = run(row_kernel(True), [(shape, BF16)], (pair_rows, theirs, share), work // 2)
     own = jnp.sum(group_swap(pair_sums).astype(F32), axis=0)
     pre_gate, pre_up, grad_hidden = own[:each], own[each : 2 * each], own[2 * each :]
     sigma = jax.nn.sigmoid(pre_gate)
@@ -229,9 +242,9 @@
     ).astype(BF16)
     near = group_swap(jnp.broadcast_to(block[None], (group,) + block.shape))
     outs_shape = (cols, 2 * pitch)
-    (sent,) = run(out_kernel, [(outs_shape, BF16)], (near,) + theirs, work // 2)
+    (sent,) = run(out_kernel, [(outs_shape, BF16)], (near, theirs), work // 2)
     got = neighbour_swap(sent, 0)
-    (outs,) = run(out_kernel, [(outs_shape, F32)], (near,) + mine, work // 2)
+    (outs,) = run(out_kernel, [(outs_shape, F32)], (near, mine), work // 2)
     outs = (outs + got.astype(F32)).astype(BF16)
     outs, late = lax.optimization_barrier((outs, near))
     far = tuple(

time: 159 us -> 198 us (1.25)
  Pallas kernels: 6.56 us -> 48.7 us
  starting transfers between devices: 53.4 us -> 48.4 us
  waiting for transfers between devices: 29.7 us -> 32 us
    pallas_call x0 -> x1, Pallas kernels: none -> 44.3 us  [local(): pl.pallas_call(pick_kernel, out_shape=[jax.ShapeDtypeStruct(dims, BF16) f...]
    all_to_all x2, waiting for transfers between devices: 0.01 us -> 10.8 us  [expert_swap(): lax.all_to_all(rows.reshape(count, CAP, rows.shape[1]), 'expert', split_a...]
    ppermute x7 -> x5, waiting for transfers between devices: 29.7 us -> 21.3 us  [neighbour_swap(): return lax.ppermute(block, 'dp', pairs)]
    ppermute x7 -> x5, starting transfers between devices: 19.2 us -> 13.8 us  [neighbour_swap(): return lax.ppermute(block, 'dp', pairs)]
    pallas_call x7 -> x6, Pallas kernels: 6.56 us -> 4.41 us  [run(): pl.pallas_call(kernel, out_shape=outs, in_specs=[SMEM if a.shape == (1,)...]
  transfers between devices with their start and end apart: 9 -> 7, of which waited for: 7 -> 6; matrix products, arithmetic and copies ran while one was open for 1% -> 1% of each run, Pallas kernels for 2% -> 1%
where the time goes in v8:
time: 198 us
  blocking collectives  65.4 us (33%)
  Pallas kernels  48.7 us (25%)
  starting transfers between devices  48.4 us (24%)
  waiting for transfers between devices  32 us (16%)
  other arithmetic  2.23 us (1%)
    all_to_all x2, blocking collectives, group_swap(): lax.all_to_all(blocks, 'dp', split_axis=0, concat_axis=0, axis_index_grou...  65.4 us
    pallas_call x1, Pallas kernels, local(): pl.pallas_call(pick_kernel, out_shape=[jax.ShapeDtypeStruct(dims, BF16) f...  44.3 us
    all_to_all x2, starting transfers between devices, expert_swap(): lax.all_to_all(rows.reshape(count, CAP, rows.shape[1]), 'expert', split_a...  34.7 us
    ppermute x5, waiting for transfers between devices, neighbour_swap(): return lax.ppermute(block, 'dp', pairs)  21.3 us
    ppermute x5, starting transfers between devices, neighbour_swap(): return lax.ppermute(block, 'dp', pairs)  13.8 us
    all_to_all x2, waiting for transfers between devices, expert_swap(): lax.all_to_all(rows.reshape(count, CAP, rows.shape[1]), 'expert', split_a...  10.8 us
    pallas_call x6, Pallas kernels, run(): pl.pallas_call(kernel, out_shape=outs, in_specs=[SMEM if a.shape == (1,)...  4.41 us
  transfers between devices with their start and end apart: 7, of which 6 were waited for; matrix products, arithmetic and copies ran while one was open for 1% of the time, Pallas kernels for 1%

profile of v8, /device:TPU:1, one launch (start us, length us, event | category | flops | bytes accessed | tf_op | source)
XLA Modules:
  0.0 197.8 jit_solution(14660030409951875797)
XLA Ops:
  0.7 44.3 %shard_map.110 = (bf16[256,512]{1,0:T(8,128)(2,1)}, bf16[64,256]{1,0:T(8,128)(2,1)}, bf16[224,512]{1,0:T(8,128)(2,1)}, bf16[224,512]{1,0:T(8,128)(2,1)}, bf16[22...) custom-call(s32[1]{0:T(128)} %bitcast.odd_ref, ...), custom_call_target="tpu_custom_call" | custom-call | tf_op jit(solution)/shard_map/pallas_call | solution.py:216
  45.0 0.0 copy-start.1
  45.0 0.0 copy-start.2
  45.0 0.0 copy-start.3
  45.0 20.6 %all-to-all-start = ((bf16[32,8,512]{2,1,0:T(8,128)(2,1)}), bf16[32,8,512]{2,1,0:T(8,128)(2,1)S(1)}, u32[]{:S(2)}, u32[]{:S(2)}) async-start(bf16[32,8,512]{2,1,0:T(8,128)(2,1)} %bitcast.26), calls=%async_computation | async-start | bytes 524288 | tf_op jit(solution)/shard_map/all_to_all | solution.py:194
  65.7 1.2 pad_maximum_fusion
  66.9 3.3 %collective-permute-start.1 = (bf16[3,224,512]{2,1,0:T(8,128)(2,1)S(1)}, bf16[3,224,512]{2,1,0:T(8,128)(2,1)S(1)}, u32[]{:S(2)}, u32[]{:S(2)}) collective-permute-start(bf16[3,224,512]{2,1,0:T(8,128)(2,1)S(1)} %pad_maximum_fusion), channel_id=1, source_target_pairs={{0,128},{32,160},{64,192},{96,224},{128,0},{160,32},{192,64},{224,... | collective-permute-start | bytes 2064392 | tf_op jit(solution)/shard_map/ppermute | solution.py:189
  70.2 10.8 %all-to-all-done = bf16[32,8,512]{2,1,0:T(8,128)(2,1)S(1)} async-done(((bf16[32,8,512]{2,1,0:T(8,128)(2,1)}), bf16[32,8,512]{2,1,0:T(8,128)(2,1)S(1)}, u32[]{:S(2)}, u32[]{:S(2)}) %all-to-all-start) | async-done | bytes 262176 | tf_op jit(solution)/shard_map/all_to_all | solution.py:194
  81.0 3.3 %collective-permute-start = (bf16[256,512]{1,0:T(8,128)(2,1)S(1)}, bf16[256,512]{1,0:T(8,128)(2,1)S(1)}, u32[]{:S(2)}, u32[]{:S(2)}) collective-permute-start(bf16[256,512]{1,0:T(8,128)(2,1)S(1)} %bitcast.19), channel_id=1, source_target_pairs={{0,128},{32,160},{64,192},{96,224},{128,0},{160,32},{192,64},{224,... | collective-permute-start | bytes 786440 | tf_op jit(solution)/shard_map/ppermute | solution.py:189
  84.3 0.0 copy-done.1
  84.3 0.0 copy-done.2
  84.3 0.0 copy-done.3
  84.3 0.1 pad_maximum_fusion.1.weights_ref
  84.4 0.5 shard_map.111.refs_0_
  85.0 0.6 collective-permute-done.1.weights_ref
  85.6 5.6 %collective-permute-done.rows_ref = bf16[256,512]{1,0:T(8,128)(2,1)S(1)} collective-permute-done((bf16[256,512]{1,0:T(8,128)(2,1)S(1)}, bf16[256,512]{1,0:T(8,128)(2,1)S(1)}, u32[]{:S(2)}, u32[]{:S(2)}) %collective-permute-start) | collective-permute-done | bytes 262176 | tf_op jit(solution)/shard_map/ppermute | solution.py:189
  91.2 0.5 shard_map.112
  91.8 36.0 %all_to_all.20 = bf16[16,96,256]{2,1,0:T(8,128)(2,1)S(1)} all-to-all(bf16[16,96,256]{2,1,0:T(8,128)(2,1)S(1)} %shard_map.112), channel_id=1, replica_groups={{0,32,64,96,256,288,320,352,512,544,576,608,768,800,832,864},{128,160,1..., dimensions={0} | all-to-all | bytes 1572864 | tf_op jit(solution)/shard_map/all_to_all | solution.py:176
  127.8 0.1 convert_reduce_fusion
  128.0 0.1 broadcast_in_dim.15
  128.0 29.4 %all_to_all.21.near_ref = bf16[16,96,256]{2,1,0:T(8,128)(2,1)S(1)} all-to-all(bf16[16,96,256]{2,1,0:T(8,128)(2,1)S(1)} %broadcast_in_dim.15), channel_id=1, replica_groups={{0,32,64,96,256,288,320,352,512,544,576,608,768,800,832,864},{128,160,1..., dimensions={0} | all-to-all | bytes 1572864 | tf_op jit(solution)/shard_map/all_to_all | solution.py:176
  157.4 0.4 shard_map.114
  157.9 1.9 collective-permute-start.2
  159.8 0.4 shard_map.113
  160.2 5.9 %collective-permute-done.2 = bf16[256,512]{1,0:T(8,128)(2,1)S(1)} collective-permute-done((bf16[256,512]{1,0:T(8,128)(2,1)S(1)}, bf16[256,512]{1,0:T(8,128)(2,1)S(1)}, u32[]{:S(2)}, u32[]{:S(2)}) %collective-permute-start.2) | collective-permute-done | bytes 262176 | tf_op jit(solution)/shard_map/ppermute | solution.py:189
  166.2 0.8 add_convert_fusion
  166.9 14.0 %all-to-all-start.3 = ((bf16[32,8,512]{2,1,0:T(8,128)(2,1)}), bf16[32,8,512]{2,1,0:T(8,128)(2,1)S(1)}, u32[]{:S(2)}, u32[]{:S(2)}) async-start(bf16[32,8,512]{2,1,0:T(8,128)(2,1)} %bitcast.14), calls=%async_computation.3 | async-start | bytes 524288 | tf_op jit(solution)/shard_map/all_to_all | solution.py:194
  181.0 0.0 copy-start
  181.0 0.1 fusion.1
  181.0 1.9 collective-permute-start.4
  183.0 3.3 %collective-permute-start.3 = (bf16[8,96,256]{2,1,0:T(8,128)(2,1)S(1)}, bf16[8,96,256]{2,1,0:T(8,128)(2,1)S(1)}, u32[]{:S(2)}, u32[]{:S(2)}) collective-permute-start(bf16[8,96,256]{2,1,0:T(8,128)(2,1)S(1)} %get-tuple-element.36), channel_id=1, source_target_pairs={{0,128},{32,160},{64,192},{96,224},{128,0},{160,32},{192,64},{224,... | collective-permute-start | bytes 1179656 | tf_op jit(solution)/shard_map/ppermute | solution.py:189
  186.3 8.4 %collective-permute-done.4.far1_ref = bf16[8,96,256]{2,1,0:T(8,128)(2,1)S(1)} collective-permute-done((bf16[8,96,256]{2,1,0:T(8,128)(2,1)S(1)}, bf16[8,96,256]{2,1,0:T(8,128)(2,1)S(1)}, u32[]{:S(2)}, u32[]{:S(2)}) %collective-permute-start.4) | collective-permute-done | bytes 393248 | tf_op jit(solution)/shard_map/ppermute | solution.py:189
  194.6 0.7 collective-permute-done.3.far0_ref
  195.3 1.7 shard_map.116
  197.0 0.0 all-to-all-done.3
  197.0 0.0 copy-done
  197.0 0.8 shard_map.115
  (2 shorter events, 0.0 us)
Async XLA Ops:
  45.0 39.3 %copy-start.1 = (bf16[224,512]{1,0:T(8,128)(2,1)S(1)}, bf16[224,512]{1,0:T(8,128)(2,1)}, u32[]{:S(2)}) copy-start(bf16[224,512]{1,0:T(8,128)(2,1)} %get-tuple-element.24) | copy-start | bytes 688132
  45.0 39.3 %copy-start.2 = (bf16[224,512]{1,0:T(8,128)(2,1)S(1)}, bf16[224,512]{1,0:T(8,128)(2,1)}, u32[]{:S(2)}) copy-start(bf16[224,512]{1,0:T(8,128)(2,1)} %get-tuple-element.25) | copy-start | bytes 688132
  45.0 39.3 %copy-start.3 = (bf16[224,512]{1,0:T(8,128)(2,1)S(1)}, bf16[224,512]{1,0:T(8,128)(2,1)}, u32[]{:S(2)}) copy-start(bf16[224,512]{1,0:T(8,128)(2,1)} %get-tuple-element.26) | copy-start | bytes 688132
  45.0 36.0 %all-to-all-start = ((bf16[32,8,512]{2,1,0:T(8,128)(2,1)}), bf16[32,8,512]{2,1,0:T(8,128)(2,1)S(1)}, u32[]{:S(2)}, u32[]{:S(2)}) async-start(bf16[32,8,512]{2,1,0:T(8,128)(2,1)} %bitcast.26), calls=%async_computation | async-start | bytes 524288 | tf_op jit(solution)/shard_map/all_to_all | solution.py:194
  66.9 18.7 %collective-permute-start.1 = (bf16[3,224,512]{2,1,0:T(8,128)(2,1)S(1)}, bf16[3,224,512]{2,1,0:T(8,128)(2,1)S(1)}, u32[]{:S(2)}, u32[]{:S(2)}) collective-permute-start(bf16[3,224,512]{2,1,0:T(8,128)(2,1)S(1)} %pad_maximum_fusion), channel_id=1, source_target_pairs={{0,128},{32,160},{64,192},{96,224},{128,0},{160,32},{192,64},{224,... | collective-permute-start | bytes 2064392 | tf_op jit(solution)/shard_map/ppermute | solution.py:189
  81.0 10.2 %collective-permute-start = (bf16[256,512]{1,0:T(8,128)(2,1)S(1)}, bf16[256,512]{1,0:T(8,128)(2,1)S(1)}, u32[]{:S(2)}, u32[]{:S(2)}) collective-permute-start(bf16[256,512]{1,0:T(8,128)(2,1)S(1)} %bitcast.19), channel_id=1, source_target_pairs={{0,128},{32,160},{64,192},{96,224},{128,0},{160,32},{192,64},{224,... | collective-permute-start | bytes 786440 | tf_op jit(solution)/shard_map/ppermute | solution.py:189
  157.9 8.3 %collective-permute-start.2 = (bf16[256,512]{1,0:T(8,128)(2,1)S(1)}, bf16[256,512]{1,0:T(8,128)(2,1)S(1)}, u32[]{:S(2)}, u32[]{:S(2)}) collective-permute-start(bf16[256,512]{1,0:T(8,128)(2,1)S(1)} %shard_map.114), channel_id=1, source_target_pairs={{0,128},{32,160},{64,192},{96,224},{128,0},{160,32},{192,64},{224,... | collective-permute-start | bytes 786440 | tf_op jit(solution)/shard_map/ppermute | solution.py:189
  166.9 30.1 %all-to-all-start.3 = ((bf16[32,8,512]{2,1,0:T(8,128)(2,1)}), bf16[32,8,512]{2,1,0:T(8,128)(2,1)S(1)}, u32[]{:S(2)}, u32[]{:S(2)}) async-start(bf16[32,8,512]{2,1,0:T(8,128)(2,1)} %bitcast.14), calls=%async_computation.3 | async-start | bytes 524288 | tf_op jit(solution)/shard_map/all_to_all | solution.py:194
  181.0 16.1 %copy-start = (bf16[64,256]{1,0:T(8,128)(2,1)S(1)}, bf16[64,256]{1,0:T(8,128)(2,1)}, u32[]{:S(2)}) copy-start(bf16[64,256]{1,0:T(8,128)(2,1)} %get-tuple-element.28.mix_ref) | copy-start | bytes 98308
  181.0 13.6 %collective-permute-start.4 = (bf16[8,96,256]{2,1,0:T(8,128)(2,1)S(1)}, bf16[8,96,256]{2,1,0:T(8,128)(2,1)S(1)}, u32[]{:S(2)}, u32[]{:S(2)}) collective-permute-start(bf16[8,96,256]{2,1,0:T(8,128)(2,1)S(1)} %get-tuple-element.35), channel_id=1, source_target_pairs={{0,896},{32,928},{64,960},{96,992},{128,256},{160,288},{192,320},{... | collective-permute-start | bytes 1179656 | tf_op jit(solution)/shard_map/ppermute | solution.py:189
  183.0 12.4 %collective-permute-start.3 = (bf16[8,96,256]{2,1,0:T(8,128)(2,1)S(1)}, bf16[8,96,256]{2,1,0:T(8,128)(2,1)S(1)}, u32[]{:S(2)}, u32[]{:S(2)}) collective-permute-start(bf16[8,96,256]{2,1,0:T(8,128)(2,1)S(1)} %get-tuple-element.36), channel_id=1, source_target_pairs={{0,128},{32,160},{64,192},{96,224},{128,0},{160,32},{192,64},{224,... | collective-permute-start | bytes 1179656 | tf_op jit(solution)/shard_map/ppermute | solution.py:189

commit v9 on v6

--- a/solution.py
+++ b/solution.py
@@ -103,22 +103,31 @@
     outs_ref[:, pitch : pitch + width] = grad.T.astype(outs_ref.dtype)
 
 
-def grad_kernel(odd_ref, near_ref, far0_ref, far1_ref, rows_ref, gate_ref, up_ref, down_ref):
-    odd = odd_ref[0]
-    width = gate_ref.shape[0]
+def outer_products(rows_ref, width, ref):
     pitch = rows_ref.shape[1] // 2
-    half = gate_ref.shape[1] // 2
     x = flip(rows_ref[:, :width])
     do = flip(rows_ref[:, pitch : pitch + width])
-    places = ((near_ref, odd * half), (far0_ref, (1 - odd) * half))
-    places += ((far1_ref, (1 - odd) * half + half // 2),)
-    for ref, start in places:
-        for to_ref, r, index in ((gate_ref, x, 1), (up_ref, x, 2), (down_ref, do, 0)):
-            block = array_rows(ref, index)
-            span = block.shape[0]
-            to_ref[:, pl.ds(pl.multiple_of(start, half // 2), span)] = lax.dot_general(
-                r, block, (((1,), (1,)), ((), ())), preferred_element_type=F32
-            ).astype(BF16)
+    for r, index in ((x, 1), (x, 2), (do, 0)):
+        yield lax.dot_general(
+            r, array_rows(ref, index), (((1,), (1,)), ((), ())), preferred_element_type=F32
+        ).astype(BF16)
+
+
+def near_grad_kernel(near_ref, rows_ref, *to_refs):
+    for to_ref, block in zip(to_refs, outer_products(rows_ref, to_refs[0].shape[0], near_ref)):
+        to_ref[...] = block
+
+
+def grad_kernel(odd_ref, far0_ref, far1_ref, rows_ref, *refs):
+    odd = odd_ref[0]
+    nears, to_refs = refs[:3], refs[3:]
+    width, half = nears[0].shape
+    for near_ref, to_ref in zip(nears, to_refs):
+        to_ref[:, pl.ds(pl.multiple_of(odd * half, half), half)] = near_ref[...]
+    for side, ref in enumerate((far0_ref, far1_ref)):
+        start = pl.multiple_of((1 - odd) * half + side * (half // 2), half // 2)
+        for to_ref, block in zip(to_refs, outer_products(rows_ref, width, ref)):
+            to_ref[:, pl.ds(start, half // 2)] = block
 
 
 def combine_kernel(home_ref, mix_ref, out_ref, grad_ref):
@@ -238,7 +247,10 @@
         neighbour_swap(late[side * group // 2 : (side + 1) * group // 2], side) for side in range(2)
     )
     home = expert_swap(outs)
-    grads = run(grad_kernel, [((width, HID), BF16)] * 3, (odd, near) + far + (rows,), work)
+    nears = run(near_grad_kernel, [((width, half), BF16)] * 3, (late, rows), work // 2)
+    grads = run(
+        grad_kernel, [((width, HID), BF16)] * 3, (odd,) + far + (rows,) + tuple(nears), work // 2
+    )
     layer_out, grad_tokens = run(
         combine_kernel,
         [((tok_count, width), BF16)] * 2,

time: 152 us -> 152 us (level)
    pallas_call x7 -> x8, Pallas kernels: 6.49 us -> 6.7 us  [run(): pl.pallas_call(kernel, out_shape=outs, in_specs=[SMEM if a.shape == (1,)...]
where the time goes in v9:
time: 152 us; the launch traced here: 151 us
  blocking collectives  97.7 us (64%)
  starting transfers between devices  22.3 us (15%)
  waiting for transfers between devices  20.2 us (13%)
  Pallas kernels  6.7 us (4%)
  local copies, waits for them, and re-layouts  2.64 us (2%)
    all_to_all x2, blocking collectives, group_swap(): lax.all_to_all(blocks, 'dp', split_axis=0, concat_axis=0, axis_index_grou...  62.6 us
    all_to_all x1, blocking collectives, expert_swap(): lax.all_to_all(rows.reshape(count, CAP, rows.shape[1]), 'expert', split_a...  35.1 us
    ppermute x5, waiting for transfers between devices, neighbour_swap(): return lax.ppermute(block, 'dp', pairs)  20.2 us
    ppermute x5, starting transfers between devices, neighbour_swap(): return lax.ppermute(block, 'dp', pairs)  16.1 us
    pallas_call x8, Pallas kernels, run(): pl.pallas_call(kernel, out_shape=outs, in_specs=[SMEM if a.shape == (1,)...  6.7 us
    all_to_all x1, starting transfers between devices, expert_swap(): lax.all_to_all(rows.reshape(count, CAP, rows.shape[1]), 'expert', split_a...  6.19 us
  transfers between devices with their start and end apart: 6, of which 4 were waited for; matrix products, arithmetic and copies ran while one was open for 0% of the time, Pallas kernels for 2%

profile of v9, /device:TPU:1, one launch (start us, length us, event | category | flops | bytes accessed | tf_op | source)
XLA Modules:
  0.0 151.2 jit_solution(13282893685752982949)
XLA Ops:
  0.7 2.1 %shard_map.110 = (bf16[256,512]{1,0:T(8,128)(2,1)}, bf16[64,256]{1,0:T(8,128)(2,1)}) custom-call(s32[8,16]{1,0:T(8,128)} %bitcast.30, f32[8,16]{1,0:T(8,128)} %bitcast.31, bf16[16,224]{1,0:T(8,128)(2,1)} %tokens_ref.1, bf16[16,224]{1,0:T(8,128)(2,1)} %cotangent_ref.1), custom_call_target="tpu_custom_call" | custom-call | flops 3670016 | bytes 310272 | tf_op jit(solution)/shard_map/pallas_call | solution.py:149
  2.7 1.1 dynamic-slice_bitcast_fusion.2
  3.8 0.0 copy-start.1
  3.8 1.4 dynamic-slice_bitcast_fusion
  5.2 0.1 pad_maximum_fusion
  5.3 4.1 %collective-permute-start.1 = (bf16[3,224,512]{2,1,0:T(8,128)(2,1)S(1)}, bf16[3,224,512]{2,1,0:T(8,128)(2,1)S(1)}, u32[]{:S(2)}, u32[]{:S(2)}) collective-permute-start(bf16[3,224,512]{2,1,0:T(8,128)(2,1)S(1)} %pad_maximum_fusion), channel_id=1, source_target_pairs={{0,128},{32,160},{64,192},{96,224},{128,0},{160,32},{192,64},{224,... | collective-permute-start | bytes 2064392 | tf_op jit(solution)/shard_map/ppermute | solution.py:180
  9.5 0.0 copy-done.1
  9.5 35.1 %all_to_all.20 = bf16[32,8,512]{2,1,0:T(8,128)(2,1)S(1)} all-to-all(bf16[32,8,512]{2,1,0:T(8,128)(2,1)S(1)} %bitcast.29), channel_id=1, replica_groups=mesh['dp'=32,'expert'=32] {'expert'}, dimensions={0} | all-to-all | bytes 524288 | tf_op jit(solution)/shard_map/all_to_all | solution.py:185
  44.5 2.0 %collective-permute-start = (bf16[256,512]{1,0:T(8,128)(2,1)S(1)}, bf16[256,512]{1,0:T(8,128)(2,1)S(1)}, u32[]{:S(2)}, u32[]{:S(2)}) collective-permute-start(bf16[256,512]{1,0:T(8,128)(2,1)S(1)} %bitcast.24), channel_id=1, source_target_pairs={{0,128},{32,160},{64,192},{96,224},{128,0},{160,32},{192,64},{224,... | collective-permute-start | bytes 786440 | tf_op jit(solution)/shard_map/ppermute | solution.py:180
  46.5 0.5 shard_map.111.refs_0_
  47.1 0.0 collective-permute-done.1
  47.1 6.8 %collective-permute-done.rows_ref = bf16[256,512]{1,0:T(8,128)(2,1)S(1)} collective-permute-done((bf16[256,512]{1,0:T(8,128)(2,1)S(1)}, bf16[256,512]{1,0:T(8,128)(2,1)S(1)}, u32[]{:S(2)}, u32[]{:S(2)}) %collective-permute-start) | collective-permute-done | bytes 262176 | tf_op jit(solution)/shard_map/ppermute | solution.py:180
  53.9 0.5 shard_map.112
  54.5 32.4 %all_to_all.21 = bf16[16,96,256]{2,1,0:T(8,128)(2,1)S(1)} all-to-all(bf16[16,96,256]{2,1,0:T(8,128)(2,1)S(1)} %shard_map.112), channel_id=1, replica_groups={{0,32,64,96,256,288,320,352,512,544,576,608,768,800,832,864},{128,160,1..., dimensions={0} | all-to-all | bytes 1572864 | tf_op jit(solution)/shard_map/all_to_all | solution.py:167
  86.9 0.1 convert_reduce_fusion
  87.1 0.1 broadcast_in_dim.15
  87.2 30.1 %all_to_all.22.near_ref = bf16[16,96,256]{2,1,0:T(8,128)(2,1)S(1)} all-to-all(bf16[16,96,256]{2,1,0:T(8,128)(2,1)S(1)} %broadcast_in_dim.15), channel_id=1, replica_groups={{0,32,64,96,256,288,320,352,512,544,576,608,768,800,832,864},{128,160,1..., dimensions={0} | all-to-all | bytes 1572864 | tf_op jit(solution)/shard_map/all_to_all | solution.py:167
  117.3 0.4 shard_map.114
  117.7 4.5 %collective-permute-start.2 = (bf16[256,512]{1,0:T(8,128)(2,1)S(1)}, bf16[256,512]{1,0:T(8,128)(2,1)S(1)}, u32[]{:S(2)}, u32[]{:S(2)}) collective-permute-start(bf16[256,512]{1,0:T(8,128)(2,1)S(1)} %shard_map.114), channel_id=1, source_target_pairs={{0,128},{32,160},{64,192},{96,224},{128,0},{160,32},{192,64},{224,... | collective-permute-start | bytes 786440 | tf_op jit(solution)/shard_map/ppermute | solution.py:180
  122.3 0.4 shard_map.113
  122.7 4.5 %collective-permute-done.2 = bf16[256,512]{1,0:T(8,128)(2,1)S(1)} collective-permute-done((bf16[256,512]{1,0:T(8,128)(2,1)S(1)}, bf16[256,512]{1,0:T(8,128)(2,1)S(1)}, u32[]{:S(2)}, u32[]{:S(2)}) %collective-permute-start.2) | collective-permute-done | bytes 262176 | tf_op jit(solution)/shard_map/ppermute | solution.py:180
  127.2 0.8 add_convert_fusion
  127.9 6.2 %all-to-all-start.3 = ((bf16[32,8,512]{2,1,0:T(8,128)(2,1)}), bf16[32,8,512]{2,1,0:T(8,128)(2,1)S(1)}, u32[]{:S(2)}, u32[]{:S(2)}) async-start(bf16[32,8,512]{2,1,0:T(8,128)(2,1)} %bitcast.13), calls=%async_computation.3 | async-start | bytes 524288 | tf_op jit(solution)/shard_map/all_to_all | solution.py:185
  134.1 0.1 fusion.1
  134.2 0.0 copy-start
  134.2 2.8 %collective-permute-start.4 = (bf16[8,96,256]{2,1,0:T(8,128)(2,1)S(1)}, bf16[8,96,256]{2,1,0:T(8,128)(2,1)S(1)}, u32[]{:S(2)}, u32[]{:S(2)}) collective-permute-start(bf16[8,96,256]{2,1,0:T(8,128)(2,1)S(1)} %get-tuple-element.33), channel_id=1, source_target_pairs={{0,896},{32,928},{64,960},{96,992},{128,256},{160,288},{192,320},{... | collective-permute-start | bytes 1179656 | tf_op jit(solution)/shard_map/ppermute | solution.py:180
  137.0 2.6 %collective-permute-start.3 = (bf16[8,96,256]{2,1,0:T(8,128)(2,1)S(1)}, bf16[8,96,256]{2,1,0:T(8,128)(2,1)S(1)}, u32[]{:S(2)}, u32[]{:S(2)}) collective-permute-start(bf16[8,96,256]{2,1,0:T(8,128)(2,1)S(1)} %get-tuple-element.34), channel_id=1, source_target_pairs={{0,128},{32,160},{64,192},{96,224},{128,0},{160,32},{192,64},{224,... | collective-permute-start | bytes 1179656 | tf_op jit(solution)/shard_map/ppermute | solution.py:180
  139.6 0.4 shard_map.116
  140.1 7.7 %collective-permute-done.4.far1_ref = bf16[8,96,256]{2,1,0:T(8,128)(2,1)S(1)} collective-permute-done((bf16[8,96,256]{2,1,0:T(8,128)(2,1)S(1)}, bf16[8,96,256]{2,1,0:T(8,128)(2,1)S(1)}, u32[]{:S(2)}, u32[]{:S(2)}) %collective-permute-start.4) | collective-permute-done | bytes 393248 | tf_op jit(solution)/shard_map/ppermute | solution.py:180
  147.8 1.2 collective-permute-done.3.far0_ref
  149.0 1.5 shard_map.117
  150.5 0.0 all-to-all-done.3
  150.5 0.0 copy-done
  150.5 0.8 shard_map.115
  (3 shorter events, 0.1 us)
Async XLA Ops:
  3.8 5.6 %copy-start.1 = (bf16[256,512]{1,0:T(8,128)(2,1)S(1)}, bf16[256,512]{1,0:T(8,128)(2,1)}, u32[]{:S(2)}) copy-start(bf16[256,512]{1,0:T(8,128)(2,1)} %get-tuple-element.20) | copy-start | bytes 786436
  5.3 41.8 %collective-permute-start.1 = (bf16[3,224,512]{2,1,0:T(8,128)(2,1)S(1)}, bf16[3,224,512]{2,1,0:T(8,128)(2,1)S(1)}, u32[]{:S(2)}, u32[]{:S(2)}) collective-permute-start(bf16[3,224,512]{2,1,0:T(8,128)(2,1)S(1)} %pad_maximum_fusion), channel_id=1, source_target_pairs={{0,128},{32,160},{64,192},{96,224},{128,0},{160,32},{192,64},{224,... | collective-permute-start | bytes 2064392 | tf_op jit(solution)/shard_map/ppermute | solution.py:180
  44.5 9.4 %collective-permute-start = (bf16[256,512]{1,0:T(8,128)(2,1)S(1)}, bf16[256,512]{1,0:T(8,128)(2,1)S(1)}, u32[]{:S(2)}, u32[]{:S(2)}) collective-permute-start(bf16[256,512]{1,0:T(8,128)(2,1)S(1)} %bitcast.24), channel_id=1, source_target_pairs={{0,128},{32,160},{64,192},{96,224},{128,0},{160,32},{192,64},{224,... | collective-permute-start | bytes 786440 | tf_op jit(solution)/shard_map/ppermute | solution.py:180
  117.7 9.4 %collective-permute-start.2 = (bf16[256,512]{1,0:T(8,128)(2,1)S(1)}, bf16[256,512]{1,0:T(8,128)(2,1)S(1)}, u32[]{:S(2)}, u32[]{:S(2)}) collective-permute-start(bf16[256,512]{1,0:T(8,128)(2,1)S(1)} %shard_map.114), channel_id=1, source_target_pairs={{0,128},{32,160},{64,192},{96,224},{128,0},{160,32},{192,64},{224,... | collective-permute-start | bytes 786440 | tf_op jit(solution)/shard_map/ppermute | solution.py:180
  127.9 22.5 %all-to-all-start.3 = ((bf16[32,8,512]{2,1,0:T(8,128)(2,1)}), bf16[32,8,512]{2,1,0:T(8,128)(2,1)S(1)}, u32[]{:S(2)}, u32[]{:S(2)}) async-start(bf16[32,8,512]{2,1,0:T(8,128)(2,1)} %bitcast.13), calls=%async_computation.3 | async-start | bytes 524288 | tf_op jit(solution)/shard_map/all_to_all | solution.py:185
  134.2 16.3 %copy-start = (bf16[64,256]{1,0:T(8,128)(2,1)S(1)}, bf16[64,256]{1,0:T(8,128)(2,1)}, u32[]{:S(2)}) copy-start(bf16[64,256]{1,0:T(8,128)(2,1)} %get-tuple-element.23.mix_ref) | copy-start | bytes 98308
  134.2 13.6 %collective-permute-start.4 = (bf16[8,96,256]{2,1,0:T(8,128)(2,1)S(1)}, bf16[8,96,256]{2,1,0:T(8,128)(2,1)S(1)}, u32[]{:S(2)}, u32[]{:S(2)}) collective-permute-start(bf16[8,96,256]{2,1,0:T(8,128)(2,1)S(1)} %get-tuple-element.33), channel_id=1, source_target_pairs={{0,896},{32,928},{64,960},{96,992},{128,256},{160,288},{192,320},{... | collective-permute-start | bytes 1179656 | tf_op jit(solution)/shard_map/ppermute | solution.py:180
  137.0 12.0 %collective-permute-start.3 = (bf16[8,96,256]{2,1,0:T(8,128)(2,1)S(1)}, bf16[8,96,256]{2,1,0:T(8,128)(2,1)S(1)}, u32[]{:S(2)}, u32[]{:S(2)}) collective-permute-start(bf16[8,96,256]{2,1,0:T(8,128)(2,1)S(1)} %get-tuple-element.34), channel_id=1, source_target_pairs={{0,128},{32,160},{64,192},{96,224},{128,0},{160,32},{192,64},{224,... | collective-permute-start | bytes 1179656 | tf_op jit(solution)/shard_map/ppermute | solution.py:180
